TPU v7x, 256 devices: a whole 4x4x8 slice. The times are simulated.
256 devices in a mesh: src: 8 (over z_hi, core), gx: 8 (over x, z_lo), gy: 4 (over y).
Axes of the slice: x: 4, y: 4, z: 8 (z_hi: 4, z_lo: 2; z = z_hi * 2 + z_lo), core: 2. Of those that a mesh axis runs over, the one named last changes fastest.
Arguments:
- labels: int32 [64, 128, 128], P('gx', 'gy'), may hold values from 0 to 15
- kappa_table: float32 [16], replicated, may hold values from 0.5 to 2
- absorb_table: float32 [16], replicated, may hold values from 0.02 to 0.1
- background: float32 [32, 64, 128, 128], P('src', 'gx', 'gy'), may hold values from 0.1 to 10
- det_cells: int32 [1024], replicated, may hold values from 0 to 1048575
- v_kappa: float32 [64, 128, 128], P('gx', 'gy', 'src'), may hold values from -6 to 6
- v_absorb: float32 [64, 128, 128], P('gx', 'gy', 'src'), may hold values from -6 to 6
- q_kappa: float32 [64, 128, 128], P('gx', 'gy', 'src'), may hold values from -6 to 6
- q_absorb: float32 [64, 128, 128], P('gx', 'gy', 'src'), may hold values from -6 to 6
- beta_prev: float32 [1], replicated, may hold values from 0.2 to 2
Outputs:
- next_kappa: float32 [64, 128, 128], P('gx', 'gy', 'src')
- next_absorb: float32 [64, 128, 128], P('gx', 'gy', 'src')
- coefs: float32 [2], replicated
Inputs may be any that keep to these rules, and one draw needn't show every extreme that they name: `labels`: a region number for every cell. `det_cells`: flat index (x * 128 + y) * 128 + z of a grid cell; indices may repeat.
All inputs are finite; a program needn't handle non-finite values.
Results may differ from a plain program's by a relative error of at most 0.0001.
Values sent between devices are 32-bit elements; how exact they have to be, the bound alone decides.
A program may use at most 128 MiB of HBM per device.

v0:
```python
import functools

import jax
import jax.numpy as jnp
from jax import lax
from jax.experimental import pallas as pl
from jax.experimental.pallas import tpu as pltpu
from jax.sharding import PartitionSpec as P

ITERS = 6
MESH = pl.DeviceIdType.MESH


lam_low = 0.02
lam_high = 24.1
eps_norm = 1e-06


def _exchange_kernel(axis, n, scatter, x_ref, o_ref, slots, send_sem, recv_sem, local_sem):
    me = lax.axis_index(axis)
    barrier = pltpu.get_barrier_semaphore()
    for k in range(1, n):
        peer = lax.rem(me + k, n)
        pl.semaphore_signal(barrier, inc=1, device_id={axis: peer}, device_id_type=MESH)
    pl.semaphore_wait(barrier, n - 1)
    copies = []
    for k in range(1, n):
        peer = lax.rem(me + k, n)
        copy = pltpu.make_async_remote_copy(
            src_ref=x_ref.at[peer] if scatter else x_ref,
            dst_ref=slots.at[me],
            send_sem=send_sem.at[k - 1],
            recv_sem=recv_sem.at[k - 1],
            device_id={axis: peer},
            device_id_type=MESH,
        )
        copy.start()
        copies.append(copy)
    local = pltpu.make_async_copy(x_ref.at[me] if scatter else x_ref, slots.at[me], local_sem)
    local.start()
    local.wait()
    for copy in copies:
        copy.wait()
    o_ref[...] = slots[...]


def exchange(x, axis, cid, scatter=False):
    n = lax.axis_size(axis)
    block = x.shape[1:] if scatter else x.shape
    return pl.pallas_call(
        functools.partial(_exchange_kernel, axis, n, scatter),
        out_shape=jax.ShapeDtypeStruct((n,) + block, x.dtype),
        in_specs=[pl.BlockSpec(memory_space=pltpu.VMEM)],
        out_specs=pl.BlockSpec(memory_space=pltpu.VMEM),
        scratch_shapes=[
            pltpu.VMEM((n,) + block, x.dtype),
            pltpu.SemaphoreType.DMA((n - 1,)),
            pltpu.SemaphoreType.DMA((n - 1,)),
            pltpu.SemaphoreType.DMA,
        ],
        compiler_params=pltpu.CompilerParams(collective_id=cid, has_side_effects=True),
    )(x)


def small_sum(values, axes, first_id):
    count = values.shape[0]
    packed = jnp.pad(values, (0, 1024 - count)).reshape(8, 128)
    for i, axis in enumerate(axes):
        packed = jnp.sum(exchange(packed, axis, first_id + i), axis=0)
    return packed.reshape(-1)[:count]


def padded_2(block, sides, width):
    for axis, dim in sides:
        count = lax.axis_size(axis)
        forward = [(i, i + 1) for i in range(count - 1)]
        backward = [(target, source) for source, target in forward]
        low = lax.ppermute(
            lax.slice_in_dim(block, block.shape[dim] - width, None, axis=dim), axis, forward
        )
        high = lax.ppermute(lax.slice_in_dim(block, 0, width, axis=dim), axis, backward)
        block = jnp.concatenate([low, block, high], axis=dim)
    return block


def regional(labels, table):
    field = jnp.zeros(labels.shape, jnp.float32)
    for region in range(table.shape[0]):
        field = field + jnp.where(labels == region, table[region], 0.0)
    return field


def beside(padded):
    widths = [(0, 0)] * (padded.ndim - 1) + [(1, 1)]
    full = jnp.pad(padded, widths)
    return [
        full[..., 2:, 1:-1, 1:-1],
        full[..., :-2, 1:-1, 1:-1],
        full[..., 1:-1, 2:, 1:-1],
        full[..., 1:-1, :-2, 1:-1],
        full[..., 1:-1, 1:-1, 2:],
        full[..., 1:-1, 1:-1, :-2],
    ]


def around(field):
    widths = [(0, 0)] * (field.ndim - 3) + [(1, 1)] * 3
    full = jnp.pad(field, widths)
    return [
        full[..., 2:, 1:-1, 1:-1],
        full[..., :-2, 1:-1, 1:-1],
        full[..., 1:-1, 2:, 1:-1],
        full[..., 1:-1, :-2, 1:-1],
        full[..., 1:-1, 1:-1, 2:],
        full[..., 1:-1, 1:-1, :-2],
    ]


def chebyshev(rhs, apply_op):
    theta = 0.5 * (lam_high + lam_low)
    delta = 0.5 * (lam_high - lam_low)
    sigma = theta / delta
    rho = 1.0 / sigma
    solution = jnp.zeros_like(rhs)
    remain = rhs
    step_dir = rhs / theta
    for step in range(ITERS):
        solution = solution + step_dir
        if step + 1 < ITERS:
            remain = remain - apply_op(step_dir)
            rho_next = 1.0 / (2.0 * sigma - rho)
            step_dir = rho_next * rho * step_dir + 2.0 * rho_next / delta * remain
            rho = rho_next
    return solution


def per_device(
    labels,
    kappa_table,
    absorb_table,
    background,
    det_cells,
    v_kappa,
    v_absorb,
    q_kappa,
    q_absorb,
    beta_prev,
):
    sources, cx, cy, cz = background.shape
    kappa = regional(labels, kappa_table)
    absorb = regional(labels, absorb_table)
    n_src = lax.axis_size("src")
    slab = v_kappa.shape[2]
    pair = jnp.stack([v_kappa, v_absorb]).reshape(-1, 128)
    gathered = exchange(pair, "src", 0).reshape((n_src, 2, cx, cy, slab))
    full_k, full_a = jnp.transpose(gathered, (1, 2, 3, 0, 4)).reshape(2, cx, cy, cz)
    width = ITERS
    stacked = jnp.concatenate([background, kappa[None], absorb[None], full_k[None], full_a[None]], axis=0)
    wide = padded_2(stacked, (("gx", 1), ("gy", 2)), width)
    phi_w, kappa_w, absorb_w, vk_w, va_w = (
        wide[:sources], wide[sources], wide[sources + 1], wide[sources + 2], wide[sources + 3]
    )
    wx = cx + 2 * width
    wy = cy + 2 * width
    gx_at = lax.axis_index("gx") * cx - width + jnp.arange(wx)
    gy_at = lax.axis_index("gy") * cy - width + jnp.arange(wy)
    inside = ((gx_at >= 0) & (gx_at < cx * lax.axis_size("gx")))[:, None, None] & (
        (gy_at >= 0) & (gy_at < cy * lax.axis_size("gy"))
    )[None, :, None]
    mask = inside.astype(jnp.float32)
    kappa_faces = [mask * (0.5 * (kappa_w + near)) for near in around(kappa_w)]
    vk_faces = [mask * (0.5 * (vk_w + near)) for near in around(vk_w)]

    def apply_op(field):
        result = absorb_w * field
        for face, near in zip(kappa_faces, around(field)):
            result = result + face * (field - near)
        return result

    rhs = va_w * phi_w
    for face, near in zip(vk_faces, around(phi_w)):
        rhs = rhs + face * (phi_w - near)
    rhs = -rhs
    change = chebyshev(rhs, apply_op)[:, width : width + cx, width : width + cy, :]
    span_y = cy * lax.axis_size("gy")
    ix = det_cells // (span_y * cz)
    iy = det_cells // cz % span_y
    iz = det_cells % cz
    anchor_x = lax.axis_index("gx") * cx
    anchor_y = lax.axis_index("gy") * cy
    owned = (ix >= anchor_x) & (ix < anchor_x + cx) & (iy >= anchor_y) & (iy < anchor_y + cy)
    local = jnp.where(owned, ((ix - anchor_x) * cy + (iy - anchor_y)) * cz + iz, 0)
    seen = jnp.where(owned[None, :], change.reshape(sources, -1)[:, local], 0.0)
    base = jnp.where(owned[None, :], background.reshape(sources, -1)[:, local], 0.0)
    partial = jnp.stack(
        [
            jnp.sum(base, axis=1),
            jnp.sum(seen, axis=1),
            jnp.sum(base * seen, axis=1),
            jnp.sum(base * base, axis=1),
        ],
        axis=1,
    )
    sums = small_sum(partial.reshape(-1), ("gy", "gx"), 1).reshape(sources, 4, 1)
    total, seen_sum, cross, square = sums[:, 0], sums[:, 1], sums[:, 2], sums[:, 3]
    mean_base = total / det_cells.shape[0]
    ratio = base / total
    jv_vals = (seen - ratio * seen_sum) / mean_base
    ratio_jv = (cross / total - seen_sum * (square / (total * total))) / mean_base
    weight = (jv_vals - ratio_jv) / mean_base
    deposit = jnp.where(owned[None, :], weight, 0.0)
    source = (
        jnp.zeros((sources, cx * cy * cz), jnp.float32)
        .at[:, local]
        .add(deposit)
        .reshape(change.shape)
    )
    dual_w = chebyshev(padded_2(source, (("gx", 1), ("gy", 2)), width), apply_op)
    ring = (slice(None), slice(width - 1, width + cx + 1), slice(width - 1, width + cy + 1))
    phi_near = beside(phi_w[ring])
    dual_near = beside(dual_w[ring])
    dual = dual_w[:, width : width + cx, width : width + cy, :]
    grad_a = -jnp.sum(background * dual, axis=0)
    grad_k = jnp.zeros_like(kappa)
    for near_phi, near_dual in zip(phi_near, dual_near):
        grad_k = grad_k - 0.5 * jnp.sum((background - near_phi) * (dual - near_dual), axis=0)
    grads = jnp.stack([grad_k, grad_a]).reshape(2, cx, cy, n_src, slab)
    grads = jnp.transpose(grads, (3, 0, 1, 2, 4)).reshape(n_src, -1, 128)
    hv = jnp.sum(exchange(grads, "src", 3, scatter=True), axis=0).reshape(2, cx, cy, slab)
    hv_k, hv_a = hv[0], hv[1]
    cell_count = cx * lax.axis_size("gx") * cy * lax.axis_size("gy") * cz
    w_k = hv_k - beta_prev[0] * q_kappa
    w_a = hv_a - beta_prev[0] * q_absorb
    local_wv = jnp.sum(w_k * v_kappa) + jnp.sum(w_a * v_absorb)
    local_vv = jnp.sum(v_kappa * v_kappa) + jnp.sum(v_absorb * v_absorb)
    wv_sum, vv_sum = small_sum(jnp.stack([local_wv, local_vv]), ("gy", "gx", "src"), 4)
    alpha = wv_sum / cell_count / (vv_sum / cell_count + eps_norm)
    r_k = w_k - alpha * v_kappa
    r_a = w_a - alpha * v_absorb
    rr_sum = small_sum((jnp.sum(r_k * r_k) + jnp.sum(r_a * r_a))[None], ("gy", "gx", "src"), 7)[0]
    beta = jnp.sqrt(rr_sum / cell_count + eps_norm)
    return (r_k / beta, r_a / beta, jnp.stack([alpha, beta]))


def solution(mesh):
    return jax.shard_map(
        per_device,
        mesh=mesh,
        in_specs=(
            P("gx", "gy", None),
            P(),
            P(),
            P("src", "gx", "gy", None),
            P(),
            P("gx", "gy", "src"),
            P("gx", "gy", "src"),
            P("gx", "gy", "src"),
            P("gx", "gy", "src"),
            P(),
        ),
        out_specs=(P("gx", "gy", "src"), P("gx", "gy", "src"), P()),
        check_vma=False,
    )
```

profile of v0, /device:TPU:1, one launch (start us, length us, event | category | flops | bytes accessed | tf_op | source)
XLA Modules:
  0.0 356.9 jit_solution(4292479667554551249)
XLA Ops:
  7.4 16.7 %shard_map.121 = f32[8,64,128]{2,1,0:T(8,128)} custom-call(f32[64,128]{1,0:T(8,128)} %reshape.293.x_ref), custom_call_target="tpu_custom_call" | custom-call | tf_op jit(solution)/shard_map/pallas_call | solution.py:50
  29.7 10.5 %bitcast_dynamic-update-slice_fusion.1 = (f32[8,8,32,128]{3,2,1,0:T(8,128)S(1)}, pred[8,32,128]{2,1,0:T(8,128)(4,1)S(1)}, pred[8,32,128]{2,1,0:T(8,128)(4,1)S(1)...) fusion(f32[8,8,32,128]{3,2,1,0:T(8,128)S(1)} %constant_dynamic-, ...), kind=kLoop, calls=%fused_computation.418 | loop fusion | flops 1540096 | bytes 786496
  40.2 10.2 %bitcast_dynamic-update-slice_fusion = f32[8,8,32,128]{3,2,1,0:T(8,128)S(1)} fusion(f32[8,8,32,128]{3,2,1,0:T(8,128)S(1)} %get-tuple-element.59, pred[8,32,128]{2,1,0:T(8,128)(4,1)S(1)} %get-tuple-element.75, pred[8,32,128]{2,1,0:T(8,128)(4,1)S(1)} %get-tuple-element.74, pred[8,32,128]{2,1,0:T(8,128)(4,1)S(1)} %get-tuple-element.73, ...), kind=kLoop, calls=%fused_computation.417 | loop fusion | flops 1015808 | bytes 655424
  52.8 4.0 %collective-permute-start.1 = (f32[8,6,32,128]{3,2,1,0:T(8,128)S(1)}, f32[8,6,32,128]{3,2,1,0:T(8,128)S(1)}, u32[]{:S(2)}, u32[]{:S(2)}) collective-permute-start(f32[8,6,32,128]{3,2,1,0:T(8,128)S(1)} %get-tuple-element.88), channel_id=1, source_target_pairs={{0,4},{4,8},{8,12},{12,16},{16,20},{20,24},{24,28},{1,5},{5,9},{9,... | collective-permute-start | bytes 2359304 | tf_op jit(solution)/shard_map/ppermute | solution.py:78
  56.9 15.5 %collective-permute-done = f32[8,6,32,128]{3,2,1,0:T(8,128)S(1)} collective-permute-done((f32[8,6,32,128]{3,2,1,0:T(8,128)}, f32[8,6,32,128]{3,2,1,0:T(8,128)S(1)}, u32[]{:S(2)}, u32[]{:S(2)}) %collective-permute-start) | collective-permute-done | bytes 786464 | tf_op jit(solution)/shard_map/ppermute | solution.py:81
  74.3 4.0 %collective-permute-start.2 = (f32[8,20,6,128]{3,0,2,1:T(8,128)}, f32[8,20,6,128]{3,0,2,1:T(8,128)}, u32[]{:S(2)}, u32[]{:S(2)}) collective-permute-start(f32[8,20,6,128]{3,0,2,1:T(8,128)} %copy.144), channel_id=1, source_target_pairs={{0,1},{1,2},{2,3},{4,5},{5,6},{6,7},{8,9},{9,10},{10,11},{12,13},{... | collective-permute-start | bytes 1474568 | tf_op jit(solution)/shard_map/ppermute | solution.py:78
  80.9 8.7 %copy.149 = f32[4,8,32,128]{0,3,2,1:T(8,128)} copy(f32[4,8,32,128]{3,2,1,0:T(8,128)S(1)} %copy-done.16) | data formatting | bytes 1048576 | tf_op args[3]
  89.5 9.7 %gather_fusion.1 = f32[1024,4]{1,0:T(8,128)} fusion(f32[4,32768]{0,1:T(8,128)} %bitcast.110, s32[1024]{0:T(1024)S(1)} %get-tuple-element.44), kind=kCustom, calls=%fused_computation.1 | custom fusion | bytes 36864 | tf_op jit(solution)/shard_map/gather | solution.py:194
  108.3 2.3 multiply_add_fusion.7
  120.5 9.7 %copy.148 = f32[4,8,32,128]{0,3,2,1:T(8,128)} copy(f32[4,8,32,128]{3,2,1,0:T(8,128)} %fusion.229) | data formatting | bytes 1048576 | tf_op jit(solution)/shard_map/slice | solution.py:184
  130.3 9.8 %gather_fusion = f32[1024,4]{1,0:T(8,128)} fusion(f32[4,32768]{0,1:T(8,128)} %bitcast.109, s32[1024]{0:T(1024)S(1)} %get-tuple-element.44), kind=kCustom, calls=%fused_computation | custom fusion | bytes 36864 | tf_op jit(solution)/shard_map/gather | solution.py:193
  143.7 6.9 %shard_map.122 = f32[4,8,128]{2,1,0:T(8,128)} custom-call(f32[8,128]{1,0:T(8,128)} %pad_bitcast_fusion.1.x_ref), custom_call_target="tpu_custom_call" | custom-call | tf_op jit(solution)/shard_map/pallas_call | solution.py:50
  151.9 24.0 %shard_map.123 = f32[8,8,128]{2,1,0:T(8,128)} custom-call(f32[8,128]{1,0:T(8,128)} %reduce_sum.238.x_ref), custom_call_target="tpu_custom_call" | custom-call | tf_op jit(solution)/shard_map/pallas_call | solution.py:50
  178.6 15.3 %scatter_custom_fusion = f32[4,32768]{0,1:T(8,128)} fusion(s32[1024]{0:T(1024)S(1)} %get-tuple-element.45, f32[]{:T(128)} %constant.49.clone.1, f32[1024,4]{1,0:T(8,128)} %gather_fusion, f32[1024,4]{1,0:T(8,128)} %gather_fusion.1, f32[4]{0:T(128)S(1)} %get-tuple-element.115, f32[4]{0:T(128)S(1)} %get-tuple-element.114, f32[4]{0:T(128)S(1)} %get-tuple-element.28, ...), kind=kCustom, calls=%fused_computation.69 | custom fusion | flops 40960 | bytes 1578496 | tf_op jit(solution)/shard_map/scatter-add | solution.py:215
  193.9 10.7 %copy.151 = f32[4,8,32,128]{3,2,1,0:T(8,128)} copy(f32[4,8,32,128]{0,3,2,1:T(8,128)} %bitcast.108) | data formatting | bytes 1048576 | tf_op jit(solution)/shard_map/reshape | solution.py:216
  205.8 3.1 collective-permute-start.4
  210.2 3.4 collective-permute-done.4
  213.6 9.4 %collective-permute-done.5 = f32[4,6,32,128]{3,2,1,0:T(8,128)S(1)} collective-permute-done((f32[4,6,32,128]{3,2,1,0:T(8,128)S(1)}, f32[4,6,32,128]{3,2,1,0:T(8,128)S(1)}, u32[]{:S(2)}, u32[]{:S(2)}) %collective-permute-start.5) | collective-permute-done | bytes 393248 | tf_op jit(solution)/shard_map/ppermute | solution.py:81
  225.0 3.1 collective-permute-start.6
  238.4 3.0 select_maximum_fusion
  243.0 4.3 %multiply_add_fusion.3 = (f32[4,20,44,128]{3,2,1,0:T(8,128)S(1)}, f32[4,20,44,128]{3,2,1,0:T(8,128)S(1)}) fusion(f32[4,20,6,128]{3,2,1,0:T(8,128)} %collective-permute-done.7, f32[4,6,32,128]{3,2,1,0:T(8,128)S(1)} %copy-done.22, f32[4,8,32,128]{3,2,1,0:T(8,128)S(1)} %copy-done.14, f32[4,6,32,128]{3,2,1,0:T(8,128)S(1)} %copy-done.19, ...), kind=kLoop, calls=%fused_computation.298 | loop fusion | flops 12165120 | bytes 10362880 | tf_op jit(solution)/shard_map/add | solution.py:132
  247.3 2.2 multiply_add_fusion.2
  249.6 2.2 multiply_add_fusion.1
  251.8 3.5 multiply_add_fusion
  255.4 8.8 %fusion.199 = f32[4,20,44,128]{3,2,1,0:T(8,128)S(1)} fusion(f32[4,20,44,128]{3,2,1,0:T(8,128)} %get-tuple-element.37, f32[4,20,44,128]{3,2,1,0:T(8,128)} %get-tuple-element.36, f32[4,20,44,128]{3,2,1,0:T(8,128)S(1)} %get-tuple-element.38, f32[4,20,44,128]{3,2,1,0:T(8,128)S(1)} %get-tuple-element.40, f32[4,20,44,128]{3,2,1,0:T(8,128)S(1)} %get-tuple-element.42, ...), kind=kLoop, calls=%fused_computation.283 | loop fusion | flops 14868480 | bytes 15769600 | tf_op jit(solution)/shard_map/add | solution.py:128
  270.1 17.7 %shard_map.124 = f32[8,64,128]{2,1,0:T(8,128)} custom-call(f32[8,64,128]{2,1,0:T(8,128)} %reshape.300.x_ref), custom_call_target="tpu_custom_call" | custom-call | tf_op jit(solution)/shard_map/pallas_call | solution.py:50
  291.8 8.4 %shard_map.125 = f32[4,8,128]{2,1,0:T(8,128)} custom-call(f32[8,128]{1,0:T(8,128)} %fusion.282.x_ref), custom_call_target="tpu_custom_call" | custom-call | tf_op jit(solution)/shard_map/pallas_call | solution.py:50
  301.5 7.0 %shard_map.126 = f32[8,8,128]{2,1,0:T(8,128)} custom-call(f32[8,128]{1,0:T(8,128)} %reduce_sum.252.x_ref), custom_call_target="tpu_custom_call" | custom-call | tf_op jit(solution)/shard_map/pallas_call | solution.py:50
  309.8 10.9 %shard_map.127 = f32[8,8,128]{2,1,0:T(8,128)} custom-call(f32[8,128]{1,0:T(8,128)} %reduce_sum.253.x_ref), custom_call_target="tpu_custom_call" | custom-call | tf_op jit(solution)/shard_map/pallas_call | solution.py:50
  326.6 5.4 %shard_map.128 = f32[4,8,128]{2,1,0:T(8,128)} custom-call(f32[8,128]{1,0:T(8,128)} %pad_bitcast_fusion.x_ref), custom_call_target="tpu_custom_call" | custom-call | tf_op jit(solution)/shard_map/pallas_call | solution.py:50
  333.2 6.9 %shard_map.129 = f32[8,8,128]{2,1,0:T(8,128)} custom-call(f32[8,128]{1,0:T(8,128)} %reduce_sum.257.x_ref), custom_call_target="tpu_custom_call" | custom-call | tf_op jit(solution)/shard_map/pallas_call | solution.py:50
  341.5 11.3 %shard_map.130 = f32[8,8,128]{2,1,0:T(8,128)} custom-call(f32[8,128]{1,0:T(8,128)} %reduce_sum.258.x_ref), custom_call_target="tpu_custom_call" | custom-call | tf_op jit(solution)/shard_map/pallas_call | solution.py:50
  (169 shorter events, 80.0 us)
Async XLA Ops:
  51.5 20.9 %collective-permute-start = (f32[8,6,32,128]{3,2,1,0:T(8,128)}, f32[8,6,32,128]{3,2,1,0:T(8,128)S(1)}, u32[]{:S(2)}, u32[]{:S(2)}) collective-permute-start(f32[8,6,32,128]{3,2,1,0:T(8,128)} %get-tuple-element.89), channel_id=1, source_target_pairs={{4,0},{8,4},{12,8},{16,12},{20,16},{24,20},{28,24},{5,1},{9,5},{13... | collective-permute-start | bytes 2359304 | tf_op jit(solution)/shard_map/ppermute | solution.py:81
  52.8 20.2 %collective-permute-start.1 = (f32[8,6,32,128]{3,2,1,0:T(8,128)S(1)}, f32[8,6,32,128]{3,2,1,0:T(8,128)S(1)}, u32[]{:S(2)}, u32[]{:S(2)}) collective-permute-start(f32[8,6,32,128]{3,2,1,0:T(8,128)S(1)} %get-tuple-element.88), channel_id=1, source_target_pairs={{0,4},{4,8},{8,12},{12,16},{16,20},{20,24},{24,28},{1,5},{5,9},{9,... | collective-permute-start | bytes 2359304 | tf_op jit(solution)/shard_map/ppermute | solution.py:78
  72.4 30.2 %copy-start.7 = (f32[8,6,32,128]{3,2,1,0:T(8,128)}, f32[8,6,32,128]{3,2,1,0:T(8,128)S(1)}, u32[]{:S(2)}) copy-start(f32[8,6,32,128]{3,2,1,0:T(8,128)S(1)} %collective-permute-done) | copy-start | bytes 2359300
  73.0 29.6 %copy-start.4 = (f32[8,6,32,128]{3,2,1,0:T(8,128)}, f32[8,6,32,128]{3,2,1,0:T(8,128)S(1)}, u32[]{:S(2)}) copy-start(f32[8,6,32,128]{3,2,1,0:T(8,128)S(1)} %collective-permute-done.1) | copy-start | bytes 2359300
  73.2 7.6 %copy-start.35 = (s32[1024]{0:T(1024)S(1)}, s32[1024]{0:T(1024)}, u32[]{:S(2)}) copy-start(s32[1024]{0:T(1024)} %param.14) | copy-start | bytes 12292
  73.2 7.7 %copy-start.16 = (f32[4,8,32,128]{3,2,1,0:T(8,128)S(1)}, f32[4,8,32,128]{3,2,1,0:T(8,128)}, u32[]{:S(2)}) copy-start(f32[4,8,32,128]{3,2,1,0:T(8,128)} %param.13) | copy-start | bytes 1572868
  74.3 25.1 %collective-permute-start.2 = (f32[8,20,6,128]{3,0,2,1:T(8,128)}, f32[8,20,6,128]{3,0,2,1:T(8,128)}, u32[]{:S(2)}, u32[]{:S(2)}) collective-permute-start(f32[8,20,6,128]{3,0,2,1:T(8,128)} %copy.144), channel_id=1, source_target_pairs={{0,1},{1,2},{2,3},{4,5},{5,6},{6,7},{8,9},{9,10},{10,11},{12,13},{... | collective-permute-start | bytes 1474568 | tf_op jit(solution)/shard_map/ppermute | solution.py:78
  79.4 21.2 %collective-permute-start.3 = (f32[8,20,6,128]{3,0,2,1:T(8,128)}, f32[8,20,6,128]{3,0,2,1:T(8,128)}, u32[]{:S(2)}, u32[]{:S(2)}) collective-permute-start(f32[8,20,6,128]{3,0,2,1:T(8,128)} %copy.145), channel_id=1, source_target_pairs={{1,0},{2,1},{3,2},{5,4},{6,5},{7,6},{9,8},{10,9},{11,10},{13,12},{... | collective-permute-start | bytes 1474568 | tf_op jit(solution)/shard_map/ppermute | solution.py:81
  100.6 7.6 %copy-start.10 = (f32[8,20,6,128]{3,2,1,0:T(8,128)}, f32[8,20,6,128]{3,2,1,0:T(8,128)S(1)}, u32[]{:S(2)}) copy-start(f32[8,20,6,128]{3,2,1,0:T(8,128)S(1)} %copy.146) | copy-start | bytes 1474564
  102.0 6.2 %copy-start.12 = (f32[8,20,6,128]{3,2,1,0:T(8,128)}, f32[8,20,6,128]{3,2,1,0:T(8,128)S(1)}, u32[]{:S(2)}) copy-start(f32[8,20,6,128]{3,2,1,0:T(8,128)S(1)} %copy.147) | copy-start | bytes 1474564
  105.2 10.0 %copy-start = (f32[20,44,128]{2,1,0:T(8,128)}, f32[20,44,128]{2,1,0:T(8,128)S(1)}, u32[]{:S(2)}) copy-start(f32[20,44,128]{2,1,0:T(8,128)S(1)} %get-tuple-element.97) | copy-start | bytes 1351684
  108.3 9.1 %copy-start.2 = (f32[20,44,128]{2,1,0:T(8,128)}, f32[20,44,128]{2,1,0:T(8,128)S(1)}, u32[]{:S(2)}) copy-start(f32[20,44,128]{2,1,0:T(8,128)S(1)} %get-tuple-element.56) | copy-start | bytes 1351684
  204.6 24.8 %copy-start.32 = (f32[8,32,16]{1,2,0:T(8,128)S(1)}, f32[8,32,16]{1,2,0:T(8,128)}, u32[]{:S(2)}) copy-start(f32[8,32,16]{1,2,0:T(8,128)} %param.15) | copy-start | bytes 49156
  204.6 24.8 %copy-start.33 = (f32[8,32,16]{1,2,0:T(8,128)S(1)}, f32[8,32,16]{1,2,0:T(8,128)}, u32[]{:S(2)}) copy-start(f32[8,32,16]{1,2,0:T(8,128)} %param.16) | copy-start | bytes 49156
  205.8 7.8 %collective-permute-start.4 = (f32[4,6,32,128]{3,2,1,0:T(8,128)S(1)}, f32[4,6,32,128]{3,2,1,0:T(8,128)S(1)}, u32[]{:S(2)}, u32[]{:S(2)}) collective-permute-start(f32[4,6,32,128]{3,2,1,0:T(8,128)S(1)} %get-tuple-element.90), channel_id=1, source_target_pairs={{0,4},{4,8},{8,12},{12,16},{16,20},{20,24},{24,28},{1,5},{5,9},{9,... | collective-permute-start | bytes 1179656 | tf_op jit(solution)/shard_map/ppermute | solution.py:78
  208.9 14.0 %collective-permute-start.5 = (f32[4,6,32,128]{3,2,1,0:T(8,128)S(1)}, f32[4,6,32,128]{3,2,1,0:T(8,128)S(1)}, u32[]{:S(2)}, u32[]{:S(2)}) collective-permute-start(f32[4,6,32,128]{3,2,1,0:T(8,128)S(1)} %get-tuple-element.91), channel_id=1, source_target_pairs={{4,0},{8,4},{12,8},{16,12},{20,16},{24,20},{28,24},{5,1},{9,5},{13... | collective-permute-start | bytes 1179656 | tf_op jit(solution)/shard_map/ppermute | solution.py:81
  213.6 9.4 %copy-start.18 = (f32[4,6,32,128]{3,2,1,0:T(8,128)}, f32[4,6,32,128]{3,2,1,0:T(8,128)S(1)}, u32[]{:S(2)}) copy-start(f32[4,6,32,128]{3,2,1,0:T(8,128)S(1)} %collective-permute-done.4) | copy-start | bytes 1179652
  225.0 16.4 %collective-permute-start.6 = (f32[4,20,6,128]{3,2,1,0:T(8,128)}, f32[4,20,6,128]{3,2,1,0:T(8,128)}, u32[]{:S(2)}, u32[]{:S(2)}) collective-permute-start(f32[4,20,6,128]{3,2,1,0:T(8,128)} %get-tuple-element.86), channel_id=1, source_target_pairs={{0,1},{1,2},{2,3},{4,5},{5,6},{6,7},{8,9},{9,10},{10,11},{12,13},{... | collective-permute-start | bytes 737288 | tf_op jit(solution)/shard_map/ppermute | solution.py:78
  228.1 13.3 %collective-permute-start.7 = (f32[4,20,6,128]{3,2,1,0:T(8,128)}, f32[4,20,6,128]{3,2,1,0:T(8,128)}, u32[]{:S(2)}, u32[]{:S(2)}) collective-permute-start(f32[4,20,6,128]{3,2,1,0:T(8,128)} %get-tuple-element.87), channel_id=1, source_target_pairs={{1,0},{2,1},{3,2},{5,4},{6,5},{7,6},{9,8},{10,9},{11,10},{13,12},{... | collective-permute-start | bytes 737288 | tf_op jit(solution)/shard_map/ppermute | solution.py:81
  238.4 3.1 copy-start.14
  238.4 3.1 copy-start.19
  238.4 3.1 copy-start.22
  243.0 4.4 %copy-start.3 = (f32[20,44,128]{2,1,0:T(8,128)S(1)}, f32[20,44,128]{2,1,0:T(8,128)}, u32[]{:S(2)}) copy-start(f32[20,44,128]{2,1,0:T(8,128)} %copy-done.2) | copy-start | bytes 1351684
  251.8 3.5 copy-start.20
  251.8 3.5 copy-start.23
  255.4 8.9 %copy-start.11 = (f32[8,20,6,128]{3,2,1,0:T(8,128)S(1)}, f32[8,20,6,128]{3,2,1,0:T(8,128)}, u32[]{:S(2)}) copy-start(f32[8,20,6,128]{3,2,1,0:T(8,128)} %copy-done.10) | copy-start | bytes 1474564
  255.4 8.9 %copy-start.13 = (f32[8,20,6,128]{3,2,1,0:T(8,128)S(1)}, f32[8,20,6,128]{3,2,1,0:T(8,128)}, u32[]{:S(2)}) copy-start(f32[8,20,6,128]{3,2,1,0:T(8,128)} %copy-done.12) | copy-start | bytes 1474564
  255.4 8.9 %copy-start.17 = (f32[4,8,32,128]{3,2,1,0:T(8,128)S(1)}, f32[4,8,32,128]{3,2,1,0:T(8,128)}, u32[]{:S(2)}) copy-start(f32[4,8,32,128]{3,2,1,0:T(8,128)} %param.13) | copy-start | bytes 1572868
  268.8 20.1 %copy-start.28 = (f32[8,32,16]{2,1,0:T(8,128)S(1)}, f32[8,32,16]{2,1,0:T(8,128)}, u32[]{:S(2)}) copy-start(f32[8,32,16]{2,1,0:T(8,128)} %copy.160) | copy-start | bytes 49156
  268.8 20.1 %copy-start.29 = (f32[8,32,16]{2,1,0:T(8,128)S(1)}, f32[8,32,16]{2,1,0:T(8,128)}, u32[]{:S(2)}) copy-start(f32[8,32,16]{2,1,0:T(8,128)} %copy.159) | copy-start | bytes 49156
  268.9 20.1 %copy-start.30 = (f32[8,32,16]{2,1,0:T(8,128)S(1)}, f32[8,32,16]{2,1,0:T(8,128)}, u32[]{:S(2)}) copy-start(f32[8,32,16]{2,1,0:T(8,128)} %copy.162) | copy-start | bytes 49156
  268.9 20.1 %copy-start.31 = (f32[8,32,16]{2,1,0:T(8,128)S(1)}, f32[8,32,16]{2,1,0:T(8,128)}, u32[]{:S(2)}) copy-start(f32[8,32,16]{2,1,0:T(8,128)} %copy.161) | copy-start | bytes 49156
  (13 other events, 23.3 us)
where the time goes:
time: 360 us; the launch traced here: 357 us
  Pallas kernels  115 us (32%)
  other arithmetic  98.7 us (27%)
  local copies, waits for them, and re-layouts  86.5 us (24%)
  waiting for transfers between devices  28.9 us (8%)
  starting transfers between devices  19.6 us (5%)
  between operations  8.14 us (2%)
    pallas_call x10, Pallas kernels, exchange(): pl.pallas_call(functools.partial(_exchange_kernel, axis, n, scatter), out...  115 us
    ppermute x4, waiting for transfers between devices, padded_2(): lax.ppermute(lax.slice_in_dim(block, 0, width, axis=dim), axis, backward)  24.9 us
    unnamed x81, local copies, waits for them, and re-layouts  21.5 us
    add x8, other arithmetic, chebyshev(): step_dir = rho_next * rho * step_dir + 2.0 * rho_next / delta * remain  21.4 us
    unnamed x2, other arithmetic  20.7 us
    scatter-add x1, other arithmetic, per_device(): source = jnp.zeros((sources, cx * cy * cz), jnp.float32).at[:, local].add...  15.3 us
    ppermute x4, starting transfers between devices, padded_2(): lax.ppermute(lax.slice_in_dim(block, block.shape[dim] - width, None, axis...  14.3 us
    reshape x1, local copies, waits for them, and re-layouts, per_device(): source = jnp.zeros((sources, cx * cy * cz), jnp.float32).at[:, local].add...  10.7 us
  transfers between devices with their start and end apart: 8, of which 4 were waited for; matrix products, arithmetic and copies ran while one was open for 9% of the time, Pallas kernels for 0%

commit v1 on v0

--- a/solution.py
+++ b/solution.py
@@ -147,8 +147,11 @@
     beta_prev,
 ):
     sources, cx, cy, cz = background.shape
-    kappa = regional(labels, kappa_table)
-    absorb = regional(labels, absorb_table)
+    regions = kappa_table.shape[0]
+    label_hot = (labels.reshape(1, -1) == jnp.arange(regions)[:, None]).astype(jnp.float32)
+    tables = jnp.stack([kappa_table, absorb_table])
+    fields = jnp.dot(tables, label_hot, precision=lax.Precision.HIGHEST).reshape(2, cx, cy, cz)
+    kappa, absorb = fields[0], fields[1]
     n_src = lax.axis_size("src")
     slab = v_kappa.shape[2]
     pair = jnp.stack([v_kappa, v_absorb]).reshape(-1, 128)
@@ -189,9 +192,13 @@
     anchor_x = lax.axis_index("gx") * cx
     anchor_y = lax.axis_index("gy") * cy
     owned = (ix >= anchor_x) & (ix < anchor_x + cx) & (iy >= anchor_y) & (iy < anchor_y + cy)
-    local = jnp.where(owned, ((ix - anchor_x) * cy + (iy - anchor_y)) * cz + iz, 0)
-    seen = jnp.where(owned[None, :], change.reshape(sources, -1)[:, local], 0.0)
-    base = jnp.where(owned[None, :], background.reshape(sources, -1)[:, local], 0.0)
+    plane = (ix - anchor_x) * cy + (iy - anchor_y)
+    plane_hot = (jnp.arange(cx * cy)[:, None] == plane[None, :]) & owned[None, :]
+    depth_hot = (jnp.arange(cz)[:, None] == iz[None, :]).astype(jnp.float32)
+    both = jnp.concatenate([change, background], axis=0).reshape(-1, cz)
+    picked = jnp.dot(both, depth_hot, precision=lax.Precision.HIGHEST).reshape(2 * sources, cx * cy, -1)
+    picked = jnp.sum(jnp.where(plane_hot[None], picked, 0.0), axis=1)
+    seen, base = picked[:sources], picked[sources:]
     partial = jnp.stack(
         [
             jnp.sum(base, axis=1),
@@ -208,13 +215,8 @@
     jv_vals = (seen - ratio * seen_sum) / mean_base
     ratio_jv = (cross / total - seen_sum * (square / (total * total))) / mean_base
     weight = (jv_vals - ratio_jv) / mean_base
-    deposit = jnp.where(owned[None, :], weight, 0.0)
-    source = (
-        jnp.zeros((sources, cx * cy * cz), jnp.float32)
-        .at[:, local]
-        .add(deposit)
-        .reshape(change.shape)
-    )
+    spread = jnp.where(plane_hot[None], weight[:, None, :], 0.0).reshape(sources * cx * cy, -1)
+    source = jnp.dot(spread, depth_hot.T, precision=lax.Precision.HIGHEST).reshape(change.shape)
     dual_w = chebyshev(padded_2(source, (("gx", 1), ("gy", 2)), width), apply_op)
     ring = (slice(None), slice(width - 1, width + cx + 1), slice(width - 1, width + cy + 1))
     phi_near = beside(phi_w[ring])

time: 360 us -> 280 us (0.78)
  local copies, waits for them, and re-layouts: 86.5 us -> 30 us
  other arithmetic: 98.7 us -> 58.5 us
  waiting for transfers between devices: 28.9 us -> 56.7 us
  Pallas kernels: 115 us -> 97.4 us
  matrix products: 0 us -> 9.25 us
    ppermute x4, waiting for transfers between devices: 4.04 us -> 25.6 us  [padded_2(): lax.ppermute(lax.slice_in_dim(block, block.shape[dim] - width, None, axis...]
    unnamed x2 -> x0, other arithmetic: 20.7 us -> none
    gather x2 -> x0, local copies, waits for them, and re-layouts: 19.5 us -> none  [the longest x1 9.75 us: per_device(): seen = jnp.where(owned[None, :], change.reshape(sources, -1)[:, local], 0.0)]
    pallas_call x10, Pallas kernels: 115 us -> 97.4 us  [exchange(): pl.pallas_call(functools.partial(_exchange_kernel, axis, n, scatter), out...]
    scatter-add x1 -> x0, other arithmetic: 15.3 us -> none  [per_device(): source = jnp.zeros((sources, cx * cy * cz), jnp.float32).at[:, local].add...]
    reshape x1 -> x0, local copies, waits for them, and re-layouts: 10.7 us -> none  [per_device(): source = jnp.zeros((sources, cx * cy * cz), jnp.float32).at[:, local].add...]
    slice x2 -> x1, local copies, waits for them, and re-layouts: 9.75 us -> 0.01 us  [per_device(): change = chebyshev(rhs, apply_op)[:, width:width + cx, width:width + cy, :]]
    dot_general x0 -> x3, matrix products: none -> 9.25 us  [the longest x1 4.24 us: per_device(): jnp.dot(both, depth_hot, precision=lax.Precision.HIGHEST)]
  transfers between devices with their start and end apart: 8 -> 8, of which waited for: 4 -> 6; matrix products, arithmetic and copies ran while one was open for 9% -> 4% of each run, Pallas kernels for 0% -> 0%
where the time goes in v1:
time: 280 us; the launch traced here: 278 us
  Pallas kernels  97.4 us (35%)
  other arithmetic  58.5 us (21%)
  waiting for transfers between devices  56.7 us (20%)
  local copies, waits for them, and re-layouts  30 us (11%)
  starting transfers between devices  18.1 us (6%)
  matrix products  9.25 us (3%)
  between operations  8.26 us (3%)
    pallas_call x10, Pallas kernels, exchange(): pl.pallas_call(functools.partial(_exchange_kernel, axis, n, scatter), out...  97.4 us
    ppermute x4, waiting for transfers between devices, padded_2(): lax.ppermute(lax.slice_in_dim(block, 0, width, axis=dim), axis, backward)  31.1 us
    ppermute x4, waiting for transfers between devices, padded_2(): lax.ppermute(lax.slice_in_dim(block, block.shape[dim] - width, None, axis...  25.6 us
    add x8, other arithmetic, chebyshev(): step_dir = rho_next * rho * step_dir + 2.0 * rho_next / delta * remain  21.3 us
    unnamed x82, local copies, waits for them, and re-layouts  13.7 us
    ppermute x4, starting transfers between devices, padded_2(): lax.ppermute(lax.slice_in_dim(block, block.shape[dim] - width, None, axis...  12.9 us
    add x2, other arithmetic, chebyshev(): solution = solution + step_dir  9.37 us
    reduce_sum x8, other arithmetic, small_sum(): packed = jnp.sum(exchange(packed, axis, first_id + i), axis=0)  8.98 us
  transfers between devices with their start and end apart: 8, of which 6 were waited for; matrix products, arithmetic and copies ran while one was open for 4% of the time, Pallas kernels for 0%

profile of v1, /device:TPU:1, one launch (start us, length us, event | category | flops | bytes accessed | tf_op | source)
XLA Modules:
  0.0 278.2 jit_solution(11652153939461795378)
XLA Ops:
  4.6 16.7 %shard_map.121 = f32[8,64,128]{2,1,0:T(8,128)} custom-call(f32[64,128]{1,0:T(8,128)} %reshape.347.x_ref), custom_call_target="tpu_custom_call" | custom-call | tf_op jit(solution)/shard_map/pallas_call | solution.py:50
  28.1 3.2 %collective-permute-start.1 = (f32[8,6,32,128]{3,2,1,0:T(8,128)}, f32[8,6,32,128]{3,2,1,0:T(8,128)S(1)}, u32[]{:S(2)}, u32[]{:S(2)}) collective-permute-start(f32[8,6,32,128]{3,2,1,0:T(8,128)} %get-tuple-element.65), channel_id=1, source_target_pairs={{0,4},{4,8},{8,12},{12,16},{16,20},{20,24},{24,28},{1,5},{5,9},{9,... | collective-permute-start | bytes 2359304 | tf_op jit(solution)/shard_map/ppermute | solution.py:78
  32.8 15.7 %collective-permute-done.1 = f32[8,6,32,128]{3,2,1,0:T(8,128)S(1)} collective-permute-done((f32[8,6,32,128]{3,2,1,0:T(8,128)}, f32[8,6,32,128]{3,2,1,0:T(8,128)S(1)}, u32[]{:S(2)}, u32[]{:S(2)}) %collective-permute-start.1) | collective-permute-done | bytes 786464 | tf_op jit(solution)/shard_map/ppermute | solution.py:78
  48.5 18.2 %collective-permute-done = f32[8,6,32,128]{3,2,1,0:T(8,128)S(1)} collective-permute-done((f32[8,6,32,128]{3,2,1,0:T(8,128)S(1)}, f32[8,6,32,128]{3,2,1,0:T(8,128)S(1)}, u32[]{:S(2)}, u32[]{:S(2)}) %collective-permute-start) | collective-permute-done | bytes 786464 | tf_op jit(solution)/shard_map/ppermute | solution.py:81
  67.1 3.2 %collective-permute-start.2 = (f32[8,20,6,128]{3,0,2,1:T(8,128)S(1)}, f32[8,20,6,128]{3,0,2,1:T(8,128)S(1)}, u32[]{:S(2)}, u32[]{:S(2)}) collective-permute-start(f32[8,20,6,128]{3,0,2,1:T(8,128)S(1)} %copy.52), channel_id=1, source_target_pairs={{0,1},{1,2},{2,3},{4,5},{5,6},{6,7},{8,9},{9,10},{10,11},{12,13},{... | collective-permute-start | bytes 1474568 | tf_op jit(solution)/shard_map/ppermute | solution.py:78
  73.1 6.5 %collective-permute-done.2 = f32[8,20,6,128]{3,0,2,1:T(8,128)S(1)} collective-permute-done((f32[8,20,6,128]{3,0,2,1:T(8,128)S(1)}, f32[8,20,6,128]{3,0,2,1:T(8,128)S(1)}, u32[]{:S(2)}, u32[]{:S(2)}) %collective-permute-start.2) | collective-permute-done | bytes 491552 | tf_op jit(solution)/shard_map/ppermute | solution.py:78
  79.8 4.0 %collective-permute-done.3 = f32[8,20,6,128]{3,0,2,1:T(8,128)S(1)} collective-permute-done((f32[8,20,6,128]{3,0,2,1:T(8,128)S(1)}, f32[8,20,6,128]{3,0,2,1:T(8,128)S(1)}, u32[]{:S(2)}, u32[]{:S(2)}) %collective-permute-start.3) | collective-permute-done | bytes 491552 | tf_op jit(solution)/shard_map/ppermute | solution.py:81
  90.5 2.3 multiply_add_fusion.7
  92.9 2.2 multiply_add_fusion.6
  95.1 2.2 multiply_add_fusion.5
  97.4 2.2 multiply_add_fusion.4
  102.5 4.2 %select_reduce_fusion = f32[8,1024]{1,0:T(8,128)S(1)} fusion(pred[256,1024]{1,0:T(8,128)(4,1)S(1)} %fusion.216, f32[8,256,128]{2,1,0:T(8,128)S(1)} %bitcast.63, s32[1024]{0:T(1024)S(1)} %get-tuple-element.93), kind=kOutput, calls=%fused_computation.66 | convolution fusion | flops 3225542656 | bytes 1347584 | tf_op jit(solution)/shard_map/dot_general | solution.py:199
  107.8 6.0 %shard_map.122 = f32[4,8,128]{2,1,0:T(8,128)} custom-call(f32[8,128]{1,0:T(8,128)} %pad_bitcast_fusion.1.x_ref), custom_call_target="tpu_custom_call" | custom-call | tf_op jit(solution)/shard_map/pallas_call | solution.py:50
  115.1 7.8 %shard_map.123 = f32[8,8,128]{2,1,0:T(8,128)} custom-call(f32[8,128]{1,0:T(8,128)} %reduce_sum.248.x_ref), custom_call_target="tpu_custom_call" | custom-call | tf_op jit(solution)/shard_map/pallas_call | solution.py:50
  125.6 3.3 %fusion = f32[4,8,32,128]{3,2,1,0:T(8,128)S(1)} fusion(f32[4,1024]{1,0:T(4,128)S(1)} %subtract_divide_fusion, pred[8,32,1024]{2,1,0:T(8,128)(4,1)} %compare_and_fusion, s32[1024]{0:T(1024)S(1)} %get-tuple-element.93), kind=kOutput, calls=%fused_computation.67 | convolution fusion | flops 1611792384 | bytes 806912 | tf_op jit(solution)/shard_map/dot_general | solution.py:219
  129.0 3.2 %collective-permute-start.4 = (f32[4,6,32,128]{3,2,1,0:T(8,128)S(1)}, f32[4,6,32,128]{3,2,1,0:T(8,128)S(1)}, u32[]{:S(2)}, u32[]{:S(2)}) collective-permute-start(f32[4,6,32,128]{3,2,1,0:T(8,128)S(1)} %get-tuple-element.67), channel_id=1, source_target_pairs={{0,4},{4,8},{8,12},{12,16},{16,20},{20,24},{24,28},{1,5},{5,9},{9,... | collective-permute-start | bytes 1179656 | tf_op jit(solution)/shard_map/ppermute | solution.py:78
  133.6 3.4 %collective-permute-done.4 = f32[4,6,32,128]{3,2,1,0:T(8,128)S(1)} collective-permute-done((f32[4,6,32,128]{3,2,1,0:T(8,128)S(1)}, f32[4,6,32,128]{3,2,1,0:T(8,128)S(1)}, u32[]{:S(2)}, u32[]{:S(2)}) %collective-permute-start.4) | collective-permute-done | bytes 393248 | tf_op jit(solution)/shard_map/ppermute | solution.py:78
  136.9 8.8 %collective-permute-done.5 = f32[4,6,32,128]{3,2,1,0:T(8,128)S(1)} collective-permute-done((f32[4,6,32,128]{3,2,1,0:T(8,128)S(1)}, f32[4,6,32,128]{3,2,1,0:T(8,128)S(1)}, u32[]{:S(2)}, u32[]{:S(2)}) %collective-permute-start.5) | collective-permute-done | bytes 393248 | tf_op jit(solution)/shard_map/ppermute | solution.py:81
  146.8 3.2 %collective-permute-start.6 = (f32[4,20,6,128]{3,2,1,0:T(8,128)}, f32[4,20,6,128]{3,2,1,0:T(8,128)}, u32[]{:S(2)}, u32[]{:S(2)}) collective-permute-start(f32[4,20,6,128]{3,2,1,0:T(8,128)} %get-tuple-element.63), channel_id=1, source_target_pairs={{0,1},{1,2},{2,3},{4,5},{5,6},{6,7},{8,9},{9,10},{10,11},{12,13},{... | collective-permute-start | bytes 737288 | tf_op jit(solution)/shard_map/ppermute | solution.py:78
  160.3 3.0 %select_maximum_fusion = f32[4,10,34,130]{3,2,1,0:T(8,128)} fusion(f32[8,20,6,128]{3,2,1,0:T(8,128)} %copy-done.12, f32[8,20,6,128]{3,2,1,0:T(8,128)} %copy-done.10, f32[8,6,32,128]{3,2,1,0:T(8,128)} %copy-done.7, f32[8,8,32,128]{3,2,1,0:T(8,128)S(1)} %constant_dynamic-update-slice_fusion, f32[8,6,32,128]{3,2,1,0:T(8,128)} %copy-done.4), kind=kLoop, calls=%fused_computation.308 | loop fusion | flops 2121600 | bytes 4311680 | tf_op jit(solution)/shard_map/slice | solution.py:222
  164.9 4.3 %multiply_add_fusion.3 = (f32[4,20,44,128]{3,2,1,0:T(8,128)S(1)}, f32[4,20,44,128]{3,2,1,0:T(8,128)S(1)}) fusion(f32[4,20,6,128]{3,2,1,0:T(8,128)} %collective-permute-done.7, f32[4,6,32,128]{3,2,1,0:T(8,128)S(1)} %copy-done.22, f32[4,8,32,128]{3,2,1,0:T(8,128)S(1)} %copy-done.15, f32[4,6,32,128]{3,2,1,0:T(8,128)S(1)} %copy-done.20, ...), kind=kLoop, calls=%fused_computation.301 | loop fusion | flops 12165120 | bytes 10362880 | tf_op jit(solution)/shard_map/add | solution.py:132
  169.2 2.2 multiply_add_fusion.2
  171.4 2.2 multiply_add_fusion.1
  173.7 3.5 %multiply_add_fusion = (f32[4,20,44,128]{3,2,1,0:T(8,128)}, f32[4,20,44,128]{3,2,1,0:T(8,128)}) fusion(f32[4,20,44,128]{3,2,1,0:T(8,128)S(1)} %get-tuple-element.35, f32[4,20,44,128]{3,2,1,0:T(8,128)S(1)} %get-tuple-element.36, f32[20,44,128]{2,1,0:T(8,128)S(1)} %copy-done.1, f32[20,44,128]{2,1,0:T(8,128)S(1)} %get-tuple-element.70, ...), kind=kLoop, calls=%fused_computation.298 | loop fusion | flops 10362880 | bytes 10362880 | tf_op jit(solution)/shard_map/add | solution.py:132
  177.2 8.8 %fusion.203 = f32[4,20,44,128]{3,2,1,0:T(8,128)S(1)} fusion(f32[4,20,44,128]{3,2,1,0:T(8,128)} %get-tuple-element.34, f32[4,20,44,128]{3,2,1,0:T(8,128)} %get-tuple-element.33, f32[4,20,44,128]{3,2,1,0:T(8,128)S(1)} %get-tuple-element.35, f32[4,20,44,128]{3,2,1,0:T(8,128)S(1)} %get-tuple-element.37, f32[4,20,44,128]{3,2,1,0:T(8,128)S(1)} %get-tuple-element.39, ...), kind=kLoop, calls=%fused_computation.286 | loop fusion | flops 14868480 | bytes 15769600 | tf_op jit(solution)/shard_map/add | solution.py:128
  191.9 18.3 %shard_map.124 = f32[8,64,128]{2,1,0:T(8,128)} custom-call(f32[8,64,128]{2,1,0:T(8,128)} %reshape.351.x_ref), custom_call_target="tpu_custom_call" | custom-call | tf_op jit(solution)/shard_map/pallas_call | solution.py:50
  214.2 7.4 %shard_map.125 = f32[4,8,128]{2,1,0:T(8,128)} custom-call(f32[8,128]{1,0:T(8,128)} %fusion.272.x_ref), custom_call_target="tpu_custom_call" | custom-call | tf_op jit(solution)/shard_map/pallas_call | solution.py:50
  222.9 7.1 %shard_map.126 = f32[8,8,128]{2,1,0:T(8,128)} custom-call(f32[8,128]{1,0:T(8,128)} %reduce_sum.262.x_ref), custom_call_target="tpu_custom_call" | custom-call | tf_op jit(solution)/shard_map/pallas_call | solution.py:50
  231.4 10.9 %shard_map.127 = f32[8,8,128]{2,1,0:T(8,128)} custom-call(f32[8,128]{1,0:T(8,128)} %reduce_sum.263.x_ref), custom_call_target="tpu_custom_call" | custom-call | tf_op jit(solution)/shard_map/pallas_call | solution.py:50
  248.2 5.4 %shard_map.128 = f32[4,8,128]{2,1,0:T(8,128)} custom-call(f32[8,128]{1,0:T(8,128)} %pad_bitcast_fusion.x_ref), custom_call_target="tpu_custom_call" | custom-call | tf_op jit(solution)/shard_map/pallas_call | solution.py:50
  254.9 6.4 %shard_map.129 = f32[8,8,128]{2,1,0:T(8,128)} custom-call(f32[8,128]{1,0:T(8,128)} %reduce_sum.267.x_ref), custom_call_target="tpu_custom_call" | custom-call | tf_op jit(solution)/shard_map/pallas_call | solution.py:50
  262.7 11.4 %shard_map.130 = f32[8,8,128]{2,1,0:T(8,128)} custom-call(f32[8,128]{1,0:T(8,128)} %reduce_sum.268.x_ref), custom_call_target="tpu_custom_call" | custom-call | tf_op jit(solution)/shard_map/pallas_call | solution.py:50
  (170 shorter events, 62.2 us)
Async XLA Ops:
  0.6 3.0 %copy-start.31 = (f32[8,32,16]{1,2,0:T(8,128)S(1)}, f32[8,32,16]{1,2,0:T(8,128)}, u32[]{:S(2)}) copy-start(f32[8,32,16]{1,2,0:T(8,128)} %param.15) | copy-start | bytes 49156
  0.6 3.0 %copy-start.33 = (f32[8,32,16]{1,2,0:T(8,128)S(1)}, f32[8,32,16]{1,2,0:T(8,128)}, u32[]{:S(2)}) copy-start(f32[8,32,16]{1,2,0:T(8,128)} %param.16) | copy-start | bytes 49156
  26.9 5.7 %copy-start.35 = (s32[1024]{0:T(1024)S(1)}, s32[1024]{0:T(1024)}, u32[]{:S(2)}) copy-start(s32[1024]{0:T(1024)} %param.14) | copy-start | bytes 12292
  28.1 20.4 %collective-permute-start.1 = (f32[8,6,32,128]{3,2,1,0:T(8,128)}, f32[8,6,32,128]{3,2,1,0:T(8,128)S(1)}, u32[]{:S(2)}, u32[]{:S(2)}) collective-permute-start(f32[8,6,32,128]{3,2,1,0:T(8,128)} %get-tuple-element.65), channel_id=1, source_target_pairs={{0,4},{4,8},{8,12},{12,16},{16,20},{20,24},{24,28},{1,5},{5,9},{9,... | collective-permute-start | bytes 2359304 | tf_op jit(solution)/shard_map/ppermute | solution.py:78
  31.3 35.4 %collective-permute-start = (f32[8,6,32,128]{3,2,1,0:T(8,128)S(1)}, f32[8,6,32,128]{3,2,1,0:T(8,128)S(1)}, u32[]{:S(2)}, u32[]{:S(2)}) collective-permute-start(f32[8,6,32,128]{3,2,1,0:T(8,128)S(1)} %get-tuple-element.66), channel_id=1, source_target_pairs={{4,0},{8,4},{12,8},{16,12},{20,16},{24,20},{28,24},{5,1},{9,5},{13... | collective-permute-start | bytes 2359304 | tf_op jit(solution)/shard_map/ppermute | solution.py:81
  48.5 36.1 %copy-start.4 = (f32[8,6,32,128]{3,2,1,0:T(8,128)}, f32[8,6,32,128]{3,2,1,0:T(8,128)S(1)}, u32[]{:S(2)}) copy-start(f32[8,6,32,128]{3,2,1,0:T(8,128)S(1)} %collective-permute-done.1) | copy-start | bytes 2359300
  66.7 17.9 %copy-start.7 = (f32[8,6,32,128]{3,2,1,0:T(8,128)}, f32[8,6,32,128]{3,2,1,0:T(8,128)S(1)}, u32[]{:S(2)}) copy-start(f32[8,6,32,128]{3,2,1,0:T(8,128)S(1)} %collective-permute-done) | copy-start | bytes 2359300
  67.1 12.5 %collective-permute-start.2 = (f32[8,20,6,128]{3,0,2,1:T(8,128)S(1)}, f32[8,20,6,128]{3,0,2,1:T(8,128)S(1)}, u32[]{:S(2)}, u32[]{:S(2)}) collective-permute-start(f32[8,20,6,128]{3,0,2,1:T(8,128)S(1)} %copy.52), channel_id=1, source_target_pairs={{0,1},{1,2},{2,3},{4,5},{5,6},{6,7},{8,9},{9,10},{10,11},{12,13},{... | collective-permute-start | bytes 1474568 | tf_op jit(solution)/shard_map/ppermute | solution.py:78
  70.7 13.2 %collective-permute-start.3 = (f32[8,20,6,128]{3,0,2,1:T(8,128)S(1)}, f32[8,20,6,128]{3,0,2,1:T(8,128)S(1)}, u32[]{:S(2)}, u32[]{:S(2)}) collective-permute-start(f32[8,20,6,128]{3,0,2,1:T(8,128)S(1)} %copy.53), channel_id=1, source_target_pairs={{1,0},{2,1},{3,2},{5,4},{6,5},{7,6},{9,8},{10,9},{11,10},{13,12},{... | collective-permute-start | bytes 1474568 | tf_op jit(solution)/shard_map/ppermute | solution.py:81
  79.8 10.6 %copy-start.10 = (f32[8,20,6,128]{3,2,1,0:T(8,128)}, f32[8,20,6,128]{3,2,1,0:T(8,128)S(1)}, u32[]{:S(2)}) copy-start(f32[8,20,6,128]{3,2,1,0:T(8,128)S(1)} %copy.54) | copy-start | bytes 1474564
  84.0 6.4 %copy-start.12 = (f32[8,20,6,128]{3,2,1,0:T(8,128)}, f32[8,20,6,128]{3,2,1,0:T(8,128)S(1)}, u32[]{:S(2)}) copy-start(f32[8,20,6,128]{3,2,1,0:T(8,128)S(1)} %copy.55) | copy-start | bytes 1474564
  87.4 9.9 %copy-start = (f32[20,44,128]{2,1,0:T(8,128)}, f32[20,44,128]{2,1,0:T(8,128)S(1)}, u32[]{:S(2)}) copy-start(f32[20,44,128]{2,1,0:T(8,128)S(1)} %get-tuple-element.74) | copy-start | bytes 1351684
  90.5 9.1 %copy-start.2 = (f32[20,44,128]{2,1,0:T(8,128)}, f32[20,44,128]{2,1,0:T(8,128)S(1)}, u32[]{:S(2)}) copy-start(f32[20,44,128]{2,1,0:T(8,128)S(1)} %get-tuple-element.50) | copy-start | bytes 1351684
  128.9 16.9 %copy-start.14 = (f32[4,8,32,128]{3,2,1,0:T(8,128)}, f32[4,8,32,128]{3,2,1,0:T(8,128)S(1)}, u32[]{:S(2)}) copy-start(f32[4,8,32,128]{3,2,1,0:T(8,128)S(1)} %fusion) | copy-start | bytes 1572868
  128.9 22.4 %copy-start.32 = (f32[8,32,16]{1,2,0:T(8,128)S(1)}, f32[8,32,16]{1,2,0:T(8,128)}, u32[]{:S(2)}) copy-start(f32[8,32,16]{1,2,0:T(8,128)} %param.15) | copy-start | bytes 49156
  128.9 22.4 %copy-start.34 = (f32[8,32,16]{1,2,0:T(8,128)S(1)}, f32[8,32,16]{1,2,0:T(8,128)}, u32[]{:S(2)}) copy-start(f32[8,32,16]{1,2,0:T(8,128)} %param.16) | copy-start | bytes 49156
  129.0 7.9 %collective-permute-start.4 = (f32[4,6,32,128]{3,2,1,0:T(8,128)S(1)}, f32[4,6,32,128]{3,2,1,0:T(8,128)S(1)}, u32[]{:S(2)}, u32[]{:S(2)}) collective-permute-start(f32[4,6,32,128]{3,2,1,0:T(8,128)S(1)} %get-tuple-element.67), channel_id=1, source_target_pairs={{0,4},{4,8},{8,12},{12,16},{16,20},{20,24},{24,28},{1,5},{5,9},{9,... | collective-permute-start | bytes 1179656 | tf_op jit(solution)/shard_map/ppermute | solution.py:78
  132.3 13.5 %collective-permute-start.5 = (f32[4,6,32,128]{3,2,1,0:T(8,128)S(1)}, f32[4,6,32,128]{3,2,1,0:T(8,128)S(1)}, u32[]{:S(2)}, u32[]{:S(2)}) collective-permute-start(f32[4,6,32,128]{3,2,1,0:T(8,128)S(1)} %get-tuple-element.68), channel_id=1, source_target_pairs={{4,0},{8,4},{12,8},{16,12},{20,16},{24,20},{28,24},{5,1},{9,5},{13... | collective-permute-start | bytes 1179656 | tf_op jit(solution)/shard_map/ppermute | solution.py:81
  136.9 9.8 %copy-start.19 = (f32[4,6,32,128]{3,2,1,0:T(8,128)}, f32[4,6,32,128]{3,2,1,0:T(8,128)S(1)}, u32[]{:S(2)}) copy-start(f32[4,6,32,128]{3,2,1,0:T(8,128)S(1)} %collective-permute-done.4) | copy-start | bytes 1179652
  146.8 16.5 %collective-permute-start.6 = (f32[4,20,6,128]{3,2,1,0:T(8,128)}, f32[4,20,6,128]{3,2,1,0:T(8,128)}, u32[]{:S(2)}, u32[]{:S(2)}) collective-permute-start(f32[4,20,6,128]{3,2,1,0:T(8,128)} %get-tuple-element.63), channel_id=1, source_target_pairs={{0,1},{1,2},{2,3},{4,5},{5,6},{6,7},{8,9},{9,10},{10,11},{12,13},{... | collective-permute-start | bytes 737288 | tf_op jit(solution)/shard_map/ppermute | solution.py:78
  150.0 13.3 %collective-permute-start.7 = (f32[4,20,6,128]{3,2,1,0:T(8,128)}, f32[4,20,6,128]{3,2,1,0:T(8,128)}, u32[]{:S(2)}, u32[]{:S(2)}) collective-permute-start(f32[4,20,6,128]{3,2,1,0:T(8,128)} %get-tuple-element.64), channel_id=1, source_target_pairs={{1,0},{2,1},{3,2},{5,4},{6,5},{7,6},{9,8},{10,9},{11,10},{13,12},{... | collective-permute-start | bytes 737288 | tf_op jit(solution)/shard_map/ppermute | solution.py:81
  160.3 3.1 %copy-start.15 = (f32[4,8,32,128]{3,2,1,0:T(8,128)S(1)}, f32[4,8,32,128]{3,2,1,0:T(8,128)}, u32[]{:S(2)}) copy-start(f32[4,8,32,128]{3,2,1,0:T(8,128)} %copy-done.14) | copy-start | bytes 1572868
  160.3 3.1 %copy-start.20 = (f32[4,6,32,128]{3,2,1,0:T(8,128)S(1)}, f32[4,6,32,128]{3,2,1,0:T(8,128)}, u32[]{:S(2)}) copy-start(f32[4,6,32,128]{3,2,1,0:T(8,128)} %copy-done.19) | copy-start | bytes 1179652
  160.3 3.1 %copy-start.22 = (f32[4,6,32,128]{3,2,1,0:T(8,128)S(1)}, f32[4,6,32,128]{3,2,1,0:T(8,128)}, u32[]{:S(2)}) copy-start(f32[4,6,32,128]{3,2,1,0:T(8,128)} %copy-done.21) | copy-start | bytes 1179652
  164.9 4.3 %copy-start.3 = (f32[20,44,128]{2,1,0:T(8,128)S(1)}, f32[20,44,128]{2,1,0:T(8,128)}, u32[]{:S(2)}) copy-start(f32[20,44,128]{2,1,0:T(8,128)} %copy-done.2) | copy-start | bytes 1351684
  177.2 8.9 %copy-start.11 = (f32[8,20,6,128]{3,2,1,0:T(8,128)S(1)}, f32[8,20,6,128]{3,2,1,0:T(8,128)}, u32[]{:S(2)}) copy-start(f32[8,20,6,128]{3,2,1,0:T(8,128)} %copy-done.10) | copy-start | bytes 1474564
  177.2 8.9 %copy-start.13 = (f32[8,20,6,128]{3,2,1,0:T(8,128)S(1)}, f32[8,20,6,128]{3,2,1,0:T(8,128)}, u32[]{:S(2)}) copy-start(f32[8,20,6,128]{3,2,1,0:T(8,128)} %copy-done.12) | copy-start | bytes 1474564
  177.2 9.0 %copy-start.18 = (f32[4,8,32,128]{3,2,1,0:T(8,128)S(1)}, f32[4,8,32,128]{3,2,1,0:T(8,128)}, u32[]{:S(2)}) copy-start(f32[4,8,32,128]{3,2,1,0:T(8,128)} %param.13) | copy-start | bytes 1572868
  190.7 20.8 %copy-start.27 = (f32[8,32,16]{2,1,0:T(8,128)S(1)}, f32[8,32,16]{2,1,0:T(8,128)}, u32[]{:S(2)}) copy-start(f32[8,32,16]{2,1,0:T(8,128)} %copy.63) | copy-start | bytes 49156
  190.7 20.8 %copy-start.28 = (f32[8,32,16]{2,1,0:T(8,128)S(1)}, f32[8,32,16]{2,1,0:T(8,128)}, u32[]{:S(2)}) copy-start(f32[8,32,16]{2,1,0:T(8,128)} %copy.62) | copy-start | bytes 49156
  190.7 20.8 %copy-start.29 = (f32[8,32,16]{2,1,0:T(8,128)S(1)}, f32[8,32,16]{2,1,0:T(8,128)}, u32[]{:S(2)}) copy-start(f32[8,32,16]{2,1,0:T(8,128)} %copy.65) | copy-start | bytes 49156
  190.7 20.8 %copy-start.30 = (f32[8,32,16]{2,1,0:T(8,128)S(1)}, f32[8,32,16]{2,1,0:T(8,128)}, u32[]{:S(2)}) copy-start(f32[8,32,16]{2,1,0:T(8,128)} %copy.64) | copy-start | bytes 49156
  (13 other events, 21.0 us)

commit v2 on v1

--- a/solution.py
+++ b/solution.py
@@ -62,6 +62,91 @@
     )(x)
 
 
+def _halo_kernel(hx, hy, x_ref, o_ref, wide, send_sem, recv_sem, local_sem):
+    fields, cx, cy, cz = x_ref.shape
+    ax, ay = lax.axis_index("gx"), lax.axis_index("gy")
+    nx, ny = lax.axis_size("gx"), lax.axis_size("gy")
+    wide[...] = jnp.zeros_like(wide)
+    steps = [(dx, dy) for dx in (-1, 0, 1) for dy in (-1, 0, 1) if (dx, dy) != (0, 0)]
+
+    def exists(dx, dy):
+        return (ax + dx >= 0) & (ax + dx < nx) & (ay + dy >= 0) & (ay + dy < ny)
+
+    def window(d, block, halo):
+        if d < 0:
+            return pl.ds(0, halo), pl.ds(block + halo, halo)
+        if d > 0:
+            return pl.ds(block - halo, halo), pl.ds(0, halo)
+        return pl.ds(0, block), pl.ds(halo, block)
+
+    barrier = pltpu.get_barrier_semaphore()
+    for dx, dy in steps:
+        @pl.when(exists(dx, dy))
+        def _():
+            pl.semaphore_signal(
+                barrier, inc=1, device_id={"gx": ax + dx, "gy": ay + dy}, device_id_type=MESH
+            )
+    across = 1 + (ax + nx - 1) // nx + (2 * nx - 2 - ax) // nx
+    along = 1 + (ay + ny - 1) // ny + (2 * ny - 2 - ay) // ny
+    pl.semaphore_wait(barrier, across * along - 1)
+
+    local = pltpu.make_async_copy(
+        x_ref, wide.at[:, pl.ds(hx, cx), pl.ds(hy, cy), :], local_sem
+    )
+    local.start()
+    copies = []
+    for k, (dx, dy) in enumerate(steps):
+        src_x, dst_x = window(dx, cx, hx)
+        src_y, dst_y = window(dy, cy, hy)
+        tx = jnp.clip(ax + dx, 0, nx - 1)
+        ty = jnp.clip(ay + dy, 0, ny - 1)
+        copy = pltpu.make_async_remote_copy(
+            src_ref=x_ref.at[:, src_x, src_y, :],
+            dst_ref=wide.at[:, dst_x, dst_y, :],
+            send_sem=send_sem.at[k],
+            recv_sem=recv_sem.at[k],
+            device_id={"gx": tx, "gy": ty},
+            device_id_type=MESH,
+        )
+        copies.append(copy)
+
+        @pl.when(exists(dx, dy))
+        def _():
+            copy.start()
+
+    local.wait()
+    for copy, (dx, dy) in zip(copies, steps):
+        @pl.when(exists(dx, dy))
+        def _():
+            copy.wait_send()
+
+        @pl.when(exists(-dx, -dy))
+        def _():
+            copy.wait_recv()
+
+    o_ref[...] = wide[...]
+
+
+def halo_block(x, hx, hy, cid):
+    fields, cx, cy, cz = x.shape
+    shape = (fields, cx + 2 * hx, cy + 2 * hy, cz)
+    return pl.pallas_call(
+        functools.partial(_halo_kernel, hx, hy),
+        out_shape=jax.ShapeDtypeStruct(shape, x.dtype),
+        in_specs=[pl.BlockSpec(memory_space=pltpu.VMEM)],
+        out_specs=pl.BlockSpec(memory_space=pltpu.VMEM),
+        scratch_shapes=[
+            pltpu.VMEM(shape, x.dtype),
+            pltpu.SemaphoreType.DMA((8,)),
+            pltpu.SemaphoreType.DMA((8,)),
+            pltpu.SemaphoreType.DMA,
+        ],
+        compiler_params=pltpu.CompilerParams(
+            collective_id=cid, has_side_effects=True, vmem_limit_bytes=48 * 1024 * 1024
+        ),
+    )(x)
+
+
 def small_sum(values, axes, first_id):
     count = values.shape[0]
     packed = jnp.pad(values, (0, 1024 - count)).reshape(8, 128)
@@ -158,15 +243,16 @@
     gathered = exchange(pair, "src", 0).reshape((n_src, 2, cx, cy, slab))
     full_k, full_a = jnp.transpose(gathered, (1, 2, 3, 0, 4)).reshape(2, cx, cy, cz)
     width = ITERS
+    width_y = 8
     stacked = jnp.concatenate([background, kappa[None], absorb[None], full_k[None], full_a[None]], axis=0)
-    wide = padded_2(stacked, (("gx", 1), ("gy", 2)), width)
+    wide = halo_block(stacked, width, width_y, 10)
     phi_w, kappa_w, absorb_w, vk_w, va_w = (
         wide[:sources], wide[sources], wide[sources + 1], wide[sources + 2], wide[sources + 3]
     )
     wx = cx + 2 * width
-    wy = cy + 2 * width
+    wy = cy + 2 * width_y
     gx_at = lax.axis_index("gx") * cx - width + jnp.arange(wx)
-    gy_at = lax.axis_index("gy") * cy - width + jnp.arange(wy)
+    gy_at = lax.axis_index("gy") * cy - width_y + jnp.arange(wy)
     inside = ((gx_at >= 0) & (gx_at < cx * lax.axis_size("gx")))[:, None, None] & (
         (gy_at >= 0) & (gy_at < cy * lax.axis_size("gy"))
     )[None, :, None]
@@ -184,7 +270,7 @@
     for face, near in zip(vk_faces, around(phi_w)):
         rhs = rhs + face * (phi_w - near)
     rhs = -rhs
-    change = chebyshev(rhs, apply_op)[:, width : width + cx, width : width + cy, :]
+    change = chebyshev(rhs, apply_op)[:, width : width + cx, width_y : width_y + cy, :]
     span_y = cy * lax.axis_size("gy")
     ix = det_cells // (span_y * cz)
     iy = det_cells // cz % span_y
@@ -217,11 +303,11 @@
     weight = (jv_vals - ratio_jv) / mean_base
     spread = jnp.where(plane_hot[None], weight[:, None, :], 0.0).reshape(sources * cx * cy, -1)
     source = jnp.dot(spread, depth_hot.T, precision=lax.Precision.HIGHEST).reshape(change.shape)
-    dual_w = chebyshev(padded_2(source, (("gx", 1), ("gy", 2)), width), apply_op)
-    ring = (slice(None), slice(width - 1, width + cx + 1), slice(width - 1, width + cy + 1))
+    dual_w = chebyshev(halo_block(source, width, width_y, 11), apply_op)
+    ring = (slice(None), slice(width - 1, width + cx + 1), slice(width_y - 1, width_y + cy + 1))
     phi_near = beside(phi_w[ring])
     dual_near = beside(dual_w[ring])
-    dual = dual_w[:, width : width + cx, width : width + cy, :]
+    dual = dual_w[:, width : width + cx, width_y : width_y + cy, :]
     grad_a = -jnp.sum(background * dual, axis=0)
     grad_k = jnp.zeros_like(kappa)
     for near_phi, near_dual in zip(phi_near, dual_near):

time: 280 us -> 260 us (0.929)
  Pallas kernels: 97.4 us -> 178 us
  waiting for transfers between devices: 56.7 us -> 0 us
  starting transfers between devices: 18.1 us -> 0 us
  other arithmetic: 58.5 us -> 42.8 us
  local copies, waits for them, and re-layouts: 30 us -> 21.2 us
    ppermute x8 -> x0, waiting for transfers between devices: 56.7 us -> none  [the longest x4 31.1 us: padded_2(): lax.ppermute(lax.slice_in_dim(block, 0, width, axis=dim), axis, backward)]
    pallas_call x10, Pallas kernels: 97.4 us -> 142 us  [exchange(): pl.pallas_call(functools.partial(_exchange_kernel, axis, n, scatter), out...]
    pallas_call x0 -> x2, Pallas kernels: none -> 35.8 us  [halo_block(): pl.pallas_call(functools.partial(_halo_kernel, hx, hy), out_shape=jax.Sha...]
    ppermute x8 -> x0, starting transfers between devices: 18.1 us -> none  [the longest x4 12.9 us: padded_2(): lax.ppermute(lax.slice_in_dim(block, block.shape[dim] - width, None, axis...]
    unnamed x82 -> x48, local copies, waits for them, and re-layouts: 13.7 us -> 5.8 us
    add x2, other arithmetic: 9.37 us -> 3.28 us  [chebyshev(): solution = solution + step_dir]
    slice x3 -> x0, other arithmetic: 4.08 us -> none  [the longest x1 3.01 us: per_device(): phi_near = beside(phi_w[ring])]
    add x8, other arithmetic: 21.3 us -> 18 us  [chebyshev(): step_dir = rho_next * rho * step_dir + 2.0 * rho_next / delta * remain]
  transfers between devices with their start and end apart: 8 -> 0, of which waited for: 6 -> 0; matrix products, arithmetic and copies ran while one was open for 4% -> 0% of each run, Pallas kernels for 0% -> 0%
where the time goes in v2:
time: 260 us; the launch traced here: 259 us
  Pallas kernels  178 us (68%)
  other arithmetic  42.8 us (16%)
  local copies, waits for them, and re-layouts  21.2 us (8%)
  matrix products  9.39 us (4%)
  between operations  7.94 us (3%)
    pallas_call x10, Pallas kernels, exchange(): pl.pallas_call(functools.partial(_exchange_kernel, axis, n, scatter), out...  142 us
    pallas_call x2, Pallas kernels, halo_block(): pl.pallas_call(functools.partial(_halo_kernel, hx, hy), out_shape=jax.Sha...  35.8 us
    add x8, other arithmetic, chebyshev(): step_dir = rho_next * rho * step_dir + 2.0 * rho_next / delta * remain  18 us
    reduce_sum x8, other arithmetic, small_sum(): packed = jnp.sum(exchange(packed, axis, first_id + i), axis=0)  8.98 us
    unnamed x48, local copies, waits for them, and re-layouts  5.8 us
    dot_general x1, matrix products, per_device(): jnp.dot(both, depth_hot, precision=lax.Precision.HIGHEST)  5.35 us

profile of v2, /device:TPU:1, one launch (start us, length us, event | category | flops | bytes accessed | tf_op | source)
XLA Modules:
  0.0 258.9 jit_solution(7830806629090319588)
XLA Ops:
  0.7 1.7 fusion.5
  4.6 16.7 %shard_map.121 = f32[8,64,128]{2,1,0:T(8,128)} custom-call(f32[64,128]{1,0:T(8,128)} %reshape.347.x_ref), custom_call_target="tpu_custom_call" | custom-call | tf_op jit(solution)/shard_map/pallas_call | solution.py:50
  21.3 1.7 reshape.348
  23.0 1.6 fusion.286
  24.6 1.6 copy.47
  27.0 26.6 %shard_map.122 = f32[8,20,48,128]{3,2,1,0:T(8,128)S(1)} custom-call(f32[8,8,32,128]{3,2,1,0:T(8,128)S(1)} %constant_dynamic-update-slice_fusion.x_ref), custom_call_target="tpu_custom_call" | custom-call | tf_op jit(solution)/shard_map/pallas_call | solution.py:133
  56.6 2.0 slice-done
  58.8 2.1 broadcast_multiply_fusion.1
  60.9 2.3 multiply_add_fusion.7
  63.3 2.2 multiply_add_fusion.6
  65.5 2.3 multiply_add_fusion.5
  67.8 2.3 multiply_add_fusion.4
  70.1 1.8 fusion.106
  74.2 5.3 %select_reduce_fusion = f32[8,1024]{1,0:T(8,128)S(1)} fusion(pred[256,1024]{1,0:T(8,128)(4,1)S(1)} %fusion.215, f32[8,256,128]{2,1,0:T(8,128)} %bitcast.64, s32[1024]{0:T(1024)S(1)} %get-tuple-element.87), kind=kOutput, calls=%fused_computation.66 | convolution fusion | flops 3225542656 | bytes 1347584 | tf_op jit(solution)/shard_map/dot_general | solution.py:285
  80.5 12.6 %shard_map.123 = f32[4,8,128]{2,1,0:T(8,128)} custom-call(f32[8,128]{1,0:T(8,128)} %pad_bitcast_fusion.1.x_ref), custom_call_target="tpu_custom_call" | custom-call | tf_op jit(solution)/shard_map/pallas_call | solution.py:50
  94.4 32.8 %shard_map.124 = f32[8,8,128]{2,1,0:T(8,128)} custom-call(f32[8,128]{1,0:T(8,128)} %reduce_sum.248.x_ref), custom_call_target="tpu_custom_call" | custom-call | tf_op jit(solution)/shard_map/pallas_call | solution.py:50
  128.8 2.3 fusion.x_ref
  131.1 9.2 %shard_map.125 = f32[4,20,48,128]{3,2,1,0:T(8,128)S(1)} custom-call(f32[4,8,32,128]{3,2,1,0:T(8,128)S(1)} %fusion.x_ref), custom_call_target="tpu_custom_call" | custom-call | tf_op jit(solution)/shard_map/pallas_call | solution.py:133
  141.6 2.3 multiply_add_fusion.3
  143.9 2.2 multiply_add_fusion.2
  146.2 2.2 multiply_add_fusion.1
  148.4 2.2 multiply_add_fusion
  150.6 3.0 %fusion.203 = f32[4,20,48,128]{3,2,1,0:T(8,128)S(1)} fusion(f32[4,20,48,128]{3,2,1,0:T(8,128)S(1)} %get-tuple-element.32, f32[4,20,48,128]{3,2,1,0:T(8,128)S(1)} %get-tuple-element.31, f32[4,20,48,128]{3,2,1,0:T(8,128)S(1)} %get-tuple-element.33, f32[4,20,48,128]{3,2,1,0:T(8,128)S(1)} %get-tuple-element.35, f32[4,20,48,128]{3,2,1,0:T(8,128)S(1)} %get-tuple-element.37, ...), kind=kLoop, calls=%fused_computation.283 | loop fusion | flops 14254080 | bytes 17203200 | tf_op jit(solution)/shard_map/add | solution.py:213
  157.0 17.8 %shard_map.126 = f32[8,64,128]{2,1,0:T(8,128)} custom-call(f32[8,64,128]{2,1,0:T(8,128)} %reshape.351.x_ref), custom_call_target="tpu_custom_call" | custom-call | tf_op jit(solution)/shard_map/pallas_call | solution.py:50
  181.7 10.3 %shard_map.127 = f32[4,8,128]{2,1,0:T(8,128)} custom-call(f32[8,128]{1,0:T(8,128)} %fusion.269.x_ref), custom_call_target="tpu_custom_call" | custom-call | tf_op jit(solution)/shard_map/pallas_call | solution.py:50
  193.3 17.3 %shard_map.128 = f32[8,8,128]{2,1,0:T(8,128)} custom-call(f32[8,128]{1,0:T(8,128)} %reduce_sum.262.x_ref), custom_call_target="tpu_custom_call" | custom-call | tf_op jit(solution)/shard_map/pallas_call | solution.py:50
  210.6 1.4 reduce_sum.263.x_ref
  212.0 11.0 %shard_map.129 = f32[8,8,128]{2,1,0:T(8,128)} custom-call(f32[8,128]{1,0:T(8,128)} %reduce_sum.263.x_ref), custom_call_target="tpu_custom_call" | custom-call | tf_op jit(solution)/shard_map/pallas_call | solution.py:50
  228.9 5.4 %shard_map.130 = f32[4,8,128]{2,1,0:T(8,128)} custom-call(f32[8,128]{1,0:T(8,128)} %pad_bitcast_fusion.x_ref), custom_call_target="tpu_custom_call" | custom-call | tf_op jit(solution)/shard_map/pallas_call | solution.py:50
  235.6 6.6 %shard_map.131 = f32[8,8,128]{2,1,0:T(8,128)} custom-call(f32[8,128]{1,0:T(8,128)} %reduce_sum.267.x_ref), custom_call_target="tpu_custom_call" | custom-call | tf_op jit(solution)/shard_map/pallas_call | solution.py:50
  242.1 1.4 reduce_sum.268.x_ref
  243.5 11.3 %shard_map.132 = f32[8,8,128]{2,1,0:T(8,128)} custom-call(f32[8,128]{1,0:T(8,128)} %reduce_sum.268.x_ref), custom_call_target="tpu_custom_call" | custom-call | tf_op jit(solution)/shard_map/pallas_call | solution.py:50
  (112 shorter events, 29.5 us)
Async XLA Ops:
  0.6 3.1 %copy-start.13 = (f32[8,32,16]{1,2,0:T(8,128)S(1)}, f32[8,32,16]{1,2,0:T(8,128)}, u32[]{:S(2)}) copy-start(f32[8,32,16]{1,2,0:T(8,128)} %param.15) | copy-start | bytes 49156
  0.6 3.1 %copy-start.14 = (f32[8,32,16]{1,2,0:T(8,128)S(1)}, f32[8,32,16]{1,2,0:T(8,128)}, u32[]{:S(2)}) copy-start(f32[8,32,16]{1,2,0:T(8,128)} %param.16) | copy-start | bytes 49156
  24.6 1.8 copy-start.11
  53.6 2.2 copy-start
  56.6 13.4 %copy-start.3 = (f32[20,48,128]{2,1,0:T(8,128)}, f32[20,48,128]{2,1,0:T(8,128)S(1)}, u32[]{:S(2)}) copy-start(f32[20,48,128]{2,1,0:T(8,128)S(1)} %get-tuple-element.66) | copy-start | bytes 1474564
  56.6 13.4 %copy-start.5 = (f32[20,48,128]{2,1,0:T(8,128)}, f32[20,48,128]{2,1,0:T(8,128)S(1)}, u32[]{:S(2)}) copy-start(f32[20,48,128]{2,1,0:T(8,128)S(1)} %get-tuple-element.67) | copy-start | bytes 1474564
  56.6 15.2 %copy-start.7 = (f32[20,48,128]{2,1,0:T(8,128)}, f32[20,48,128]{2,1,0:T(8,128)S(1)}, u32[]{:S(2)}) copy-start(f32[20,48,128]{2,1,0:T(8,128)S(1)} %get-tuple-element.68) | copy-start | bytes 1474564
  56.6 2.1 slice-start
  56.6 2.1 copy-start.12
  58.8 2.1 copy-start.1
  60.9 2.3 copy-start.9
  71.8 1.0 copy-start.10
  72.9 1.1 copy-start.18
  140.3 1.0 copy-start.4
  140.3 1.2 copy-start.6
  140.3 1.3 copy-start.8
  150.6 3.0 %copy-start.2 = (f32[8,20,48,128]{3,2,1,0:T(8,128)S(1)}, f32[8,20,48,128]{3,2,1,0:T(8,128)}, u32[]{:S(2)}) copy-start(f32[8,20,48,128]{3,2,1,0:T(8,128)} %copy-done) | copy-start | bytes 11796484
  155.8 20.9 %copy-start.16 = (f32[8,32,16]{1,2,0:T(8,128)S(1)}, f32[8,32,16]{1,2,0:T(8,128)}, u32[]{:S(2)}) copy-start(f32[8,32,16]{1,2,0:T(8,128)} %param.17) | copy-start | bytes 49156
  155.8 21.1 %copy-start.17 = (f32[8,32,16]{1,2,0:T(8,128)S(1)}, f32[8,32,16]{1,2,0:T(8,128)}, u32[]{:S(2)}) copy-start(f32[8,32,16]{1,2,0:T(8,128)} %param.18) | copy-start | bytes 49156
  155.8 21.2 %copy-start.15 = (f32[8,32,16]{1,2,0:T(8,128)S(1)}, f32[8,32,16]{1,2,0:T(8,128)}, u32[]{:S(2)}) copy-start(f32[8,32,16]{1,2,0:T(8,128)} %param.16) | copy-start | bytes 49156

commit v3 on v2

--- a/solution.py
+++ b/solution.py
@@ -147,12 +147,69 @@
     )(x)
 
 
-def small_sum(values, axes, first_id):
+def _reduce_kernel(axes, x_ref, o_ref, *scratch):
+    stages = len(axes)
+    slots, sends, recvs = scratch[:stages], scratch[stages : 2 * stages], scratch[2 * stages : 3 * stages]
+    held = scratch[3 * stages :]
+    barrier = pltpu.get_barrier_semaphore()
+    peers = 0
+    for axis in axes:
+        n = lax.axis_size(axis)
+        me = lax.axis_index(axis)
+        for k in range(1, n):
+            pl.semaphore_signal(
+                barrier, inc=1, device_id={axis: lax.rem(me + k, n)}, device_id_type=MESH
+            )
+        peers += n - 1
+    pl.semaphore_wait(barrier, peers)
+    value = x_ref
+    for i, axis in enumerate(axes):
+        n = lax.axis_size(axis)
+        me = lax.axis_index(axis)
+        copies = []
+        for k in range(1, n):
+            copy = pltpu.make_async_remote_copy(
+                src_ref=value,
+                dst_ref=slots[i].at[me],
+                send_sem=sends[i].at[k - 1],
+                recv_sem=recvs[i].at[k - 1],
+                device_id={axis: lax.rem(me + k, n)},
+                device_id_type=MESH,
+            )
+            copy.start()
+            copies.append(copy)
+        slots[i][me] = value[...]
+        for copy in copies:
+            copy.wait()
+        total = slots[i][0]
+        for j in range(1, n):
+            total = total + slots[i][j]
+        if i + 1 < stages:
+            held[i][...] = total
+            value = held[i]
+        else:
+            o_ref[...] = total
+
+
+def small_sum(values, axes, cid):
     count = values.shape[0]
     packed = jnp.pad(values, (0, 1024 - count)).reshape(8, 128)
-    for i, axis in enumerate(axes):
-        packed = jnp.sum(exchange(packed, axis, first_id + i), axis=0)
-    return packed.reshape(-1)[:count]
+    sizes = [lax.axis_size(axis) for axis in axes]
+    scratch = (
+        [pltpu.VMEM((n, 8, 128), jnp.float32) for n in sizes]
+        + [pltpu.SemaphoreType.DMA((n - 1,)) for n in sizes]
+        + [pltpu.SemaphoreType.DMA((n - 1,)) for n in sizes]
+        + [pltpu.VMEM((8, 128), jnp.float32) for n in sizes[:-1]]
+    )
+    total = pl.pallas_call(
+        functools.partial(_reduce_kernel, tuple(axes)),
+        out_shape=jax.ShapeDtypeStruct((8, 128), jnp.float32),
+        in_specs=[pl.BlockSpec(memory_space=pltpu.VMEM)],
+        out_specs=pl.BlockSpec(memory_space=pltpu.VMEM),
+        scratch_shapes=scratch,
+        compiler_params=pltpu.CompilerParams(collective_id=cid, has_side_effects=True),
+    )(packed)
+    return total.reshape(-1)[:count]
 
 
 def padded_2(block, sides, width):

time: 260 us -> 238 us (0.915)
  Pallas kernels: 178 us -> 163 us
  other arithmetic: 42.8 us -> 33.8 us
    pallas_call x10 -> x2, Pallas kernels: 142 us -> 33.9 us  [exchange(): pl.pallas_call(functools.partial(_exchange_kernel, axis, n, scatter), out...]
    pallas_call x0 -> x3, Pallas kernels: none -> 92.8 us  [small_sum(): pl.pallas_call(functools.partial(_reduce_kernel, tuple(axes)), out_shape=...]
    reduce_sum x8 -> x0, other arithmetic: 8.98 us -> none  [small_sum(): packed = jnp.sum(exchange(packed, axis, first_id + i), axis=0)]
where the time goes in v3:
time: 238 us; the launch traced here: 237 us
  Pallas kernels  163 us (68%)
  other arithmetic  33.8 us (14%)
  local copies, waits for them, and re-layouts  23.4 us (10%)
  matrix products  9.61 us (4%)
  between operations  7.9 us (3%)
    pallas_call x3, Pallas kernels, small_sum(): pl.pallas_call(functools.partial(_reduce_kernel, tuple(axes)), out_shape=...  92.8 us
    pallas_call x2, Pallas kernels, halo_block(): pl.pallas_call(functools.partial(_halo_kernel, hx, hy), out_shape=jax.Sha...  36 us
    pallas_call x2, Pallas kernels, exchange(): pl.pallas_call(functools.partial(_exchange_kernel, axis, n, scatter), out...  33.9 us
    add x8, other arithmetic, chebyshev(): step_dir = rho_next * rho * step_dir + 2.0 * rho_next / delta * remain  18 us
    unnamed x48, local copies, waits for them, and re-layouts  5.8 us
    dot_general x1, matrix products, per_device(): jnp.dot(both, depth_hot, precision=lax.Precision.HIGHEST)  5.57 us

profile of v3, /device:TPU:1, one launch (start us, length us, event | category | flops | bytes accessed | tf_op | source)
XLA Modules:
  0.0 237.3 jit_solution(6217155991321459026)
XLA Ops:
  0.7 1.7 fusion.5
  2.6 1.1 constant_dynamic-update-slice_fusion.4
  4.6 16.7 %shard_map.121 = f32[8,64,128]{2,1,0:T(8,128)} custom-call(f32[64,128]{1,0:T(8,128)} %reshape.347.x_ref), custom_call_target="tpu_custom_call" | custom-call | tf_op jit(solution)/shard_map/pallas_call | solution.py:50
  21.3 1.7 reshape.348
  23.0 1.6 fusion.286
  24.6 1.6 copy.51
  27.0 26.6 %shard_map.122 = f32[8,20,48,128]{3,2,1,0:T(8,128)S(1)} custom-call(f32[8,8,32,128]{3,2,1,0:T(8,128)S(1)} %constant_dynamic-update-slice_fusion.x_ref), custom_call_target="tpu_custom_call" | custom-call | tf_op jit(solution)/shard_map/pallas_call | solution.py:133
  53.6 1.3 slice_bitcast_fusion.1
  56.6 2.0 slice-done
  58.8 2.1 broadcast_multiply_fusion.1
  60.9 2.3 multiply_add_fusion.7
  63.3 2.2 multiply_add_fusion.6
  65.5 2.3 multiply_add_fusion.5
  67.8 2.3 multiply_add_fusion.4
  70.1 1.8 fusion.106
  72.9 1.1 pad_maximum_fusion
  74.2 5.6 %select_reduce_fusion = f32[8,1024]{1,0:T(8,128)S(1)} fusion(pred[256,1024]{1,0:T(8,128)(4,1)S(1)} %fusion.215, f32[8,256,128]{2,1,0:T(8,128)} %bitcast.64, s32[1024]{0:T(1024)S(1)} %get-tuple-element.87), kind=kOutput, calls=%fused_computation.66 | convolution fusion | flops 3225542656 | bytes 1347584 | tf_op jit(solution)/shard_map/dot_general | solution.py:342
  80.8 43.0 %shard_map.123 = f32[8,128]{1,0:T(8,128)} custom-call(f32[8,128]{1,0:T(8,128)} %pad_bitcast_fusion.1.x_ref), custom_call_target="tpu_custom_call" | custom-call | tf_op jit(solution)/shard_map/pallas_call | solution.py:204
  125.2 2.3 fusion.x_ref
  127.5 9.5 %shard_map.124 = f32[4,20,48,128]{3,2,1,0:T(8,128)S(1)} custom-call(f32[4,8,32,128]{3,2,1,0:T(8,128)S(1)} %fusion.x_ref), custom_call_target="tpu_custom_call" | custom-call | tf_op jit(solution)/shard_map/pallas_call | solution.py:133
  138.3 2.3 multiply_add_fusion.3
  140.6 2.2 multiply_add_fusion.2
  142.8 2.2 multiply_add_fusion.1
  145.0 2.2 multiply_add_fusion
  147.3 3.0 %fusion.203 = f32[4,20,48,128]{3,2,1,0:T(8,128)S(1)} fusion(f32[4,20,48,128]{3,2,1,0:T(8,128)S(1)} %get-tuple-element.32, f32[4,20,48,128]{3,2,1,0:T(8,128)S(1)} %get-tuple-element.31, f32[4,20,48,128]{3,2,1,0:T(8,128)S(1)} %get-tuple-element.33, f32[4,20,48,128]{3,2,1,0:T(8,128)S(1)} %get-tuple-element.35, f32[4,20,48,128]{3,2,1,0:T(8,128)S(1)} %get-tuple-element.37, ...), kind=kLoop, calls=%fused_computation.283 | loop fusion | flops 14254080 | bytes 17203200 | tf_op jit(solution)/shard_map/add | solution.py:270
  152.5 1.3 reshape.351.x_ref
  153.7 17.2 %shard_map.125 = f32[8,64,128]{2,1,0:T(8,128)} custom-call(f32[8,64,128]{2,1,0:T(8,128)} %reshape.351.x_ref), custom_call_target="tpu_custom_call" | custom-call | tf_op jit(solution)/shard_map/pallas_call | solution.py:50
  170.9 1.0 reduce_sum.183
  177.8 33.7 %shard_map.126 = f32[8,128]{1,0:T(8,128)} custom-call(f32[8,128]{1,0:T(8,128)} %fusion.269.x_ref), custom_call_target="tpu_custom_call" | custom-call | tf_op jit(solution)/shard_map/pallas_call | solution.py:204
  211.5 1.3 fusion.289
  217.3 16.0 %shard_map.127 = f32[8,128]{1,0:T(8,128)} custom-call(f32[8,128]{1,0:T(8,128)} %pad_bitcast_fusion.x_ref), custom_call_target="tpu_custom_call" | custom-call | tf_op jit(solution)/shard_map/pallas_call | solution.py:204
  233.4 1.2 slice.480
  (99 shorter events, 17.2 us)
Async XLA Ops:
  0.6 3.1 %copy-start.13 = (f32[8,32,16]{1,2,0:T(8,128)S(1)}, f32[8,32,16]{1,2,0:T(8,128)}, u32[]{:S(2)}) copy-start(f32[8,32,16]{1,2,0:T(8,128)} %param.15) | copy-start | bytes 49156
  0.6 3.1 %copy-start.14 = (f32[8,32,16]{1,2,0:T(8,128)S(1)}, f32[8,32,16]{1,2,0:T(8,128)}, u32[]{:S(2)}) copy-start(f32[8,32,16]{1,2,0:T(8,128)} %param.16) | copy-start | bytes 49156
  24.6 1.8 copy-start.11
  53.6 2.2 copy-start
  56.6 13.4 %copy-start.3 = (f32[20,48,128]{2,1,0:T(8,128)}, f32[20,48,128]{2,1,0:T(8,128)S(1)}, u32[]{:S(2)}) copy-start(f32[20,48,128]{2,1,0:T(8,128)S(1)} %get-tuple-element.66) | copy-start | bytes 1474564
  56.6 13.4 %copy-start.5 = (f32[20,48,128]{2,1,0:T(8,128)}, f32[20,48,128]{2,1,0:T(8,128)S(1)}, u32[]{:S(2)}) copy-start(f32[20,48,128]{2,1,0:T(8,128)S(1)} %get-tuple-element.67) | copy-start | bytes 1474564
  56.6 15.2 %copy-start.7 = (f32[20,48,128]{2,1,0:T(8,128)}, f32[20,48,128]{2,1,0:T(8,128)S(1)}, u32[]{:S(2)}) copy-start(f32[20,48,128]{2,1,0:T(8,128)S(1)} %get-tuple-element.68) | copy-start | bytes 1474564
  56.6 2.1 slice-start
  56.6 2.1 copy-start.12
  58.8 2.1 copy-start.1
  60.9 2.3 copy-start.9
  71.8 1.0 copy-start.10
  72.9 1.1 copy-start.18
  137.0 1.0 copy-start.4
  137.0 1.2 copy-start.6
  137.0 1.3 copy-start.8
  147.3 3.0 %copy-start.2 = (f32[8,20,48,128]{3,2,1,0:T(8,128)S(1)}, f32[8,20,48,128]{3,2,1,0:T(8,128)}, u32[]{:S(2)}) copy-start(f32[8,20,48,128]{3,2,1,0:T(8,128)} %copy-done) | copy-start | bytes 11796484
  152.4 20.4 %copy-start.16 = (f32[8,32,16]{1,2,0:T(8,128)S(1)}, f32[8,32,16]{1,2,0:T(8,128)}, u32[]{:S(2)}) copy-start(f32[8,32,16]{1,2,0:T(8,128)} %param.17) | copy-start | bytes 49156
  152.4 20.6 %copy-start.17 = (f32[8,32,16]{1,2,0:T(8,128)S(1)}, f32[8,32,16]{1,2,0:T(8,128)}, u32[]{:S(2)}) copy-start(f32[8,32,16]{1,2,0:T(8,128)} %param.18) | copy-start | bytes 49156
  152.4 20.6 %copy-start.15 = (f32[8,32,16]{1,2,0:T(8,128)S(1)}, f32[8,32,16]{1,2,0:T(8,128)}, u32[]{:S(2)}) copy-start(f32[8,32,16]{1,2,0:T(8,128)} %param.16) | copy-start | bytes 49156

commit v4 on v3

--- a/solution.py
+++ b/solution.py
@@ -289,11 +289,6 @@
     beta_prev,
 ):
     sources, cx, cy, cz = background.shape
-    regions = kappa_table.shape[0]
-    label_hot = (labels.reshape(1, -1) == jnp.arange(regions)[:, None]).astype(jnp.float32)
-    tables = jnp.stack([kappa_table, absorb_table])
-    fields = jnp.dot(tables, label_hot, precision=lax.Precision.HIGHEST).reshape(2, cx, cy, cz)
-    kappa, absorb = fields[0], fields[1]
     n_src = lax.axis_size("src")
     slab = v_kappa.shape[2]
     pair = jnp.stack([v_kappa, v_absorb]).reshape(-1, 128)
@@ -301,11 +296,10 @@
     full_k, full_a = jnp.transpose(gathered, (1, 2, 3, 0, 4)).reshape(2, cx, cy, cz)
     width = ITERS
     width_y = 8
-    stacked = jnp.concatenate([background, kappa[None], absorb[None], full_k[None], full_a[None]], axis=0)
+    region_of = labels.astype(jnp.float32)[None]
+    stacked = jnp.concatenate([background, region_of, full_k[None], full_a[None]], axis=0)
     wide = halo_block(stacked, width, width_y, 10)
-    phi_w, kappa_w, absorb_w, vk_w, va_w = (
-        wide[:sources], wide[sources], wide[sources + 1], wide[sources + 2], wide[sources + 3]
-    )
+    phi_w, region_w, vk_w, va_w = wide[:sources], wide[sources], wide[sources + 1], wide[sources + 2]
     wx = cx + 2 * width
     wy = cy + 2 * width_y
     gx_at = lax.axis_index("gx") * cx - width + jnp.arange(wx)
@@ -314,6 +308,11 @@
         (gy_at >= 0) & (gy_at < cy * lax.axis_size("gy"))
     )[None, :, None]
     mask = inside.astype(jnp.float32)
+    regions = kappa_table.shape[0]
+    label_hot = (region_w.reshape(1, -1) == jnp.arange(regions, dtype=jnp.float32)[:, None]).astype(jnp.float32)
+    tables = jnp.stack([kappa_table, absorb_table])
+    fields = jnp.dot(tables, label_hot, precision=lax.Precision.HIGHEST).reshape(2, wx, wy, cz)
+    kappa_w, absorb_w = mask * fields[0], mask * fields[1]
     kappa_faces = [mask * (0.5 * (kappa_w + near)) for near in around(kappa_w)]
     vk_faces = [mask * (0.5 * (vk_w + near)) for near in around(vk_w)]
 
@@ -366,7 +365,7 @@
     dual_near = beside(dual_w[ring])
     dual = dual_w[:, width : width + cx, width_y : width_y + cy, :]
     grad_a = -jnp.sum(background * dual, axis=0)
-    grad_k = jnp.zeros_like(kappa)
+    grad_k = jnp.zeros_like(background[0])
     for near_phi, near_dual in zip(phi_near, dual_near):
         grad_k = grad_k - 0.5 * jnp.sum((background - near_phi) * (dual - near_dual), axis=0)
     grads = jnp.stack([grad_k, grad_a]).reshape(2, cx, cy, n_src, slab)

time: 238 us -> 234 us (0.983)
  Pallas kernels: 163 us -> 155 us
  other arithmetic: 33.8 us -> 36.9 us
    pallas_call x3, Pallas kernels: 92.8 us -> 89.1 us  [small_sum(): pl.pallas_call(functools.partial(_reduce_kernel, tuple(axes)), out_shape=...]
    pallas_call x2, Pallas kernels: 36 us -> 32.5 us  [halo_block(): pl.pallas_call(functools.partial(_halo_kernel, hx, hy), out_shape=jax.Sha...]
    unnamed x48 -> x60, local copies, waits for them, and re-layouts: 5.8 us -> 6.06 us
where the time goes in v4:
time: 234 us; the launch traced here: 233 us
  Pallas kernels  155 us (66%)
  other arithmetic  36.9 us (16%)
  local copies, waits for them, and re-layouts  22.1 us (9%)
  matrix products  10.2 us (4%)
  between operations  7.98 us (3%)
    pallas_call x3, Pallas kernels, small_sum(): pl.pallas_call(functools.partial(_reduce_kernel, tuple(axes)), out_shape=...  89.1 us
    pallas_call x2, Pallas kernels, exchange(): pl.pallas_call(functools.partial(_exchange_kernel, axis, n, scatter), out...  33.9 us
    pallas_call x2, Pallas kernels, halo_block(): pl.pallas_call(functools.partial(_halo_kernel, hx, hy), out_shape=jax.Sha...  32.5 us
    add x8, other arithmetic, chebyshev(): step_dir = rho_next * rho * step_dir + 2.0 * rho_next / delta * remain  18.4 us
    unnamed x60, local copies, waits for them, and re-layouts  6.06 us
    dot_general x1, matrix products, per_device(): jnp.dot(both, depth_hot, precision=lax.Precision.HIGHEST)  5.58 us

profile of v4, /device:TPU:1, one launch (start us, length us, event | category | flops | bytes accessed | tf_op | source)
XLA Modules:
  0.0 232.7 jit_solution(10578666404767521211)
XLA Ops:
  2.5 16.7 %shard_map.121 = f32[8,64,128]{2,1,0:T(8,128)} custom-call(f32[64,128]{1,0:T(8,128)} %reshape.353.x_ref), custom_call_target="tpu_custom_call" | custom-call | tf_op jit(solution)/shard_map/pallas_call | solution.py:50
  19.2 1.7 reshape.354
  20.9 1.2 fusion.287
  22.1 1.6 copy.51
  24.8 23.0 %shard_map.122 = f32[7,20,48,128]{3,2,1,0:T(8,128)S(1)} custom-call(f32[7,8,32,128]{3,2,1,0:T(8,128)S(1)} %pad_maximum_fusion.1.x_ref), custom_call_target="tpu_custom_call" | custom-call | tf_op jit(solution)/shard_map/pallas_call | solution.py:133
  48.5 2.3 fusion
  52.9 2.2 broadcast_multiply_fusion.1
  55.0 2.3 %multiply_add_fusion.7 = (f32[4,20,48,128]{3,2,1,0:T(8,128)S(1)}, f32[4,20,48,128]{3,2,1,0:T(8,128)S(1)}) fusion(f32[4,20,48,128]{3,2,1,0:T(8,128)S(1)} %get-tuple-element.50, f32[4,20,48,128]{3,2,1,0:T(8,128)S(1)} %get-tuple-element.49, f32[20,48,128]{2,1,0:T(8,128)S(1)} %get-tuple-element.71, f32[20,48,128]{2,1,0:T(8,128)S(1)} %get-tuple-element.67, ...), kind=kLoop, calls=%fused_computation.302 | loop fusion | flops 11304960 | bytes 11304960 | tf_op jit(solution)/shard_map/add | solution.py:274
  57.4 2.3 multiply_add_fusion.6
  59.7 2.3 multiply_add_fusion.5
  61.9 2.3 multiply_add_fusion.4
  64.3 1.8 fusion.107
  67.2 1.1 pad_maximum_fusion
  68.5 5.6 %select_reduce_fusion = f32[8,1024]{1,0:T(8,128)S(1)} fusion(pred[256,1024]{1,0:T(8,128)(4,1)S(1)} %fusion.215, f32[8,256,128]{2,1,0:T(8,128)} %bitcast.62, s32[1024]{0:T(1024)S(1)} %get-tuple-element.89), kind=kOutput, calls=%fused_computation.66 | convolution fusion | flops 3225542656 | bytes 1347584 | tf_op jit(solution)/shard_map/dot_general | solution.py:341
  75.0 39.3 %shard_map.123 = f32[8,128]{1,0:T(8,128)} custom-call(f32[8,128]{1,0:T(8,128)} %pad_bitcast_fusion.1.x_ref), custom_call_target="tpu_custom_call" | custom-call | tf_op jit(solution)/shard_map/pallas_call | solution.py:204
  114.4 1.4 slice.419
  115.8 1.0 slice_reduce_fusion.3
  117.2 2.3 %fusion.1.x_ref = f32[4,8,32,128]{3,2,1,0:T(8,128)S(1)} fusion(f32[4,1024]{1,0:T(4,128)S(1)} %subtract_divide_fusion, pred[8,32,1024]{2,1,0:T(8,128)(4,1)S(1)} %compare_and_fusion, s32[1024]{0:T(1024)S(1)} %get-tuple-element.89), kind=kOutput, calls=%fused_computation.69 | convolution fusion | flops 1611792384 | bytes 806912 | tf_op jit(solution)/shard_map/dot_general | solution.py:361
  119.5 9.5 %shard_map.124 = f32[4,20,48,128]{3,2,1,0:T(8,128)S(1)} custom-call(f32[4,8,32,128]{3,2,1,0:T(8,128)S(1)} %fusion.1.x_ref), custom_call_target="tpu_custom_call" | custom-call | tf_op jit(solution)/shard_map/pallas_call | solution.py:133
  130.9 2.3 multiply_add_fusion.3
  133.3 2.3 %multiply_add_fusion.2 = (f32[4,20,48,128]{3,2,1,0:T(8,128)S(1)}, f32[4,20,48,128]{3,2,1,0:T(8,128)S(1)}) fusion(f32[4,20,48,128]{3,2,1,0:T(8,128)S(1)} %get-tuple-element.37, f32[4,20,48,128]{3,2,1,0:T(8,128)S(1)} %get-tuple-element.38, f32[20,48,128]{2,1,0:T(8,128)S(1)} %copy-done.11, f32[20,48,128]{2,1,0:T(8,128)S(1)} %copy-done.3, ...), kind=kLoop, calls=%fused_computation.297 | loop fusion | flops 11304960 | bytes 11304960 | tf_op jit(solution)/shard_map/add | solution.py:274
  135.6 2.3 %multiply_add_fusion.1 = (f32[4,20,48,128]{3,2,1,0:T(8,128)S(1)}, f32[4,20,48,128]{3,2,1,0:T(8,128)S(1)}) fusion(f32[4,20,48,128]{3,2,1,0:T(8,128)S(1)} %get-tuple-element.35, f32[4,20,48,128]{3,2,1,0:T(8,128)S(1)} %get-tuple-element.36, f32[20,48,128]{2,1,0:T(8,128)S(1)} %copy-done.11, f32[20,48,128]{2,1,0:T(8,128)S(1)} %copy-done.3, ...), kind=kLoop, calls=%fused_computation.296 | loop fusion | flops 11304960 | bytes 11304960 | tf_op jit(solution)/shard_map/add | solution.py:274
  138.0 2.2 multiply_add_fusion
  140.2 2.9 %fusion.204 = f32[4,20,48,128]{3,2,1,0:T(8,128)S(1)} fusion(f32[4,20,48,128]{3,2,1,0:T(8,128)S(1)} %get-tuple-element.32, f32[4,20,48,128]{3,2,1,0:T(8,128)S(1)} %get-tuple-element.31, f32[4,20,48,128]{3,2,1,0:T(8,128)S(1)} %get-tuple-element.33, f32[4,20,48,128]{3,2,1,0:T(8,128)S(1)} %get-tuple-element.35, f32[4,20,48,128]{3,2,1,0:T(8,128)S(1)} %get-tuple-element.37, ...), kind=kLoop, calls=%fused_computation.284 | loop fusion | flops 14254080 | bytes 17203200 | tf_op jit(solution)/shard_map/add | solution.py:270
  144.2 1.3 fusion.218
  147.7 1.3 reshape.357.x_ref
  149.0 17.2 %shard_map.125 = f32[8,64,128]{2,1,0:T(8,128)} custom-call(f32[8,64,128]{2,1,0:T(8,128)} %reshape.357.x_ref), custom_call_target="tpu_custom_call" | custom-call | tf_op jit(solution)/shard_map/pallas_call | solution.py:50
  166.2 1.0 reduce_sum.183
  173.0 33.7 %shard_map.126 = f32[8,128]{1,0:T(8,128)} custom-call(f32[8,128]{1,0:T(8,128)} %fusion.269.x_ref), custom_call_target="tpu_custom_call" | custom-call | tf_op jit(solution)/shard_map/pallas_call | solution.py:204
  206.7 1.3 fusion.290
  212.6 16.1 %shard_map.127 = f32[8,128]{1,0:T(8,128)} custom-call(f32[8,128]{1,0:T(8,128)} %pad_bitcast_fusion.x_ref), custom_call_target="tpu_custom_call" | custom-call | tf_op jit(solution)/shard_map/pallas_call | solution.py:204
  228.7 1.2 slice.470
  (112 shorter events, 19.6 us)
Async XLA Ops:
  22.1 2.3 copy-start.21
  23.7 1.1 copy-start.14
  47.8 0.7 copy-start.25
  47.8 0.7 copy-start.26
  51.8 3.3 %copy-start.17 = (f32[20,48,128]{2,1,0:T(8,128)}, f32[20,48,128]{2,1,0:T(8,128)S(1)}, u32[]{:S(2)}) copy-start(f32[20,48,128]{2,1,0:T(8,128)S(1)} %get-tuple-element.47) | copy-start | bytes 1474564
  51.8 12.5 %copy-start.12 = (f32[20,48,128]{2,1,0:T(8,128)}, f32[20,48,128]{2,1,0:T(8,128)S(1)}, u32[]{:S(2)}) copy-start(f32[20,48,128]{2,1,0:T(8,128)S(1)} %get-tuple-element.48) | copy-start | bytes 1474564
  52.6 11.6 %copy-start = (f32[20,48,128]{2,1,0:T(8,128)}, f32[20,48,128]{2,1,0:T(8,128)S(1)}, u32[]{:S(2)}) copy-start(f32[20,48,128]{2,1,0:T(8,128)S(1)} %get-tuple-element.66) | copy-start | bytes 1474564
  52.7 11.6 %copy-start.2 = (f32[20,48,128]{2,1,0:T(8,128)}, f32[20,48,128]{2,1,0:T(8,128)S(1)}, u32[]{:S(2)}) copy-start(f32[20,48,128]{2,1,0:T(8,128)S(1)} %get-tuple-element.67) | copy-start | bytes 1474564
  52.7 11.6 %copy-start.4 = (f32[20,48,128]{2,1,0:T(8,128)}, f32[20,48,128]{2,1,0:T(8,128)S(1)}, u32[]{:S(2)}) copy-start(f32[20,48,128]{2,1,0:T(8,128)S(1)} %get-tuple-element.68) | copy-start | bytes 1474564
  52.7 11.6 %copy-start.6 = (f32[20,48,128]{2,1,0:T(8,128)}, f32[20,48,128]{2,1,0:T(8,128)S(1)}, u32[]{:S(2)}) copy-start(f32[20,48,128]{2,1,0:T(8,128)S(1)} %get-tuple-element.69) | copy-start | bytes 1474564
  52.7 11.6 %copy-start.8 = (f32[20,48,128]{2,1,0:T(8,128)}, f32[20,48,128]{2,1,0:T(8,128)S(1)}, u32[]{:S(2)}) copy-start(f32[20,48,128]{2,1,0:T(8,128)S(1)} %get-tuple-element.70) | copy-start | bytes 1474564
  52.7 13.4 %copy-start.10 = (f32[20,48,128]{2,1,0:T(8,128)}, f32[20,48,128]{2,1,0:T(8,128)S(1)}, u32[]{:S(2)}) copy-start(f32[20,48,128]{2,1,0:T(8,128)S(1)} %get-tuple-element.71) | copy-start | bytes 1474564
  66.1 1.0 copy-start.15
  67.2 1.1 copy-start.24
  129.0 1.0 copy-start.1
  129.0 1.2 copy-start.3
  129.0 1.3 copy-start.5
  129.0 1.5 copy-start.7
  129.1 1.6 copy-start.9
  129.1 1.7 copy-start.11
  129.1 1.9 copy-start.18
  130.9 2.3 %copy-start.13 = (f32[20,48,128]{2,1,0:T(8,128)S(1)}, f32[20,48,128]{2,1,0:T(8,128)}, u32[]{:S(2)}) copy-start(f32[20,48,128]{2,1,0:T(8,128)} %copy-done.12) | copy-start | bytes 1474564
  143.1 1.0 copy-start.16
  147.7 20.4 %copy-start.22 = (f32[8,32,16]{1,2,0:T(8,128)S(1)}, f32[8,32,16]{1,2,0:T(8,128)}, u32[]{:S(2)}) copy-start(f32[8,32,16]{1,2,0:T(8,128)} %param.17) | copy-start | bytes 49156
  147.7 20.5 %copy-start.19 = (f32[8,32,16]{1,2,0:T(8,128)S(1)}, f32[8,32,16]{1,2,0:T(8,128)}, u32[]{:S(2)}) copy-start(f32[8,32,16]{1,2,0:T(8,128)} %param.15) | copy-start | bytes 49156
  147.7 20.6 %copy-start.23 = (f32[8,32,16]{1,2,0:T(8,128)S(1)}, f32[8,32,16]{1,2,0:T(8,128)}, u32[]{:S(2)}) copy-start(f32[8,32,16]{1,2,0:T(8,128)} %param.18) | copy-start | bytes 49156
  147.7 20.7 %copy-start.20 = (f32[8,32,16]{1,2,0:T(8,128)S(1)}, f32[8,32,16]{1,2,0:T(8,128)}, u32[]{:S(2)}) copy-start(f32[8,32,16]{1,2,0:T(8,128)} %param.16) | copy-start | bytes 49156

commit v5 on v4

--- a/solution.py
+++ b/solution.py
@@ -258,6 +258,31 @@
     ]
 
 
+def trim(field):
+    return field[:, 1:-1]
+
+
+def chebyshev_trimmed(rhs, apply_at, lo):
+    theta = 0.5 * (lam_high + lam_low)
+    delta = 0.5 * (lam_high - lam_low)
+    sigma = theta / delta
+    rho = 1.0 / sigma
+    solution = jnp.zeros_like(rhs)
+    remain = rhs
+    step_dir = rhs / theta
+    for step in range(ITERS):
+        solution = solution + step_dir
+        if step + 1 < ITERS:
+            applied = apply_at(step_dir, lo)
+            lo += 1
+            remain = trim(remain) - trim(applied)
+            rho_next = 1.0 / (2.0 * sigma - rho)
+            step_dir = rho_next * rho * trim(step_dir) + 2.0 * rho_next / delta * remain
+            rho = rho_next
+            solution = trim(solution)
+    return solution
+
+
 def chebyshev(rhs, apply_op):
     theta = 0.5 * (lam_high + lam_low)
     delta = 0.5 * (lam_high - lam_low)
@@ -316,17 +341,18 @@
     kappa_faces = [mask * (0.5 * (kappa_w + near)) for near in around(kappa_w)]
     vk_faces = [mask * (0.5 * (vk_w + near)) for near in around(vk_w)]
 
-    def apply_op(field):
-        result = absorb_w * field
+    def apply_at(field, lo):
+        hi = wx - lo
+        result = absorb_w[lo:hi] * field
         for face, near in zip(kappa_faces, around(field)):
-            result = result + face * (field - near)
+            result = result + face[lo:hi] * (field - near)
         return result
 
     rhs = va_w * phi_w
     for face, near in zip(vk_faces, around(phi_w)):
         rhs = rhs + face * (phi_w - near)
     rhs = -rhs
-    change = chebyshev(rhs, apply_op)[:, width : width + cx, width_y : width_y + cy, :]
+    change = chebyshev_trimmed(trim(rhs), apply_at, 1)[:, :, width_y : width_y + cy, :]
     span_y = cy * lax.axis_size("gy")
     ix = det_cells // (span_y * cz)
     iy = det_cells // cz % span_y
@@ -359,11 +385,11 @@
     weight = (jv_vals - ratio_jv) / mean_base
     spread = jnp.where(plane_hot[None], weight[:, None, :], 0.0).reshape(sources * cx * cy, -1)
     source = jnp.dot(spread, depth_hot.T, precision=lax.Precision.HIGHEST).reshape(change.shape)
-    dual_w = chebyshev(halo_block(source, width, width_y, 11), apply_op)
+    dual_w = chebyshev_trimmed(halo_block(source, width, width_y, 11), apply_at, 0)
     ring = (slice(None), slice(width - 1, width + cx + 1), slice(width_y - 1, width_y + cy + 1))
     phi_near = beside(phi_w[ring])
-    dual_near = beside(dual_w[ring])
-    dual = dual_w[:, width : width + cx, width_y : width_y + cy, :]
+    dual_near = beside(dual_w[:, :, width_y - 1 : width_y + cy + 1])
+    dual = dual_w[:, 1 : 1 + cx, width_y : width_y + cy, :]
     grad_a = -jnp.sum(background * dual, axis=0)
     grad_k = jnp.zeros_like(background[0])
     for near_phi, near_dual in zip(phi_near, dual_near):

time: 234 us -> 309 us (1.32)
  other arithmetic: 36.9 us -> 92.3 us
  local copies, waits for them, and re-layouts: 22.1 us -> 38.5 us
    mul x1 -> x22, other arithmetic: 0.2 us -> 76.8 us  [the longest x12 41.4 us: apply_at(): result = absorb_w[lo:hi] * field]
    add x11 -> x2, other arithmetic: 23.4 us -> 1.71 us  [chebyshev_trimmed(): solution = solution + step_dir]
    unnamed x60 -> x170, local copies, waits for them, and re-layouts: 6.06 us -> 18 us
    slice x3 -> x48, local copies, waits for them, and re-layouts: 0.18 us -> 4.52 us  [the longest x32 3.33 us: trim(): return field[:, 1:-1]]
where the time goes in v5:
time: 309 us; the launch traced here: 306 us
  Pallas kernels  156 us (50%)
  other arithmetic  92.3 us (30%)
  local copies, waits for them, and re-layouts  38.5 us (12%)
  matrix products  10.1 us (3%)
  between operations  9.01 us (3%)
    pallas_call x3, Pallas kernels, small_sum(): pl.pallas_call(functools.partial(_reduce_kernel, tuple(axes)), out_shape=...  89.2 us
    mul x12, other arithmetic, apply_at(): result = absorb_w[lo:hi] * field  41.4 us
    mul x10, other arithmetic, apply_at(): result = result + face[lo:hi] * (field - near)  35.4 us
    pallas_call x2, Pallas kernels, exchange(): pl.pallas_call(functools.partial(_exchange_kernel, axis, n, scatter), out...  33.9 us
    pallas_call x2, Pallas kernels, halo_block(): pl.pallas_call(functools.partial(_halo_kernel, hx, hy), out_shape=jax.Sha...  32.5 us
    unnamed x170, local copies, waits for them, and re-layouts  18 us

profile of v5, /device:TPU:1, one launch (start us, length us, event | category | flops | bytes accessed | tf_op | source)
XLA Modules:
  0.0 305.6 jit_solution(897401541550936717)
XLA Ops:
  2.5 16.7 %shard_map.121 = f32[8,64,128]{2,1,0:T(8,128)} custom-call(f32[64,128]{1,0:T(8,128)} %reshape.388.x_ref), custom_call_target="tpu_custom_call" | custom-call | tf_op jit(solution)/shard_map/pallas_call | solution.py:50
  19.2 1.7 reshape.389
  22.1 1.5 copy.51
  24.8 23.0 %shard_map.122 = f32[7,20,48,128]{3,2,1,0:T(8,128)S(1)} custom-call(f32[7,8,32,128]{3,2,1,0:T(8,128)S(1)} %pad_maximum_fusion.1.x_ref), custom_call_target="tpu_custom_call" | custom-call | tf_op jit(solution)/shard_map/pallas_call | solution.py:133
  48.5 2.3 fusion
  52.7 1.8 fusion.195
  54.6 2.0 fusion.15
  57.6 1.5 slice_multiply_fusion.1
  59.9 5.8 %fusion.30 = (f32[4,18,48,128]{3,2,1,0:T(8,128)}, f32[4,18,48,128]{3,2,1,0:T(8,128)}, f32[4,18,48,128]{3,2,1,0:T(8,128)}, f32[4,18,48,128]{3,2,1,0:T(8,128)}, f3...) fusion(f32[4,18,48,128]{3,2,1,0:T(8,128)S(1)} %get-tuple-element.71, f32[18,48,128]{2,1,0:T(8,128)} %slice.804), kind=kLoop, calls=%fused_computation.114 | loop fusion | flops 1327104 | bytes 12828672 | tf_op jit(solution)/shard_map/mul | solution.py:348
  70.2 5.7 %broadcast_multiply_fusion.4 = (f32[4,16,48,128]{3,2,1,0:T(8,128)}, f32[4,16,48,128]{3,2,1,0:T(8,128)S(1)}, f32[4,16,48,128]{3,2,1,0:T(8,128)}) fusion(f32[16,48,128]{2,1,0:T(8,128)S(1)} %slice.827, f32[4,18,48,128]{3,2,1,0:T(8,128)S(1)} %get-tuple-element.71, f32[4,18,48,128]{3,2,1,0:T(8,128)} %get-tuple-element.81, f32[16,48,128]{2,1,0:T(8,128)S(1)} %slice.822, ...), kind=kLoop, calls=%fused_computation.323 | loop fusion | flops 7864320 | bytes 21233664 | tf_op jit(solution)/shard_map/mul | solution.py:346
  76.0 4.6 %fusion.46 = (f32[4,16,48,128]{3,2,1,0:T(8,128)}, f32[4,16,48,128]{3,2,1,0:T(8,128)}, f32[4,16,48,128]{3,2,1,0:T(8,128)}, f32[4,16,48,128]{3,2,1,0:T(8,128)}, f3...) fusion(f32[4,16,48,128]{3,2,1,0:T(8,128)S(1)} %get-tuple-element.55, f32[16,48,128]{2,1,0:T(8,128)S(1)} %slice.828), kind=kLoop, calls=%fused_computation.139 | loop fusion | flops 1179648 | bytes 11403264 | tf_op jit(solution)/shard_map/mul | solution.py:348
  83.2 5.6 %broadcast_multiply_fusion.6 = (f32[4,14,48,128]{3,2,1,0:T(8,128)}, f32[4,14,48,128]{3,2,1,0:T(8,128)S(1)}, f32[4,14,48,128]{3,2,1,0:T(8,128)}) fusion(f32[14,48,128]{2,1,0:T(8,128)S(1)} %slice.852, f32[4,16,48,128]{3,2,1,0:T(8,128)S(1)} %get-tuple-element.55, f32[4,16,48,128]{3,2,1,0:T(8,128)} %get-tuple-element.93, f32[14,48,128]{2,1,0:T(8,128)S(1)} %slice.846, ...), kind=kLoop, calls=%fused_computation.325 | loop fusion | flops 6881280 | bytes 18579456 | tf_op jit(solution)/shard_map/mul | solution.py:346
  88.9 2.7 fusion.72
  91.9 1.7 copy-done.23
  93.9 4.3 %broadcast_multiply_fusion.8 = (f32[4,12,48,128]{3,2,1,0:T(8,128)}, f32[4,12,48,128]{3,2,1,0:T(8,128)S(1)}, f32[4,12,48,128]{3,2,1,0:T(8,128)}) fusion(f32[12,48,128]{2,1,0:T(8,128)S(1)} %slice.878, f32[4,14,48,128]{3,2,1,0:T(8,128)S(1)} %get-tuple-element.52, f32[4,14,48,128]{3,2,1,0:T(8,128)S(1)} %get-tuple-element.111, f32[12,48,128]{2,1,0:T(8,128)S(1)} %slice.871, ...), kind=kLoop, calls=%fused_computation.327 | loop fusion | flops 5898240 | bytes 15925248 | tf_op jit(solution)/shard_map/mul | solution.py:346
  106.8 5.5 %select_reduce_fusion = f32[8,1024]{1,0:T(8,128)S(1)} fusion(pred[256,1024]{1,0:T(8,128)(4,1)S(1)} %fusion.123, f32[8,256,128]{2,1,0:T(8,128)} %bitcast.62, s32[1024]{0:T(1024)S(1)} %get-tuple-element.163), kind=kOutput, calls=%fused_computation.36 | convolution fusion | flops 3225542656 | bytes 1347584 | tf_op jit(solution)/shard_map/dot_general | solution.py:367
  113.3 39.3 %shard_map.123 = f32[8,128]{1,0:T(8,128)} custom-call(f32[8,128]{1,0:T(8,128)} %pad_bitcast_fusion.1.x_ref), custom_call_target="tpu_custom_call" | custom-call | tf_op jit(solution)/shard_map/pallas_call | solution.py:204
  152.7 1.5 slice.727
  155.5 2.3 fusion.1.x_ref
  157.9 9.5 %shard_map.124 = f32[4,20,48,128]{3,2,1,0:T(8,128)S(1)} custom-call(f32[4,8,32,128]{3,2,1,0:T(8,128)S(1)} %fusion.1.x_ref), custom_call_target="tpu_custom_call" | custom-call | tf_op jit(solution)/shard_map/pallas_call | solution.py:133
  168.4 2.1 fusion.27
  172.0 3.3 %broadcast_multiply_fusion.2 = (f32[4,18,48,128]{3,2,1,0:T(8,128)}, f32[4,18,48,128]{3,2,1,0:T(8,128)}, f32[4,18,48,128]{3,2,1,0:T(8,128)}) fusion(f32[18,48,128]{2,1,0:T(8,128)S(1)} %copy-done.72, f32[4,20,48,128]{3,2,1,0:T(8,128)S(1)} %get-tuple-element.63, f32[4,20,48,128]{3,2,1,0:T(8,128)S(1)} %get-tuple-element.67, f32[18,48,128]{2,1,0:T(8,128)S(1)} %slice.809, ...), kind=kLoop, calls=%fused_computation.309 | loop fusion | flops 8847360 | bytes 23887872 | tf_op jit(solution)/shard_map/mul | solution.py:346
  175.3 10.6 %fusion.33 = (f32[4,18,48,128]{3,2,1,0:T(8,128)}, f32[4,18,48,128]{3,2,1,0:T(8,128)}, f32[4,18,48,128]{3,2,1,0:T(8,128)}, f32[4,18,48,128]{3,2,1,0:T(8,128)}, f3...) fusion(f32[4,18,48,128]{3,2,1,0:T(8,128)} %get-tuple-element.41, f32[18,48,128]{2,1,0:T(8,128)S(1)} %copy-done.28), kind=kLoop, calls=%fused_computation.117 | loop fusion | flops 1327104 | bytes 12828672 | tf_op jit(solution)/shard_map/mul | solution.py:348
  186.0 8.0 %broadcast_multiply_fusion.3 = (f32[4,16,48,128]{3,2,1,0:T(8,128)}, f32[4,16,48,128]{3,2,1,0:T(8,128)S(1)}, f32[4,16,48,128]{3,2,1,0:T(8,128)}) fusion(f32[16,48,128]{2,1,0:T(8,128)} %copy-done.40, f32[4,18,48,128]{3,2,1,0:T(8,128)} %get-tuple-element.41, f32[4,18,48,128]{3,2,1,0:T(8,128)} %get-tuple-element.75, f32[16,48,128]{2,1,0:T(8,128)} %copy-done.39, ...), kind=kLoop, calls=%fused_computation.322 | loop fusion | flops 7864320 | bytes 21233664 | tf_op jit(solution)/shard_map/mul | solution.py:346
  194.0 4.1 %fusion.49 = (f32[4,16,48,128]{3,2,1,0:T(8,128)S(1)}, f32[4,16,48,128]{3,2,1,0:T(8,128)}, f32[4,16,48,128]{3,2,1,0:T(8,128)}, f32[4,16,48,128]{3,2,1,0:T(8,128)}...) fusion(f32[4,16,48,128]{3,2,1,0:T(8,128)S(1)} %get-tuple-element.38, f32[16,48,128]{2,1,0:T(8,128)S(1)} %copy-done.32), kind=kLoop, calls=%fused_computation.142 | loop fusion | flops 1179648 | bytes 11403264 | tf_op jit(solution)/shard_map/mul | solution.py:348
  198.1 6.1 %broadcast_multiply_fusion.5 = (f32[4,14,48,128]{3,2,1,0:T(8,128)}, f32[4,14,48,128]{3,2,1,0:T(8,128)S(1)}, f32[4,14,48,128]{3,2,1,0:T(8,128)}) fusion(f32[14,48,128]{2,1,0:T(8,128)} %copy-done.49, f32[4,16,48,128]{3,2,1,0:T(8,128)S(1)} %get-tuple-element.38, f32[4,16,48,128]{3,2,1,0:T(8,128)} %get-tuple-element.87, f32[14,48,128]{2,1,0:T(8,128)} %copy-done.48, ...), kind=kLoop, calls=%fused_computation.324 | loop fusion | flops 6881280 | bytes 18579456 | tf_op jit(solution)/shard_map/mul | solution.py:346
  204.2 2.6 fusion.75
  206.8 3.8 %broadcast_multiply_fusion.7 = (f32[4,12,48,128]{3,2,1,0:T(8,128)S(1)}, f32[4,12,48,128]{3,2,1,0:T(8,128)S(1)}, f32[4,12,48,128]{3,2,1,0:T(8,128)S(1)}, f32[4,12,48,128]{3,2,1,0:T(8,128)S(1)}) fusion(f32[12,48,128]{2,1,0:T(8,128)} %copy-done.60, f32[4,14,48,128]{3,2,1,0:T(8,128)S(1)} %get-tuple-element.35, f32[4,14,48,128]{3,2,1,0:T(8,128)S(1)} %get-tuple-element.105, ...), kind=kLoop, calls=%fused_computation.326 | loop fusion | flops 5898240 | bytes 17104896 | tf_op jit(solution)/shard_map/mul | solution.py:346
  217.0 1.4 fusion.159
  221.5 17.2 %shard_map.125 = f32[8,64,128]{2,1,0:T(8,128)} custom-call(f32[8,64,128]{2,1,0:T(8,128)} %reshape.392.x_ref), custom_call_target="tpu_custom_call" | custom-call | tf_op jit(solution)/shard_map/pallas_call | solution.py:50
  245.6 33.7 %shard_map.126 = f32[8,128]{1,0:T(8,128)} custom-call(f32[8,128]{1,0:T(8,128)} %fusion.210.x_ref), custom_call_target="tpu_custom_call" | custom-call | tf_op jit(solution)/shard_map/pallas_call | solution.py:204
  285.1 16.2 %shard_map.127 = f32[8,128]{1,0:T(8,128)} custom-call(f32[8,128]{1,0:T(8,128)} %pad_bitcast_fusion.x_ref), custom_call_target="tpu_custom_call" | custom-call | tf_op jit(solution)/shard_map/pallas_call | solution.py:204
  (280 shorter events, 48.5 us)
Async XLA Ops:
  52.6 4.1 %copy-start.17 = (f32[20,48,128]{2,1,0:T(8,128)}, f32[20,48,128]{2,1,0:T(8,128)S(1)}, u32[]{:S(2)}) copy-start(f32[20,48,128]{2,1,0:T(8,128)S(1)} %get-tuple-element.44) | copy-start | bytes 1474564
  54.5 48.1 %copy-start.1 = (f32[20,48,128]{2,1,0:T(8,128)}, f32[20,48,128]{2,1,0:T(8,128)S(1)}, u32[]{:S(2)}) copy-start(f32[20,48,128]{2,1,0:T(8,128)S(1)} %get-tuple-element.138) | copy-start | bytes 1474564
  54.5 49.0 %copy-start.7 = (f32[20,48,128]{2,1,0:T(8,128)}, f32[20,48,128]{2,1,0:T(8,128)S(1)}, u32[]{:S(2)}) copy-start(f32[20,48,128]{2,1,0:T(8,128)S(1)} %get-tuple-element.140) | copy-start | bytes 1474564
  54.5 49.0 %copy-start.5 = (f32[20,48,128]{2,1,0:T(8,128)}, f32[20,48,128]{2,1,0:T(8,128)S(1)}, u32[]{:S(2)}) copy-start(f32[20,48,128]{2,1,0:T(8,128)S(1)} %get-tuple-element.139) | copy-start | bytes 1474564
  68.1 7.8 %copy-start.37 = (f32[16,48,128]{2,1,0:T(8,128)}, f32[16,48,128]{2,1,0:T(8,128)S(1)}, u32[]{:S(2)}) copy-start(f32[16,48,128]{2,1,0:T(8,128)S(1)} %slice.818) | copy-start | bytes 1179652
  68.2 7.7 %copy-start.38 = (f32[16,48,128]{2,1,0:T(8,128)}, f32[16,48,128]{2,1,0:T(8,128)S(1)}, u32[]{:S(2)}) copy-start(f32[16,48,128]{2,1,0:T(8,128)S(1)} %slice.820) | copy-start | bytes 1179652
  68.2 7.7 %copy-start.39 = (f32[16,48,128]{2,1,0:T(8,128)}, f32[16,48,128]{2,1,0:T(8,128)S(1)}, u32[]{:S(2)}) copy-start(f32[16,48,128]{2,1,0:T(8,128)S(1)} %slice.822) | copy-start | bytes 1179652
  70.2 5.7 %copy-start.40 = (f32[16,48,128]{2,1,0:T(8,128)}, f32[16,48,128]{2,1,0:T(8,128)S(1)}, u32[]{:S(2)}) copy-start(f32[16,48,128]{2,1,0:T(8,128)S(1)} %slice.827) | copy-start | bytes 1179652
  76.0 4.6 %copy-start.31 = (f32[16,48,128]{2,1,0:T(8,128)}, f32[16,48,128]{2,1,0:T(8,128)S(1)}, u32[]{:S(2)}) copy-start(f32[16,48,128]{2,1,0:T(8,128)S(1)} %slice.828) | copy-start | bytes 1179652
  76.0 4.6 %copy-start.11 = (f32[20,48,128]{2,1,0:T(8,128)S(1)}, f32[20,48,128]{2,1,0:T(8,128)}, u32[]{:S(2)}) copy-start(f32[20,48,128]{2,1,0:T(8,128)} %get-tuple-element.142) | copy-start | bytes 1474564
  76.0 4.6 %copy-start.9 = (f32[20,48,128]{2,1,0:T(8,128)S(1)}, f32[20,48,128]{2,1,0:T(8,128)}, u32[]{:S(2)}) copy-start(f32[20,48,128]{2,1,0:T(8,128)} %get-tuple-element.141) | copy-start | bytes 1474564
  80.7 8.2 %copy-start.43 = (f32[14,48,128]{2,1,0:T(8,128)}, f32[14,48,128]{2,1,0:T(8,128)S(1)}, u32[]{:S(2)}) copy-start(f32[14,48,128]{2,1,0:T(8,128)S(1)} %slice.840) | copy-start | bytes 1032196
  80.7 8.1 %copy-start.45 = (f32[14,48,128]{2,1,0:T(8,128)}, f32[14,48,128]{2,1,0:T(8,128)S(1)}, u32[]{:S(2)}) copy-start(f32[14,48,128]{2,1,0:T(8,128)S(1)} %slice.842) | copy-start | bytes 1032196
  80.8 8.1 %copy-start.47 = (f32[14,48,128]{2,1,0:T(8,128)}, f32[14,48,128]{2,1,0:T(8,128)S(1)}, u32[]{:S(2)}) copy-start(f32[14,48,128]{2,1,0:T(8,128)S(1)} %slice.844) | copy-start | bytes 1032196
  81.8 7.1 %copy-start.48 = (f32[14,48,128]{2,1,0:T(8,128)}, f32[14,48,128]{2,1,0:T(8,128)S(1)}, u32[]{:S(2)}) copy-start(f32[14,48,128]{2,1,0:T(8,128)S(1)} %slice.846) | copy-start | bytes 1032196
  83.2 5.7 %copy-start.49 = (f32[14,48,128]{2,1,0:T(8,128)}, f32[14,48,128]{2,1,0:T(8,128)S(1)}, u32[]{:S(2)}) copy-start(f32[14,48,128]{2,1,0:T(8,128)S(1)} %slice.852) | copy-start | bytes 1032196
  91.6 6.6 %copy-start.54 = (f32[12,48,128]{2,1,0:T(8,128)}, f32[12,48,128]{2,1,0:T(8,128)S(1)}, u32[]{:S(2)}) copy-start(f32[12,48,128]{2,1,0:T(8,128)S(1)} %slice.861) | copy-start | bytes 884740
  91.7 6.5 %copy-start.56 = (f32[12,48,128]{2,1,0:T(8,128)}, f32[12,48,128]{2,1,0:T(8,128)S(1)}, u32[]{:S(2)}) copy-start(f32[12,48,128]{2,1,0:T(8,128)S(1)} %slice.865) | copy-start | bytes 884740
  91.7 6.5 %copy-start.57 = (f32[12,48,128]{2,1,0:T(8,128)}, f32[12,48,128]{2,1,0:T(8,128)S(1)}, u32[]{:S(2)}) copy-start(f32[12,48,128]{2,1,0:T(8,128)S(1)} %slice.867) | copy-start | bytes 884740
  91.8 6.4 %copy-start.58 = (f32[12,48,128]{2,1,0:T(8,128)}, f32[12,48,128]{2,1,0:T(8,128)S(1)}, u32[]{:S(2)}) copy-start(f32[12,48,128]{2,1,0:T(8,128)S(1)} %slice.869) | copy-start | bytes 884740
  91.8 6.4 %copy-start.59 = (f32[12,48,128]{2,1,0:T(8,128)}, f32[12,48,128]{2,1,0:T(8,128)S(1)}, u32[]{:S(2)}) copy-start(f32[12,48,128]{2,1,0:T(8,128)S(1)} %slice.871) | copy-start | bytes 884740
  93.9 4.3 %copy-start.60 = (f32[12,48,128]{2,1,0:T(8,128)}, f32[12,48,128]{2,1,0:T(8,128)S(1)}, u32[]{:S(2)}) copy-start(f32[12,48,128]{2,1,0:T(8,128)S(1)} %slice.878) | copy-start | bytes 884740
  157.9 9.5 %copy-start.71 = (f32[20,48,128]{2,1,0:T(8,128)S(1)}, f32[20,48,128]{2,1,0:T(8,128)}, u32[]{:S(2)}) copy-start(f32[20,48,128]{2,1,0:T(8,128)} %get-tuple-element.43) | copy-start | bytes 1474564
  175.3 10.7 %copy-start.34 = (f32[16,48,128]{2,1,0:T(8,128)S(1)}, f32[16,48,128]{2,1,0:T(8,128)}, u32[]{:S(2)}) copy-start(f32[16,48,128]{2,1,0:T(8,128)} %copy-done.33) | copy-start | bytes 1179652
  175.3 10.7 %copy-start.36 = (f32[16,48,128]{2,1,0:T(8,128)S(1)}, f32[16,48,128]{2,1,0:T(8,128)}, u32[]{:S(2)}) copy-start(f32[16,48,128]{2,1,0:T(8,128)} %copy-done.35) | copy-start | bytes 1179652
  186.0 8.0 %copy-start.32 = (f32[16,48,128]{2,1,0:T(8,128)S(1)}, f32[16,48,128]{2,1,0:T(8,128)}, u32[]{:S(2)}) copy-start(f32[16,48,128]{2,1,0:T(8,128)} %copy-done.31) | copy-start | bytes 1179652
  194.0 4.1 %copy-start.42 = (f32[14,48,128]{2,1,0:T(8,128)S(1)}, f32[14,48,128]{2,1,0:T(8,128)}, u32[]{:S(2)}) copy-start(f32[14,48,128]{2,1,0:T(8,128)} %copy-done.41) | copy-start | bytes 1032196
  198.1 6.1 %copy-start.51 = (f32[14,48,128]{2,1,0:T(8,128)S(1)}, f32[14,48,128]{2,1,0:T(8,128)}, u32[]{:S(2)}) copy-start(f32[14,48,128]{2,1,0:T(8,128)} %copy-done.50) | copy-start | bytes 1032196
  220.2 20.4 %copy-start.77 = (f32[8,32,16]{1,2,0:T(8,128)S(1)}, f32[8,32,16]{1,2,0:T(8,128)}, u32[]{:S(2)}) copy-start(f32[8,32,16]{1,2,0:T(8,128)} %param.17) | copy-start | bytes 49156
  220.2 20.5 %copy-start.73 = (f32[8,32,16]{1,2,0:T(8,128)S(1)}, f32[8,32,16]{1,2,0:T(8,128)}, u32[]{:S(2)}) copy-start(f32[8,32,16]{1,2,0:T(8,128)} %param.15) | copy-start | bytes 49156
  220.3 20.6 %copy-start.78 = (f32[8,32,16]{1,2,0:T(8,128)S(1)}, f32[8,32,16]{1,2,0:T(8,128)}, u32[]{:S(2)}) copy-start(f32[8,32,16]{1,2,0:T(8,128)} %param.18) | copy-start | bytes 49156
  220.3 20.7 %copy-start.74 = (f32[8,32,16]{1,2,0:T(8,128)S(1)}, f32[8,32,16]{1,2,0:T(8,128)}, u32[]{:S(2)}) copy-start(f32[8,32,16]{1,2,0:T(8,128)} %param.16) | copy-start | bytes 49156
  (50 other events, 91.0 us)

commit v6 on v4

--- a/solution.py
+++ b/solution.py
@@ -147,8 +147,14 @@
     )(x)
 
 
-def _reduce_kernel(axes, x_ref, o_ref, *scratch):
+def _reduce_kernel(axes, scatter, *refs):
     stages = len(axes)
+    if scatter:
+        g_ref, x_ref, h_ref, o_ref, g_slots, g_send, g_recv, g_local = refs[:8]
+        scratch = refs[8:]
+    else:
+        x_ref, o_ref = refs[:2]
+        scratch = refs[2:]
     slots, sends, recvs = scratch[:stages], scratch[stages : 2 * stages], scratch[2 * stages : 3 * stages]
     held = scratch[3 * stages :]
     barrier = pltpu.get_barrier_semaphore()
@@ -162,6 +168,24 @@
             )
         peers += n - 1
     pl.semaphore_wait(barrier, peers)
+    if scatter:
+        n = lax.axis_size("src")
+        me = lax.axis_index("src")
+        parts = []
+        for k in range(1, n):
+            peer = lax.rem(me + k, n)
+            copy = pltpu.make_async_remote_copy(
+                src_ref=g_ref.at[peer],
+                dst_ref=g_slots.at[me],
+                send_sem=g_send.at[k - 1],
+                recv_sem=g_recv.at[k - 1],
+                device_id={"src": peer},
+                device_id_type=MESH,
+            )
+            copy.start()
+            parts.append(copy)
+        own = pltpu.make_async_copy(g_ref.at[me], g_slots.at[me], g_local)
+        own.start()
     value = x_ref
     for i, axis in enumerate(axes):
         n = lax.axis_size(axis)
@@ -189,9 +213,17 @@
             value = held[i]
         else:
             o_ref[...] = total
-
-
-def small_sum(values, axes, cid):
+    if scatter:
+        own.wait()
+        for copy in parts:
+            copy.wait()
+        total = g_slots[0]
+        for j in range(1, lax.axis_size("src")):
+            total = total + g_slots[j]
+        h_ref[...] = total
+
+
+def small_sum(values, axes, cid, spread=None):
     count = values.shape[0]
     packed = jnp.pad(values, (0, 1024 - count)).reshape(8, 128)
     sizes = [lax.axis_size(axis) for axis in axes]
@@ -201,16 +233,34 @@
         + [pltpu.SemaphoreType.DMA((n - 1,)) for n in sizes]
         + [pltpu.VMEM((8, 128), jnp.float32) for n in sizes[:-1]]
     )
-    total = pl.pallas_call(
-        functools.partial(_reduce_kernel, tuple(axes)),
-        out_shape=jax.ShapeDtypeStruct((8, 128), jnp.float32),
-        in_specs=[pl.BlockSpec(memory_space=pltpu.VMEM)],
-        out_specs=pl.BlockSpec(memory_space=pltpu.VMEM),
+    small = jax.ShapeDtypeStruct((8, 128), jnp.float32)
+    operands = (packed,)
+    out_shape = small
+    if spread is not None:
+        n = spread.shape[0]
+        scratch = [
+            pltpu.VMEM(spread.shape, jnp.float32),
+            pltpu.SemaphoreType.DMA((n - 1,)),
+            pltpu.SemaphoreType.DMA((n - 1,)),
+            pltpu.SemaphoreType.DMA,
+        ] + scratch
+        operands = (spread, packed)
+        out_shape = (jax.ShapeDtypeStruct(spread.shape[1:], jnp.float32), small)
+    result = pl.pallas_call(
+        functools.partial(_reduce_kernel, tuple(axes), spread is not None),
+        out_shape=out_shape,
+        in_specs=[pl.BlockSpec(memory_space=pltpu.VMEM)] * len(operands),
+        out_specs=(
+            (pl.BlockSpec(memory_space=pltpu.VMEM),) * 2
+            if spread is not None
+            else pl.BlockSpec(memory_space=pltpu.VMEM)
+        ),
         scratch_shapes=scratch,
         compiler_params=pltpu.CompilerParams(collective_id=cid, has_side_effects=True),
-    )(packed)
-    return total.reshape(-1)[:count]
-
+    )(*operands)
+    if spread is not None:
+        return result[0], result[1].reshape(-1)[:count]
+    return result.reshape(-1)[:count]
 
 def padded_2(block, sides, width):
     for axis, dim in sides:
@@ -291,9 +341,9 @@
     sources, cx, cy, cz = background.shape
     n_src = lax.axis_size("src")
     slab = v_kappa.shape[2]
-    pair = jnp.stack([v_kappa, v_absorb]).reshape(-1, 128)
-    gathered = exchange(pair, "src", 0).reshape((n_src, 2, cx, cy, slab))
-    full_k, full_a = jnp.transpose(gathered, (1, 2, 3, 0, 4)).reshape(2, cx, cy, cz)
+    quad = jnp.stack([v_kappa, v_absorb, q_kappa, q_absorb]).reshape(-1, 128)
+    gathered = exchange(quad, "src", 0).reshape((n_src, 4, cx, cy, slab))
+    full_k, full_a, full_qk, full_qa = jnp.transpose(gathered, (1, 2, 3, 0, 4)).reshape(4, cx, cy, cz)
     width = ITERS
     width_y = 8
     region_of = labels.astype(jnp.float32)[None]
@@ -350,7 +400,12 @@
         ],
         axis=1,
     )
-    sums = small_sum(partial.reshape(-1), ("gy", "gx"), 1).reshape(sources, 4, 1)
+    block_vv = jnp.sum(full_k * full_k) + jnp.sum(full_a * full_a)
+    block_qv = jnp.sum(full_qk * full_k) + jnp.sum(full_qa * full_a)
+    partial = jnp.concatenate([partial.reshape(-1), jnp.stack([block_vv, block_qv])])
+    sums = small_sum(partial, ("gy", "gx"), 1)
+    vv_sum, qv_sum = sums[4 * sources], sums[4 * sources + 1]
+    sums = sums[: 4 * sources].reshape(sources, 4, 1)
     total, seen_sum, cross, square = sums[:, 0], sums[:, 1], sums[:, 2], sums[:, 3]
     mean_base = total / det_cells.shape[0]
     ratio = base / total
@@ -370,14 +425,14 @@
         grad_k = grad_k - 0.5 * jnp.sum((background - near_phi) * (dual - near_dual), axis=0)
     grads = jnp.stack([grad_k, grad_a]).reshape(2, cx, cy, n_src, slab)
     grads = jnp.transpose(grads, (3, 0, 1, 2, 4)).reshape(n_src, -1, 128)
-    hv = jnp.sum(exchange(grads, "src", 3, scatter=True), axis=0).reshape(2, cx, cy, slab)
+    block_hv = jnp.sum(grad_k * full_k) + jnp.sum(grad_a * full_a)
+    hv, hv_sum = small_sum(block_hv[None], ("gy", "gx", "src"), 3, spread=grads)
+    hv = hv.reshape(2, cx, cy, slab)
     hv_k, hv_a = hv[0], hv[1]
     cell_count = cx * lax.axis_size("gx") * cy * lax.axis_size("gy") * cz
     w_k = hv_k - beta_prev[0] * q_kappa
     w_a = hv_a - beta_prev[0] * q_absorb
-    local_wv = jnp.sum(w_k * v_kappa) + jnp.sum(w_a * v_absorb)
-    local_vv = jnp.sum(v_kappa * v_kappa) + jnp.sum(v_absorb * v_absorb)
-    wv_sum, vv_sum = small_sum(jnp.stack([local_wv, local_vv]), ("gy", "gx", "src"), 4)
+    wv_sum = hv_sum[0] - beta_prev[0] * qv_sum
     alpha = wv_sum / cell_count / (vv_sum / cell_count + eps_norm)
     r_k = w_k - alpha * v_kappa
     r_a = w_a - alpha * v_absorb

time: 234 us -> 240 us (1.026)
  local copies, waits for them, and re-layouts: 22.1 us -> 27.4 us
  Pallas kernels: 155 us -> 151 us
  other arithmetic: 36.9 us -> 40.4 us
    pallas_call x2 -> x1, Pallas kernels: 33.9 us -> 21.6 us  [exchange(): pl.pallas_call(functools.partial(_exchange_kernel, axis, n, scatter), out...]
    pallas_call x3, Pallas kernels: 89.1 us -> 95.1 us  [small_sum(): pl.pallas_call(functools.partial(_reduce_kernel, tuple(axes), spread is n...]
    another operation x7 -> x5, local copies, waits for them, and re-layouts: 4.96 us -> 1.22 us  [the longest x4 1 us: per_device(): full_k, full_a, full_qk, full_qa = jnp.transpose(gathered, (1, 2, 3, 0, 4...]
    reduce_sum x4 -> x2, other arithmetic: 2.9 us -> 5.86 us  [the longest x1 3.43 us: per_device(): block_vv = jnp.sum(full_k * full_k) + jnp.sum(full_a * full_a)]
    slice x2 -> x4, local copies, waits for them, and re-layouts: 2.64 us -> 5.25 us  [the longest x1 1.45 us: per_device(): sums = sums[:4 * sources].reshape(sources, 4, 1)]
    unnamed x60 -> x66, local copies, waits for them, and re-layouts: 6.06 us -> 7.03 us
where the time goes in v6:
time: 240 us; the launch traced here: 239 us
  Pallas kernels  151 us (63%)
  other arithmetic  40.4 us (17%)
  local copies, waits for them, and re-layouts  27.4 us (11%)
  matrix products  10.2 us (4%)
  between operations  9.89 us (4%)
    pallas_call x3, Pallas kernels, small_sum(): pl.pallas_call(functools.partial(_reduce_kernel, tuple(axes), spread is n...  95.1 us
    pallas_call x2, Pallas kernels, halo_block(): pl.pallas_call(functools.partial(_halo_kernel, hx, hy), out_shape=jax.Sha...  34.6 us
    pallas_call x1, Pallas kernels, exchange(): pl.pallas_call(functools.partial(_exchange_kernel, axis, n, scatter), out...  21.6 us
    add x8, other arithmetic, chebyshev(): step_dir = rho_next * rho * step_dir + 2.0 * rho_next / delta * remain  18.3 us
    unnamed x66, local copies, waits for them, and re-layouts  7.03 us
    dot_general x1, matrix products, per_device(): jnp.dot(both, depth_hot, precision=lax.Precision.HIGHEST)  5.58 us

profile of v6, /device:TPU:1, one launch (start us, length us, event | category | flops | bytes accessed | tf_op | source)
XLA Modules:
  0.0 239.2 jit_solution(9009458479974556196)
XLA Ops:
  2.6 21.6 %shard_map.121 = f32[8,128,128]{2,1,0:T(8,128)} custom-call(f32[128,128]{1,0:T(8,128)} %reshape.364.x_ref), custom_call_target="tpu_custom_call" | custom-call | tf_op jit(solution)/shard_map/pallas_call | solution.py:50
  24.3 3.7 %reshape.365 = f32[8,4,8,32,16]{4,3,2,1,0:T(8,128)} reshape(f32[8,128,128]{2,1,0:T(8,128)} %shard_map.121) | data formatting | bytes 1048576 | tf_op jit(solution)/shard_map/reshape | solution.py:345
  28.0 3.4 %multiply_reduce_fusion.2 = (f32[]{:T(128)}, f32[]{:T(128)}, f32[]{:T(128)}, f32[]{:T(128)}, f32[1,8,32,8,16]{4,2,1,0,3:T(8,128)S(1)}, /*index=5*/f32[1,8,32,8,16]{4,2,1,0,3:T(8,128)S(1)}) fusion(f32[4,8,32,8,16]{4,2,1,0,3:T(8,128)} %bitcast.61), kind=kLoop, calls=%fused_computation.315 | loop fusion | flops 262140 | bytes 786448 | tf_op jit(solution)/shard_map/reduce_sum | solution.py:403
  32.9 24.7 %shard_map.122 = f32[7,20,48,128]{3,2,1,0:T(8,128)S(1)} custom-call(f32[7,8,32,128]{3,2,1,0:T(8,128)S(1)} %pad_maximum_fusion.1.x_ref), custom_call_target="tpu_custom_call" | custom-call | tf_op jit(solution)/shard_map/pallas_call | solution.py:133
  58.7 2.3 fusion
  61.0 1.7 fusion.289
  62.8 1.4 broadcast_multiply_fusion.2
  65.4 1.2 copy-done.19
  66.6 2.1 broadcast_multiply_fusion.1
  68.7 2.3 multiply_add_fusion.7
  71.1 2.3 multiply_add_fusion.6
  73.4 2.3 multiply_add_fusion.5
  75.6 2.3 multiply_add_fusion.4
  78.0 1.8 fusion.107
  82.2 5.6 %select_reduce_fusion = f32[8,1024]{1,0:T(8,128)S(1)} fusion(pred[256,1024]{1,0:T(8,128)(4,1)S(1)} %fusion.217, f32[8,256,128]{2,1,0:T(8,128)} %bitcast.71, s32[1024]{0:T(1024)S(1)} %get-tuple-element.99), kind=kOutput, calls=%fused_computation.66 | convolution fusion | flops 3225542656 | bytes 1347584 | tf_op jit(solution)/shard_map/dot_general | solution.py:391
  91.3 38.9 %shard_map.123 = f32[8,128]{1,0:T(8,128)} custom-call(f32[8,128]{1,0:T(8,128)} %fusion.271.refs_0_), custom_call_target="tpu_custom_call" | custom-call | tf_op jit(solution)/shard_map/pallas_call | solution.py:249
  130.2 1.4 slice.431
  133.1 2.3 fusion.1.x_ref
  135.4 9.9 %shard_map.124 = f32[4,20,48,128]{3,2,1,0:T(8,128)S(1)} custom-call(f32[4,8,32,128]{3,2,1,0:T(8,128)S(1)} %fusion.1.x_ref), custom_call_target="tpu_custom_call" | custom-call | tf_op jit(solution)/shard_map/pallas_call | solution.py:133
  147.2 2.3 multiply_add_fusion.3
  149.5 2.3 multiply_add_fusion.2
  151.9 2.3 multiply_add_fusion.1
  154.2 2.2 multiply_add_fusion
  156.4 2.9 %fusion.204 = f32[4,20,48,128]{3,2,1,0:T(8,128)S(1)} fusion(f32[4,20,48,128]{3,2,1,0:T(8,128)S(1)} %get-tuple-element.42, f32[4,20,48,128]{3,2,1,0:T(8,128)S(1)} %get-tuple-element.41, f32[4,20,48,128]{3,2,1,0:T(8,128)S(1)} %get-tuple-element.43, f32[4,20,48,128]{3,2,1,0:T(8,128)S(1)} %get-tuple-element.45, f32[4,20,48,128]{3,2,1,0:T(8,128)S(1)} %get-tuple-element.47, ...), kind=kLoop, calls=%fused_computation.284 | loop fusion | flops 14254080 | bytes 17203200 | tf_op jit(solution)/shard_map/add | solution.py:320
  160.4 1.3 fusion.220
  163.3 2.4 %multiply_reduce_fusion = (f32[]{:T(128)}, f32[]{:T(128)}) fusion(f32[1,8,32,8,16]{4,2,1,0,3:T(8,128)S(1)} %copy.63, f32[4,8,32,8,16]{4,2,1,0,3:T(8,128)} %bitcast.62, f32[1,8,32,8,16]{4,2,1,0,3:T(8,128)S(1)} %copy.62), kind=kLoop, calls=%fused_computation.313 | loop fusion | flops 131070 | bytes 524296 | tf_op jit(solution)/shard_map/reduce_sum | solution.py:428
  168.4 1.3 reshape.368.refs_0_
  169.6 38.1 %shard_map.125 = (f32[64,128]{1,0:T(8,128)}, f32[8,128]{1,0:T(8,128)}) custom-call(f32[8,64,128]{2,1,0:T(8,128)} %reshape.368.refs_0_, f32[8,128]{1,0:T(8,128)} %pad_bitcast_fusion.1.refs_1_), custom_call_target="tpu_custom_call" | custom-call | tf_op jit(solution)/shard_map/pallas_call | solution.py:249
  208.7 1.2 slice.481
  209.9 1.4 fusion.291
  217.2 18.1 %shard_map.126 = f32[8,128]{1,0:T(8,128)} custom-call(f32[8,128]{1,0:T(8,128)} %pad_bitcast_fusion.refs_0_), custom_call_target="tpu_custom_call" | custom-call | tf_op jit(solution)/shard_map/pallas_call | solution.py:249
  235.3 1.2 slice.485
  (117 shorter events, 20.8 us)
Async XLA Ops:
  31.5 1.0 copy-start.26
  31.8 1.1 copy-start.14
  57.6 1.1 copy-start.28
  57.6 1.1 copy-start.29
  62.7 1.6 copy-start.20
  64.2 4.5 %copy-start.17 = (f32[20,48,128]{2,1,0:T(8,128)}, f32[20,48,128]{2,1,0:T(8,128)S(1)}, u32[]{:S(2)}) copy-start(f32[20,48,128]{2,1,0:T(8,128)S(1)} %get-tuple-element.57) | copy-start | bytes 1474564
  64.3 13.7 %copy-start.12 = (f32[20,48,128]{2,1,0:T(8,128)}, f32[20,48,128]{2,1,0:T(8,128)S(1)}, u32[]{:S(2)}) copy-start(f32[20,48,128]{2,1,0:T(8,128)S(1)} %get-tuple-element.58) | copy-start | bytes 1474564
  65.1 12.8 %copy-start = (f32[20,48,128]{2,1,0:T(8,128)}, f32[20,48,128]{2,1,0:T(8,128)S(1)}, u32[]{:S(2)}) copy-start(f32[20,48,128]{2,1,0:T(8,128)S(1)} %get-tuple-element.76) | copy-start | bytes 1474564
  65.1 12.8 %copy-start.2 = (f32[20,48,128]{2,1,0:T(8,128)}, f32[20,48,128]{2,1,0:T(8,128)S(1)}, u32[]{:S(2)}) copy-start(f32[20,48,128]{2,1,0:T(8,128)S(1)} %get-tuple-element.77) | copy-start | bytes 1474564
  65.1 12.8 %copy-start.4 = (f32[20,48,128]{2,1,0:T(8,128)}, f32[20,48,128]{2,1,0:T(8,128)S(1)}, u32[]{:S(2)}) copy-start(f32[20,48,128]{2,1,0:T(8,128)S(1)} %get-tuple-element.78) | copy-start | bytes 1474564
  65.2 12.8 %copy-start.6 = (f32[20,48,128]{2,1,0:T(8,128)}, f32[20,48,128]{2,1,0:T(8,128)S(1)}, u32[]{:S(2)}) copy-start(f32[20,48,128]{2,1,0:T(8,128)S(1)} %get-tuple-element.79) | copy-start | bytes 1474564
  65.2 12.8 %copy-start.8 = (f32[20,48,128]{2,1,0:T(8,128)}, f32[20,48,128]{2,1,0:T(8,128)S(1)}, u32[]{:S(2)}) copy-start(f32[20,48,128]{2,1,0:T(8,128)S(1)} %get-tuple-element.80) | copy-start | bytes 1474564
  65.2 14.6 %copy-start.10 = (f32[20,48,128]{2,1,0:T(8,128)}, f32[20,48,128]{2,1,0:T(8,128)S(1)}, u32[]{:S(2)}) copy-start(f32[20,48,128]{2,1,0:T(8,128)S(1)} %get-tuple-element.81) | copy-start | bytes 1474564
  65.2 1.4 copy-start.19
  79.8 1.0 copy-start.15
  80.8 1.1 copy-start.27
  145.3 1.0 copy-start.1
  145.3 1.2 copy-start.3
  145.3 1.3 copy-start.5
  145.3 1.5 copy-start.7
  145.3 1.6 copy-start.9
  145.3 1.7 copy-start.11
  145.3 1.9 copy-start.18
  147.2 2.3 copy-start.13
  159.4 1.0 copy-start.16
  161.8 0.9 copy-start.21
  168.3 45.7 %copy-start.22 = (f32[8,32,16]{1,2,0:T(8,128)S(1)}, f32[8,32,16]{1,2,0:T(8,128)}, u32[]{:S(2)}) copy-start(f32[8,32,16]{1,2,0:T(8,128)} %param.17) | copy-start | bytes 49156
  168.4 45.8 %copy-start.23 = (f32[8,32,16]{1,2,0:T(8,128)S(1)}, f32[8,32,16]{1,2,0:T(8,128)}, u32[]{:S(2)}) copy-start(f32[8,32,16]{1,2,0:T(8,128)} %param.15) | copy-start | bytes 49156
  168.4 45.9 %copy-start.24 = (f32[8,32,16]{1,2,0:T(8,128)S(1)}, f32[8,32,16]{1,2,0:T(8,128)}, u32[]{:S(2)}) copy-start(f32[8,32,16]{1,2,0:T(8,128)} %param.18) | copy-start | bytes 49156
  168.4 46.0 %copy-start.25 = (f32[8,32,16]{1,2,0:T(8,128)S(1)}, f32[8,32,16]{1,2,0:T(8,128)}, u32[]{:S(2)}) copy-start(f32[8,32,16]{1,2,0:T(8,128)} %param.16) | copy-start | bytes 49156

commit v7 on v4

--- a/solution.py
+++ b/solution.py
@@ -193,17 +193,18 @@
 
 def small_sum(values, axes, cid):
     count = values.shape[0]
-    packed = jnp.pad(values, (0, 1024 - count)).reshape(8, 128)
+    rows = -(-count // 1024) * 8
+    packed = jnp.pad(values, (0, rows * 128 - count)).reshape(rows, 128)
     sizes = [lax.axis_size(axis) for axis in axes]
     scratch = (
-        [pltpu.VMEM((n, 8, 128), jnp.float32) for n in sizes]
+        [pltpu.VMEM((n, rows, 128), jnp.float32) for n in sizes]
         + [pltpu.SemaphoreType.DMA((n - 1,)) for n in sizes]
         + [pltpu.SemaphoreType.DMA((n - 1,)) for n in sizes]
-        + [pltpu.VMEM((8, 128), jnp.float32) for n in sizes[:-1]]
+        + [pltpu.VMEM((rows, 128), jnp.float32) for n in sizes[:-1]]
     )
     total = pl.pallas_call(
         functools.partial(_reduce_kernel, tuple(axes)),
-        out_shape=jax.ShapeDtypeStruct((8, 128), jnp.float32),
+        out_shape=jax.ShapeDtypeStruct((rows, 128), jnp.float32),
         in_specs=[pl.BlockSpec(memory_space=pltpu.VMEM)],
         out_specs=pl.BlockSpec(memory_space=pltpu.VMEM),
         scratch_shapes=scratch,
@@ -340,26 +341,25 @@
     both = jnp.concatenate([change, background], axis=0).reshape(-1, cz)
     picked = jnp.dot(both, depth_hot, precision=lax.Precision.HIGHEST).reshape(2 * sources, cx * cy, -1)
     picked = jnp.sum(jnp.where(plane_hot[None], picked, 0.0), axis=1)
-    seen, base = picked[:sources], picked[sources:]
-    partial = jnp.stack(
-        [
-            jnp.sum(base, axis=1),
-            jnp.sum(seen, axis=1),
-            jnp.sum(base * seen, axis=1),
-            jnp.sum(base * base, axis=1),
-        ],
-        axis=1,
-    )
-    sums = small_sum(partial.reshape(-1), ("gy", "gx"), 1).reshape(sources, 4, 1)
-    total, seen_sum, cross, square = sums[:, 0], sums[:, 1], sums[:, 2], sums[:, 3]
+    picks = small_sum(picked.reshape(-1), ("gy", "gx"), 1).reshape(2 * sources, -1)
+    seen, base = picks[:sources], picks[sources:]
+    total = jnp.sum(base, axis=1, keepdims=True)
     mean_base = total / det_cells.shape[0]
     ratio = base / total
-    jv_vals = (seen - ratio * seen_sum) / mean_base
-    ratio_jv = (cross / total - seen_sum * (square / (total * total))) / mean_base
-    weight = (jv_vals - ratio_jv) / mean_base
-    spread = jnp.where(plane_hot[None], weight[:, None, :], 0.0).reshape(sources * cx * cy, -1)
-    source = jnp.dot(spread, depth_hot.T, precision=lax.Precision.HIGHEST).reshape(change.shape)
-    dual_w = chebyshev(halo_block(source, width, width_y, 11), apply_op)
+    jv_vals = (seen - ratio * jnp.sum(seen, axis=1, keepdims=True)) / mean_base
+    weight = (jv_vals - jnp.sum(ratio * jv_vals, axis=1, keepdims=True)) / mean_base
+    near_x = ix - (anchor_x - width)
+    near_y = iy - (anchor_y - width_y)
+    held = (near_x >= 0) & (near_x < wx) & (near_y >= 0) & (near_y < wy)
+    wide_hot = (jnp.arange(wx * wy)[:, None] == (near_x * wy + near_y)[None, :]) & held[None, :]
+    wide_hot = wide_hot.astype(jnp.float32)
+    source_w = jnp.stack(
+        [
+            jnp.dot(wide_hot, weight[i][:, None] * depth_hot.T, precision=lax.Precision.HIGHEST)
+            for i in range(sources)
+        ]
+    ).reshape(sources, wx, wy, cz)
+    dual_w = chebyshev(source_w, apply_op)
     ring = (slice(None), slice(width - 1, width + cx + 1), slice(width_y - 1, width_y + cy + 1))
     phi_near = beside(phi_w[ring])
     dual_near = beside(dual_w[ring])

time: 234 us -> 216 us (0.923)
  Pallas kernels: 155 us -> 129 us
  matrix products: 10.2 us -> 16.4 us
    pallas_call x3, Pallas kernels: 89.1 us -> 74.4 us  [small_sum(): pl.pallas_call(functools.partial(_reduce_kernel, tuple(axes)), out_shape=...]
    pallas_call x2 -> x1, Pallas kernels: 32.5 us -> 23 us  [halo_block(): pl.pallas_call(functools.partial(_halo_kernel, hx, hy), out_shape=jax.Sha...]
    dot_general x1 -> x4, matrix products: 2.34 us -> 8.55 us  [per_device(): jnp.dot(wide_hot, weight[i][:, None] * depth_hot.T, precision=lax.Precisi...]
where the time goes in v7:
time: 216 us; the launch traced here: 213 us
  Pallas kernels  129 us (60%)
  other arithmetic  39.1 us (18%)
  local copies, waits for them, and re-layouts  20.2 us (9%)
  matrix products  16.4 us (8%)
  between operations  8.21 us (4%)
    pallas_call x3, Pallas kernels, small_sum(): pl.pallas_call(functools.partial(_reduce_kernel, tuple(axes)), out_shape=...  74.4 us
    pallas_call x2, Pallas kernels, exchange(): pl.pallas_call(functools.partial(_exchange_kernel, axis, n, scatter), out...  31.6 us
    pallas_call x1, Pallas kernels, halo_block(): pl.pallas_call(functools.partial(_halo_kernel, hx, hy), out_shape=jax.Sha...  23 us
    add x8, other arithmetic, chebyshev(): step_dir = rho_next * rho * step_dir + 2.0 * rho_next / delta * remain  18.6 us
    dot_general x4, matrix products, per_device(): jnp.dot(wide_hot, weight[i][:, None] * depth_hot.T, precision=lax.Precisi...  8.55 us
    unnamed x60, local copies, waits for them, and re-layouts  6.06 us
    dot_general x1, matrix products, per_device(): jnp.dot(both, depth_hot, precision=lax.Precision.HIGHEST)  5.53 us

profile of v7, /device:TPU:1, one launch (start us, length us, event | category | flops | bytes accessed | tf_op | source)
XLA Modules:
  0.0 212.9 jit_solution(11338219469439714594)
XLA Ops:
  2.5 16.7 %shard_map.121 = f32[8,64,128]{2,1,0:T(8,128)} custom-call(f32[64,128]{1,0:T(8,128)} %reshape.312.x_ref), custom_call_target="tpu_custom_call" | custom-call | tf_op jit(solution)/shard_map/pallas_call | solution.py:50
  19.2 1.7 reshape.313
  20.9 1.2 fusion.315
  22.1 1.6 copy.30
  24.8 23.0 %shard_map.122 = f32[7,20,48,128]{3,2,1,0:T(8,128)S(1)} custom-call(f32[7,8,32,128]{3,2,1,0:T(8,128)S(1)} %pad_maximum_fusion.2.x_ref), custom_call_target="tpu_custom_call" | custom-call | tf_op jit(solution)/shard_map/pallas_call | solution.py:133
  48.5 2.3 %fusion = f32[2,122880]{1,0:T(2,128)S(1)} fusion(f32[122880]{0:T(1024)S(1)} %bitcast.74, f32[1,16]{1,0:T(1,128)S(1)} %bitcast.81, f32[1,16]{1,0:T(1,128)S(1)} %bitcast.82), kind=kOutput, calls=%fused_computation.68 | convolution fusion | flops 49152032 | bytes 1474688 | tf_op jit(solution)/shard_map/dot_general | solution.py:315
  52.9 2.2 %broadcast_multiply_fusion.1 = (f32[4,20,48,128]{3,2,1,0:T(8,128)S(1)}, f32[4,20,48,128]{3,2,1,0:T(8,128)S(1)}) fusion(f32[4,20,48,128]{3,2,1,0:T(8,128)S(1)} %slice.361, f32[20,48,128]{2,1,0:T(8,128)S(1)} %get-tuple-element.79, f32[20,48,128]{2,1,0:T(8,128)S(1)} %get-tuple-element.83, f32[20,48,128]{2,1,0:T(8,128)S(1)} %get-tuple-element.82, ...), kind=kLoop, calls=%fused_computation.322 | loop fusion | flops 10321920 | bytes 9338880 | tf_op jit(solution)/shard_map/div | solution.py:269
  55.0 2.3 %multiply_add_fusion.7 = (f32[4,20,48,128]{3,2,1,0:T(8,128)S(1)}, f32[4,20,48,128]{3,2,1,0:T(8,128)S(1)}) fusion(f32[4,20,48,128]{3,2,1,0:T(8,128)S(1)} %get-tuple-element.41, f32[4,20,48,128]{3,2,1,0:T(8,128)S(1)} %get-tuple-element.40, f32[20,48,128]{2,1,0:T(8,128)S(1)} %get-tuple-element.62, f32[20,48,128]{2,1,0:T(8,128)S(1)} %get-tuple-element.58, ...), kind=kLoop, calls=%fused_computation.304 | loop fusion | flops 11304960 | bytes 11304960 | tf_op jit(solution)/shard_map/add | solution.py:275
  57.4 2.3 %multiply_add_fusion.6 = (f32[4,20,48,128]{3,2,1,0:T(8,128)S(1)}, f32[4,20,48,128]{3,2,1,0:T(8,128)S(1)}) fusion(f32[4,20,48,128]{3,2,1,0:T(8,128)S(1)} %get-tuple-element.36, f32[4,20,48,128]{3,2,1,0:T(8,128)S(1)} %get-tuple-element.37, f32[20,48,128]{2,1,0:T(8,128)S(1)} %get-tuple-element.62, f32[20,48,128]{2,1,0:T(8,128)S(1)} %get-tuple-element.58, ...), kind=kLoop, calls=%fused_computation.303 | loop fusion | flops 11304960 | bytes 11304960 | tf_op jit(solution)/shard_map/add | solution.py:275
  59.7 2.3 %multiply_add_fusion.5 = (f32[4,20,48,128]{3,2,1,0:T(8,128)S(1)}, f32[4,20,48,128]{3,2,1,0:T(8,128)S(1)}) fusion(f32[4,20,48,128]{3,2,1,0:T(8,128)S(1)} %get-tuple-element.34, f32[4,20,48,128]{3,2,1,0:T(8,128)S(1)} %get-tuple-element.35, f32[20,48,128]{2,1,0:T(8,128)S(1)} %get-tuple-element.62, f32[20,48,128]{2,1,0:T(8,128)S(1)} %get-tuple-element.58, ...), kind=kLoop, calls=%fused_computation.302 | loop fusion | flops 11304960 | bytes 11304960 | tf_op jit(solution)/shard_map/add | solution.py:275
  61.9 2.3 %multiply_add_fusion.4 = (f32[4,20,48,128]{3,2,1,0:T(8,128)S(1)}, f32[4,20,48,128]{3,2,1,0:T(8,128)S(1)}) fusion(f32[4,20,48,128]{3,2,1,0:T(8,128)S(1)} %get-tuple-element.32, f32[4,20,48,128]{3,2,1,0:T(8,128)S(1)} %get-tuple-element.33, f32[20,48,128]{2,1,0:T(8,128)S(1)} %get-tuple-element.62, f32[20,48,128]{2,1,0:T(8,128)S(1)} %get-tuple-element.58, ...), kind=kLoop, calls=%fused_computation.301 | loop fusion | flops 11304960 | bytes 11304960 | tf_op jit(solution)/shard_map/add | solution.py:275
  64.3 1.8 fusion.111
  67.2 1.1 pad_maximum_fusion.1
  68.5 5.5 %select_reduce_fusion = f32[8,1024]{1,0:T(8,128)S(1)} fusion(pred[256,1024]{1,0:T(8,128)(4,1)S(1)} %fusion.227, f32[8,256,128]{2,1,0:T(8,128)} %bitcast.71, s32[1024]{0:T(1024)S(1)} %get-tuple-element.87), kind=kOutput, calls=%fused_computation.66 | convolution fusion | flops 3225542656 | bytes 1347584 | tf_op jit(solution)/shard_map/dot_general | solution.py:342
  74.7 41.1 %shard_map.123 = f32[64,128]{1,0:T(8,128)} custom-call(f32[64,128]{1,0:T(8,128)} %reshape.314.x_ref), custom_call_target="tpu_custom_call" | custom-call | tf_op jit(solution)/shard_map/pallas_call | solution.py:205
  118.8 2.1 %fusion.9 = f32[960,128]{1,0:T(8,128)S(1)} fusion(s32[1024]{0:T(1024)S(1)} %get-tuple-element.89, pred[1024]{0:T(1024)(128)(4,1)S(1)} %get-tuple-element.91, f32[1024]{0:T(1024)S(1)} %bitcast.80, s32[1024]{0:T(1024)S(1)} %get-tuple-element.87), kind=kOutput, calls=%fused_computation.75 | convolution fusion | flops 1512177664 | bytes 504832 | tf_op jit(solution)/shard_map/dot_general | solution.py:358
  121.0 2.1 %fusion.7 = f32[960,128]{1,0:T(8,128)S(1)} fusion(s32[1024]{0:T(1024)S(1)} %get-tuple-element.89, pred[1024]{0:T(1024)(128)(4,1)S(1)} %get-tuple-element.91, f32[1024]{0:T(1024)S(1)} %bitcast.79, s32[1024]{0:T(1024)S(1)} %get-tuple-element.87), kind=kOutput, calls=%fused_computation.74 | convolution fusion | flops 1512177664 | bytes 504832 | tf_op jit(solution)/shard_map/dot_general | solution.py:358
  123.1 2.1 %fusion.5 = f32[960,128]{1,0:T(8,128)S(1)} fusion(s32[1024]{0:T(1024)S(1)} %get-tuple-element.89, pred[1024]{0:T(1024)(128)(4,1)S(1)} %get-tuple-element.91, f32[1024]{0:T(1024)S(1)} %bitcast.78, s32[1024]{0:T(1024)S(1)} %get-tuple-element.87), kind=kOutput, calls=%fused_computation.73 | convolution fusion | flops 1512177664 | bytes 504832 | tf_op jit(solution)/shard_map/dot_general | solution.py:358
  125.3 2.1 %fusion.3 = f32[960,128]{1,0:T(8,128)S(1)} fusion(s32[1024]{0:T(1024)S(1)} %get-tuple-element.89, pred[1024]{0:T(1024)(128)(4,1)S(1)} %get-tuple-element.91, f32[1024]{0:T(1024)S(1)} %bitcast.77, s32[1024]{0:T(1024)S(1)} %get-tuple-element.87), kind=kOutput, calls=%fused_computation.72 | convolution fusion | flops 1512177664 | bytes 504832 | tf_op jit(solution)/shard_map/dot_general | solution.py:358
  129.3 2.5 %multiply_add_fusion.3 = (f32[4,20,48,128]{3,2,1,0:T(8,128)S(1)}, f32[4,20,48,128]{3,2,1,0:T(8,128)S(1)}) fusion(f32[1,20,48,128]{3,2,1,0:T(8,128)S(1)} %bitcast.63, f32[1,20,48,128]{3,2,1,0:T(8,128)S(1)} %bitcast.60, f32[1,20,48,128]{3,2,1,0:T(8,128)S(1)} %bitcast.57, f32[1,20,48,128]{3,2,1,0:T(8,128)S(1)} %bitcast.54, ...), kind=kLoop, calls=%fused_computation.300 | loop fusion | flops 12779520 | bytes 11304960 | tf_op jit(solution)/shard_map/add | solution.py:275
  131.8 2.3 %multiply_add_fusion.2 = (f32[4,20,48,128]{3,2,1,0:T(8,128)S(1)}, f32[4,20,48,128]{3,2,1,0:T(8,128)S(1)}) fusion(f32[4,20,48,128]{3,2,1,0:T(8,128)S(1)} %get-tuple-element.28, f32[4,20,48,128]{3,2,1,0:T(8,128)S(1)} %get-tuple-element.29, f32[20,48,128]{2,1,0:T(8,128)S(1)} %copy-done.11, f32[20,48,128]{2,1,0:T(8,128)S(1)} %copy-done.3, ...), kind=kLoop, calls=%fused_computation.299 | loop fusion | flops 11304960 | bytes 11304960 | tf_op jit(solution)/shard_map/add | solution.py:275
  134.2 2.3 %multiply_add_fusion.1 = (f32[4,20,48,128]{3,2,1,0:T(8,128)S(1)}, f32[4,20,48,128]{3,2,1,0:T(8,128)S(1)}) fusion(f32[4,20,48,128]{3,2,1,0:T(8,128)S(1)} %get-tuple-element.26, f32[4,20,48,128]{3,2,1,0:T(8,128)S(1)} %get-tuple-element.27, f32[20,48,128]{2,1,0:T(8,128)S(1)} %copy-done.11, f32[20,48,128]{2,1,0:T(8,128)S(1)} %copy-done.3, ...), kind=kLoop, calls=%fused_computation.298 | loop fusion | flops 11304960 | bytes 11304960 | tf_op jit(solution)/shard_map/add | solution.py:275
  136.5 2.3 %multiply_add_fusion = (f32[4,20,48,128]{3,2,1,0:T(8,128)S(1)}, f32[4,20,48,128]{3,2,1,0:T(8,128)S(1)}) fusion(f32[4,20,48,128]{3,2,1,0:T(8,128)S(1)} %get-tuple-element.24, f32[4,20,48,128]{3,2,1,0:T(8,128)S(1)} %get-tuple-element.25, f32[20,48,128]{2,1,0:T(8,128)S(1)} %copy-done.11, f32[20,48,128]{2,1,0:T(8,128)S(1)} %copy-done.3, ...), kind=kLoop, calls=%fused_computation.297 | loop fusion | flops 11304960 | bytes 11304960 | tf_op jit(solution)/shard_map/add | solution.py:275
  138.9 3.0 %fusion.208 = f32[4,20,48,128]{3,2,1,0:T(8,128)S(1)} fusion(f32[4,20,48,128]{3,2,1,0:T(8,128)S(1)} %get-tuple-element.23, f32[4,20,48,128]{3,2,1,0:T(8,128)S(1)} %get-tuple-element.22, f32[4,20,48,128]{3,2,1,0:T(8,128)S(1)} %get-tuple-element.24, f32[4,20,48,128]{3,2,1,0:T(8,128)S(1)} %get-tuple-element.26, f32[4,20,48,128]{3,2,1,0:T(8,128)S(1)} %get-tuple-element.28, ...), kind=kLoop, calls=%fused_computation.285 | loop fusion | flops 15728640 | bytes 17203200 | tf_op jit(solution)/shard_map/add | solution.py:271
  143.0 1.4 fusion.230
  146.6 1.3 reshape.315.x_ref
  147.8 14.9 %shard_map.124 = f32[8,64,128]{2,1,0:T(8,128)} custom-call(f32[8,64,128]{2,1,0:T(8,128)} %reshape.315.x_ref), custom_call_target="tpu_custom_call" | custom-call | tf_op jit(solution)/shard_map/pallas_call | solution.py:50
  162.8 1.0 reduce_sum.200
  169.6 16.9 %shard_map.125 = f32[8,128]{1,0:T(8,128)} custom-call(f32[8,128]{1,0:T(8,128)} %fusion.294.x_ref), custom_call_target="tpu_custom_call" | custom-call | tf_op jit(solution)/shard_map/pallas_call | solution.py:205
  186.5 1.3 fusion.319
  192.3 16.4 %shard_map.126 = f32[8,128]{1,0:T(8,128)} custom-call(f32[8,128]{1,0:T(8,128)} %pad_bitcast_fusion.x_ref), custom_call_target="tpu_custom_call" | custom-call | tf_op jit(solution)/shard_map/pallas_call | solution.py:205
  208.7 1.2 slice.469
  (123 shorter events, 21.9 us)
Async XLA Ops:
  22.1 2.3 %copy-start.21 = (s32[8,32,128]{2,1,0:T(8,128)S(1)}, s32[8,32,128]{2,1,0:T(8,128)}, u32[]{:S(2)}) copy-start(s32[8,32,128]{2,1,0:T(8,128)} %param.10) | copy-start | bytes 393220
  23.7 1.1 copy-start.14
  47.8 0.7 copy-start.25
  47.8 0.7 copy-start.26
  51.8 3.3 %copy-start.17 = (f32[20,48,128]{2,1,0:T(8,128)}, f32[20,48,128]{2,1,0:T(8,128)S(1)}, u32[]{:S(2)}) copy-start(f32[20,48,128]{2,1,0:T(8,128)S(1)} %get-tuple-element.38) | copy-start | bytes 1474564
  51.8 12.5 %copy-start.12 = (f32[20,48,128]{2,1,0:T(8,128)}, f32[20,48,128]{2,1,0:T(8,128)S(1)}, u32[]{:S(2)}) copy-start(f32[20,48,128]{2,1,0:T(8,128)S(1)} %get-tuple-element.39) | copy-start | bytes 1474564
  52.6 11.6 %copy-start = (f32[20,48,128]{2,1,0:T(8,128)}, f32[20,48,128]{2,1,0:T(8,128)S(1)}, u32[]{:S(2)}) copy-start(f32[20,48,128]{2,1,0:T(8,128)S(1)} %get-tuple-element.57) | copy-start | bytes 1474564
  52.7 11.6 %copy-start.2 = (f32[20,48,128]{2,1,0:T(8,128)}, f32[20,48,128]{2,1,0:T(8,128)S(1)}, u32[]{:S(2)}) copy-start(f32[20,48,128]{2,1,0:T(8,128)S(1)} %get-tuple-element.58) | copy-start | bytes 1474564
  52.7 11.6 %copy-start.4 = (f32[20,48,128]{2,1,0:T(8,128)}, f32[20,48,128]{2,1,0:T(8,128)S(1)}, u32[]{:S(2)}) copy-start(f32[20,48,128]{2,1,0:T(8,128)S(1)} %get-tuple-element.59) | copy-start | bytes 1474564
  52.7 11.6 %copy-start.6 = (f32[20,48,128]{2,1,0:T(8,128)}, f32[20,48,128]{2,1,0:T(8,128)S(1)}, u32[]{:S(2)}) copy-start(f32[20,48,128]{2,1,0:T(8,128)S(1)} %get-tuple-element.60) | copy-start | bytes 1474564
  52.7 11.6 %copy-start.8 = (f32[20,48,128]{2,1,0:T(8,128)}, f32[20,48,128]{2,1,0:T(8,128)S(1)}, u32[]{:S(2)}) copy-start(f32[20,48,128]{2,1,0:T(8,128)S(1)} %get-tuple-element.61) | copy-start | bytes 1474564
  52.7 13.4 %copy-start.10 = (f32[20,48,128]{2,1,0:T(8,128)}, f32[20,48,128]{2,1,0:T(8,128)S(1)}, u32[]{:S(2)}) copy-start(f32[20,48,128]{2,1,0:T(8,128)S(1)} %get-tuple-element.62) | copy-start | bytes 1474564
  66.1 1.0 copy-start.15
  67.2 1.1 copy-start.24
  127.4 1.0 copy-start.1
  127.4 1.2 copy-start.3
  127.4 1.3 copy-start.5
  127.4 1.5 copy-start.7
  127.4 1.6 copy-start.9
  127.5 1.7 copy-start.11
  127.5 1.9 copy-start.18
  129.3 2.5 %copy-start.13 = (f32[20,48,128]{2,1,0:T(8,128)S(1)}, f32[20,48,128]{2,1,0:T(8,128)}, u32[]{:S(2)}) copy-start(f32[20,48,128]{2,1,0:T(8,128)} %copy-done.12) | copy-start | bytes 1474564
  141.9 1.0 copy-start.16
  146.5 18.1 %copy-start.22 = (f32[8,32,16]{1,2,0:T(8,128)S(1)}, f32[8,32,16]{1,2,0:T(8,128)}, u32[]{:S(2)}) copy-start(f32[8,32,16]{1,2,0:T(8,128)} %param.17) | copy-start | bytes 49156
  146.5 18.2 %copy-start.19 = (f32[8,32,16]{1,2,0:T(8,128)S(1)}, f32[8,32,16]{1,2,0:T(8,128)}, u32[]{:S(2)}) copy-start(f32[8,32,16]{1,2,0:T(8,128)} %param.15) | copy-start | bytes 49156
  146.5 18.3 %copy-start.23 = (f32[8,32,16]{1,2,0:T(8,128)S(1)}, f32[8,32,16]{1,2,0:T(8,128)}, u32[]{:S(2)}) copy-start(f32[8,32,16]{1,2,0:T(8,128)} %param.18) | copy-start | bytes 49156
  146.6 18.4 %copy-start.20 = (f32[8,32,16]{1,2,0:T(8,128)S(1)}, f32[8,32,16]{1,2,0:T(8,128)}, u32[]{:S(2)}) copy-start(f32[8,32,16]{1,2,0:T(8,128)} %param.16) | copy-start | bytes 49156

commit v8 on v7

--- a/solution.py
+++ b/solution.py
@@ -147,25 +147,42 @@
     )(x)
 
 
-def _reduce_kernel(axes, x_ref, o_ref, *scratch):
-    stages = len(axes)
-    slots, sends, recvs = scratch[:stages], scratch[stages : 2 * stages], scratch[2 * stages : 3 * stages]
-    held = scratch[3 * stages :]
+def _group(axes):
+    sizes = [lax.axis_size(axis) for axis in axes]
+    n = 1
+    for size in sizes:
+        n *= size
+    me = 0
+    for axis, size in zip(axes, sizes):
+        me = me * size + lax.axis_index(axis)
+
+    def member(index):
+        ids = {}
+        for axis, size in reversed(list(zip(axes, sizes))):
+            ids[axis] = index % size
+            index = index // size
+        return ids
+
+    return n, me, member
+
+
+def _reduce_kernel(stages, x_ref, o_ref, *scratch):
+    count = len(stages)
+    slots, sends, recvs = scratch[:count], scratch[count : 2 * count], scratch[2 * count : 3 * count]
+    held = scratch[3 * count :]
     barrier = pltpu.get_barrier_semaphore()
     peers = 0
-    for axis in axes:
-        n = lax.axis_size(axis)
-        me = lax.axis_index(axis)
+    for axes in stages:
+        n, me, member = _group(axes)
         for k in range(1, n):
             pl.semaphore_signal(
-                barrier, inc=1, device_id={axis: lax.rem(me + k, n)}, device_id_type=MESH
+                barrier, inc=1, device_id=member(lax.rem(me + k, n)), device_id_type=MESH
             )
         peers += n - 1
     pl.semaphore_wait(barrier, peers)
     value = x_ref
-    for i, axis in enumerate(axes):
-        n = lax.axis_size(axis)
-        me = lax.axis_index(axis)
+    for i, axes in enumerate(stages):
+        n, me, member = _group(axes)
         copies = []
         for k in range(1, n):
             copy = pltpu.make_async_remote_copy(
@@ -173,7 +190,7 @@
                 dst_ref=slots[i].at[me],
                 send_sem=sends[i].at[k - 1],
                 recv_sem=recvs[i].at[k - 1],
-                device_id={axis: lax.rem(me + k, n)},
+                device_id=member(lax.rem(me + k, n)),
                 device_id_type=MESH,
             )
             copy.start()
@@ -184,18 +201,18 @@
         total = slots[i][0]
         for j in range(1, n):
             total = total + slots[i][j]
-        if i + 1 < stages:
+        if i + 1 < count:
             held[i][...] = total
             value = held[i]
         else:
             o_ref[...] = total
 
-
 def small_sum(values, axes, cid):
     count = values.shape[0]
     rows = -(-count // 1024) * 8
     packed = jnp.pad(values, (0, rows * 128 - count)).reshape(rows, 128)
-    sizes = [lax.axis_size(axis) for axis in axes]
+    stages = tuple(tuple(axis) if isinstance(axis, tuple) else (axis,) for axis in axes)
+    sizes = [_group(axis)[0] for axis in stages]
     scratch = (
         [pltpu.VMEM((n, rows, 128), jnp.float32) for n in sizes]
         + [pltpu.SemaphoreType.DMA((n - 1,)) for n in sizes]
@@ -203,7 +220,7 @@
         + [pltpu.VMEM((rows, 128), jnp.float32) for n in sizes[:-1]]
     )
     total = pl.pallas_call(
-        functools.partial(_reduce_kernel, tuple(axes)),
+        functools.partial(_reduce_kernel, stages),
         out_shape=jax.ShapeDtypeStruct((rows, 128), jnp.float32),
         in_specs=[pl.BlockSpec(memory_space=pltpu.VMEM)],
         out_specs=pl.BlockSpec(memory_space=pltpu.VMEM),
@@ -353,12 +370,9 @@
     held = (near_x >= 0) & (near_x < wx) & (near_y >= 0) & (near_y < wy)
     wide_hot = (jnp.arange(wx * wy)[:, None] == (near_x * wy + near_y)[None, :]) & held[None, :]
     wide_hot = wide_hot.astype(jnp.float32)
-    source_w = jnp.stack(
-        [
-            jnp.dot(wide_hot, weight[i][:, None] * depth_hot.T, precision=lax.Precision.HIGHEST)
-            for i in range(sources)
-        ]
-    ).reshape(sources, wx, wy, cz)
+    spread = (weight[:, :, None] * depth_hot.T[None]).transpose(1, 0, 2).reshape(det_cells.shape[0], -1)
+    source_w = jnp.dot(wide_hot, spread, precision=lax.Precision.HIGHEST).reshape(wx * wy, sources, cz)
+    source_w = source_w.transpose(1, 0, 2).reshape(sources, wx, wy, cz)
     dual_w = chebyshev(source_w, apply_op)
     ring = (slice(None), slice(width - 1, width + cx + 1), slice(width_y - 1, width_y + cy + 1))
     phi_near = beside(phi_w[ring])
@@ -377,11 +391,11 @@
     w_a = hv_a - beta_prev[0] * q_absorb
     local_wv = jnp.sum(w_k * v_kappa) + jnp.sum(w_a * v_absorb)
     local_vv = jnp.sum(v_kappa * v_kappa) + jnp.sum(v_absorb * v_absorb)
-    wv_sum, vv_sum = small_sum(jnp.stack([local_wv, local_vv]), ("gy", "gx", "src"), 4)
+    wv_sum, vv_sum = small_sum(jnp.stack([local_wv, local_vv]), (("gx", "gy"), "src"), 4)
     alpha = wv_sum / cell_count / (vv_sum / cell_count + eps_norm)
     r_k = w_k - alpha * v_kappa
     r_a = w_a - alpha * v_absorb
-    rr_sum = small_sum((jnp.sum(r_k * r_k) + jnp.sum(r_a * r_a))[None], ("gy", "gx", "src"), 7)[0]
+    rr_sum = small_sum((jnp.sum(r_k * r_k) + jnp.sum(r_a * r_a))[None], (("gx", "gy"), "src"), 7)[0]
     beta = jnp.sqrt(rr_sum / cell_count + eps_norm)
     return (r_k / beta, r_a / beta, jnp.stack([alpha, beta]))
 

time: 216 us -> 207 us (0.958); the launches traced: 213 us -> 206 us
  matrix products: 16.4 us -> 11.3 us
    dot_general x4 -> x1, matrix products: 8.55 us -> 3.48 us  [per_device(): jnp.dot(wide_hot, spread, precision=lax.Precision.HIGHEST)]
where the time goes in v8:
time: 207 us; the launch traced here: 206 us
  Pallas kernels  127 us (61%)
  other arithmetic  39.2 us (19%)
  local copies, waits for them, and re-layouts  20.2 us (10%)
  matrix products  11.3 us (5%)
  between operations  7.97 us (4%)
    pallas_call x3, Pallas kernels, small_sum(): pl.pallas_call(functools.partial(_reduce_kernel, stages), out_shape=jax.S...  72.8 us
    pallas_call x2, Pallas kernels, exchange(): pl.pallas_call(functools.partial(_exchange_kernel, axis, n, scatter), out...  31.6 us
    pallas_call x1, Pallas kernels, halo_block(): pl.pallas_call(functools.partial(_halo_kernel, hx, hy), out_shape=jax.Sha...  23 us
    add x8, other arithmetic, chebyshev(): step_dir = rho_next * rho * step_dir + 2.0 * rho_next / delta * remain  18.4 us
    unnamed x60, local copies, waits for them, and re-layouts  6.06 us
    dot_general x1, matrix products, per_device(): jnp.dot(both, depth_hot, precision=lax.Precision.HIGHEST)  5.58 us

profile of v8, /device:TPU:1, one launch (start us, length us, event | category | flops | bytes accessed | tf_op | source)
XLA Modules:
  0.0 206.1 jit_solution(12659604134602252893)
XLA Ops:
  2.5 16.7 %shard_map.121 = f32[8,64,128]{2,1,0:T(8,128)} custom-call(f32[64,128]{1,0:T(8,128)} %reshape.409.x_ref), custom_call_target="tpu_custom_call" | custom-call | tf_op jit(solution)/shard_map/pallas_call | solution.py:50
  19.2 1.7 reshape.410
  20.9 1.2 fusion.289
  22.1 1.6 copy.30
  24.8 23.0 %shard_map.122 = f32[7,20,48,128]{3,2,1,0:T(8,128)S(1)} custom-call(f32[7,8,32,128]{3,2,1,0:T(8,128)S(1)} %pad_maximum_fusion.1.x_ref), custom_call_target="tpu_custom_call" | custom-call | tf_op jit(solution)/shard_map/pallas_call | solution.py:133
  48.5 2.3 %fusion = f32[2,122880]{1,0:T(2,128)S(1)} fusion(f32[122880]{0:T(1024)S(1)} %bitcast.72, f32[1,16]{1,0:T(1,128)S(1)} %bitcast.75, f32[1,16]{1,0:T(1,128)S(1)} %bitcast.76), kind=kOutput, calls=%fused_computation.68 | convolution fusion | flops 49152032 | bytes 1474688 | tf_op jit(solution)/shard_map/dot_general | solution.py:332
  52.9 2.2 %broadcast_multiply_fusion.1 = (f32[4,20,48,128]{3,2,1,0:T(8,128)S(1)}, f32[4,20,48,128]{3,2,1,0:T(8,128)S(1)}) fusion(f32[4,20,48,128]{3,2,1,0:T(8,128)S(1)} %slice.349, f32[20,48,128]{2,1,0:T(8,128)S(1)} %get-tuple-element.75, f32[20,48,128]{2,1,0:T(8,128)S(1)} %get-tuple-element.79, f32[20,48,128]{2,1,0:T(8,128)S(1)} %get-tuple-element.78, ...), kind=kLoop, calls=%fused_computation.317 | loop fusion | flops 10321920 | bytes 9338880 | tf_op jit(solution)/shard_map/div | solution.py:286
  55.0 2.3 %multiply_add_fusion.7 = (f32[4,20,48,128]{3,2,1,0:T(8,128)S(1)}, f32[4,20,48,128]{3,2,1,0:T(8,128)S(1)}) fusion(f32[4,20,48,128]{3,2,1,0:T(8,128)S(1)} %get-tuple-element.41, f32[4,20,48,128]{3,2,1,0:T(8,128)S(1)} %get-tuple-element.40, f32[20,48,128]{2,1,0:T(8,128)S(1)} %get-tuple-element.62, f32[20,48,128]{2,1,0:T(8,128)S(1)} %get-tuple-element.58, ...), kind=kLoop, calls=%fused_computation.303 | loop fusion | flops 11304960 | bytes 11304960 | tf_op jit(solution)/shard_map/add | solution.py:292
  57.4 2.3 %multiply_add_fusion.6 = (f32[4,20,48,128]{3,2,1,0:T(8,128)S(1)}, f32[4,20,48,128]{3,2,1,0:T(8,128)S(1)}) fusion(f32[4,20,48,128]{3,2,1,0:T(8,128)S(1)} %get-tuple-element.36, f32[4,20,48,128]{3,2,1,0:T(8,128)S(1)} %get-tuple-element.37, f32[20,48,128]{2,1,0:T(8,128)S(1)} %get-tuple-element.62, f32[20,48,128]{2,1,0:T(8,128)S(1)} %get-tuple-element.58, ...), kind=kLoop, calls=%fused_computation.302 | loop fusion | flops 11304960 | bytes 11304960 | tf_op jit(solution)/shard_map/add | solution.py:292
  59.7 2.3 %multiply_add_fusion.5 = (f32[4,20,48,128]{3,2,1,0:T(8,128)S(1)}, f32[4,20,48,128]{3,2,1,0:T(8,128)S(1)}) fusion(f32[4,20,48,128]{3,2,1,0:T(8,128)S(1)} %get-tuple-element.34, f32[4,20,48,128]{3,2,1,0:T(8,128)S(1)} %get-tuple-element.35, f32[20,48,128]{2,1,0:T(8,128)S(1)} %get-tuple-element.62, f32[20,48,128]{2,1,0:T(8,128)S(1)} %get-tuple-element.58, ...), kind=kLoop, calls=%fused_computation.301 | loop fusion | flops 11304960 | bytes 11304960 | tf_op jit(solution)/shard_map/add | solution.py:292
  61.9 2.3 %multiply_add_fusion.4 = (f32[4,20,48,128]{3,2,1,0:T(8,128)S(1)}, f32[4,20,48,128]{3,2,1,0:T(8,128)S(1)}) fusion(f32[4,20,48,128]{3,2,1,0:T(8,128)S(1)} %get-tuple-element.32, f32[4,20,48,128]{3,2,1,0:T(8,128)S(1)} %get-tuple-element.33, f32[20,48,128]{2,1,0:T(8,128)S(1)} %get-tuple-element.62, f32[20,48,128]{2,1,0:T(8,128)S(1)} %get-tuple-element.58, ...), kind=kLoop, calls=%fused_computation.300 | loop fusion | flops 11304960 | bytes 11304960 | tf_op jit(solution)/shard_map/add | solution.py:292
  64.3 1.8 fusion.108
  67.2 1.1 pad_maximum_fusion
  68.5 5.6 %select_reduce_fusion = f32[8,1024]{1,0:T(8,128)S(1)} fusion(pred[256,1024]{1,0:T(8,128)(4,1)S(1)} %fusion.220, f32[8,256,128]{2,1,0:T(8,128)} %bitcast.69, s32[1024]{0:T(1024)S(1)} %get-tuple-element.86), kind=kOutput, calls=%fused_computation.66 | convolution fusion | flops 3225542656 | bytes 1347584 | tf_op jit(solution)/shard_map/dot_general | solution.py:359
  74.7 41.1 %shard_map.123 = f32[64,128]{1,0:T(8,128)} custom-call(f32[64,128]{1,0:T(8,128)} %reshape.411.x_ref), custom_call_target="tpu_custom_call" | custom-call | tf_op jit(solution)/shard_map/pallas_call | solution.py:222
  117.6 0.9 multiply_reduce_fusion.7
  118.9 3.5 %fusion.4 = f32[960,4,128]{2,0,1:T(8,128)S(1)} fusion(s32[1024]{0:T(1024)S(1)} %get-tuple-element.87, pred[1024]{0:T(1024)(128)(4,1)S(1)} %get-tuple-element.84, f32[1024,128]{0,1:T(8,128)S(1)} %fusion.244, f32[1024,4]{0,1:T(4,128)S(1)} %divide_bitcast_fusion), kind=kOutput, calls=%fused_computation.73 | convolution fusion | flops 6042288128 | bytes 2511872 | tf_op jit(solution)/shard_map/dot_general | solution.py:374
  124.3 2.2 %multiply_add_fusion.3 = (f32[4,20,48,128]{3,2,1,0:T(8,128)S(1)}, f32[4,20,48,128]{3,2,1,0:T(8,128)S(1)}) fusion(f32[4,20,48,128]{3,2,1,0:T(8,128)S(1)} %bitcast.60, f32[4,20,48,128]{3,2,1,0:T(8,128)S(1)} %broadcast_multiply_fusion, f32[20,48,128]{2,1,0:T(8,128)S(1)} %copy-done.11, f32[20,48,128]{2,1,0:T(8,128)S(1)} %copy-done.3, ...), kind=kLoop, calls=%fused_computation.299 | loop fusion | flops 11304960 | bytes 11304960 | tf_op jit(solution)/shard_map/add | solution.py:292
  126.6 2.3 %multiply_add_fusion.2 = (f32[4,20,48,128]{3,2,1,0:T(8,128)S(1)}, f32[4,20,48,128]{3,2,1,0:T(8,128)S(1)}) fusion(f32[4,20,48,128]{3,2,1,0:T(8,128)S(1)} %get-tuple-element.28, f32[4,20,48,128]{3,2,1,0:T(8,128)S(1)} %get-tuple-element.29, f32[20,48,128]{2,1,0:T(8,128)S(1)} %copy-done.11, f32[20,48,128]{2,1,0:T(8,128)S(1)} %copy-done.3, ...), kind=kLoop, calls=%fused_computation.298 | loop fusion | flops 11304960 | bytes 11304960 | tf_op jit(solution)/shard_map/add | solution.py:292
  128.9 2.3 %multiply_add_fusion.1 = (f32[4,20,48,128]{3,2,1,0:T(8,128)S(1)}, f32[4,20,48,128]{3,2,1,0:T(8,128)S(1)}) fusion(f32[4,20,48,128]{3,2,1,0:T(8,128)S(1)} %get-tuple-element.26, f32[4,20,48,128]{3,2,1,0:T(8,128)S(1)} %get-tuple-element.27, f32[20,48,128]{2,1,0:T(8,128)S(1)} %copy-done.11, f32[20,48,128]{2,1,0:T(8,128)S(1)} %copy-done.3, ...), kind=kLoop, calls=%fused_computation.297 | loop fusion | flops 11304960 | bytes 11304960 | tf_op jit(solution)/shard_map/add | solution.py:292
  131.3 2.3 %multiply_add_fusion = (f32[4,20,48,128]{3,2,1,0:T(8,128)S(1)}, f32[4,20,48,128]{3,2,1,0:T(8,128)S(1)}) fusion(f32[4,20,48,128]{3,2,1,0:T(8,128)S(1)} %get-tuple-element.24, f32[4,20,48,128]{3,2,1,0:T(8,128)S(1)} %get-tuple-element.25, f32[20,48,128]{2,1,0:T(8,128)S(1)} %copy-done.11, f32[20,48,128]{2,1,0:T(8,128)S(1)} %copy-done.3, ...), kind=kLoop, calls=%fused_computation.296 | loop fusion | flops 11304960 | bytes 11304960 | tf_op jit(solution)/shard_map/add | solution.py:292
  133.6 3.3 %fusion.205 = f32[4,20,48,128]{3,2,1,0:T(8,128)S(1)} fusion(f32[4,20,48,128]{3,2,1,0:T(8,128)S(1)} %get-tuple-element.23, f32[4,20,48,128]{3,2,1,0:T(8,128)S(1)} %get-tuple-element.22, f32[4,20,48,128]{3,2,1,0:T(8,128)S(1)} %get-tuple-element.24, f32[4,20,48,128]{3,2,1,0:T(8,128)S(1)} %get-tuple-element.26, f32[4,20,48,128]{3,2,1,0:T(8,128)S(1)} %get-tuple-element.28, ...), kind=kLoop, calls=%fused_computation.285 | loop fusion | flops 14254080 | bytes 17203200 | tf_op jit(solution)/shard_map/add | solution.py:288
  137.1 0.9 copy-done.16
  138.0 1.4 fusion.223
  139.7 0.9 neg.18
  141.6 1.3 reshape.413.x_ref
  142.8 15.0 %shard_map.124 = f32[8,64,128]{2,1,0:T(8,128)} custom-call(f32[8,64,128]{2,1,0:T(8,128)} %reshape.413.x_ref), custom_call_target="tpu_custom_call" | custom-call | tf_op jit(solution)/shard_map/pallas_call | solution.py:50
  157.8 1.0 reduce_sum.200
  164.6 17.2 %shard_map.125 = f32[8,128]{1,0:T(8,128)} custom-call(f32[8,128]{1,0:T(8,128)} %fusion.272.x_ref), custom_call_target="tpu_custom_call" | custom-call | tf_op jit(solution)/shard_map/pallas_call | solution.py:222
  181.8 1.3 fusion.292
  187.7 14.5 %shard_map.126 = f32[8,128]{1,0:T(8,128)} custom-call(f32[8,128]{1,0:T(8,128)} %pad_bitcast_fusion.x_ref), custom_call_target="tpu_custom_call" | custom-call | tf_op jit(solution)/shard_map/pallas_call | solution.py:222
  202.2 1.2 slice.453
  (120 shorter events, 19.2 us)
Async XLA Ops:
  22.1 2.3 %copy-start.21 = (s32[8,32,128]{2,1,0:T(8,128)S(1)}, s32[8,32,128]{2,1,0:T(8,128)}, u32[]{:S(2)}) copy-start(s32[8,32,128]{2,1,0:T(8,128)} %param.10) | copy-start | bytes 393220
  23.7 1.1 copy-start.14
  47.8 0.7 copy-start.25
  47.8 0.7 copy-start.26
  51.8 3.3 %copy-start.17 = (f32[20,48,128]{2,1,0:T(8,128)}, f32[20,48,128]{2,1,0:T(8,128)S(1)}, u32[]{:S(2)}) copy-start(f32[20,48,128]{2,1,0:T(8,128)S(1)} %get-tuple-element.38) | copy-start | bytes 1474564
  51.8 12.5 %copy-start.12 = (f32[20,48,128]{2,1,0:T(8,128)}, f32[20,48,128]{2,1,0:T(8,128)S(1)}, u32[]{:S(2)}) copy-start(f32[20,48,128]{2,1,0:T(8,128)S(1)} %get-tuple-element.39) | copy-start | bytes 1474564
  52.6 11.6 %copy-start = (f32[20,48,128]{2,1,0:T(8,128)}, f32[20,48,128]{2,1,0:T(8,128)S(1)}, u32[]{:S(2)}) copy-start(f32[20,48,128]{2,1,0:T(8,128)S(1)} %get-tuple-element.57) | copy-start | bytes 1474564
  52.7 11.6 %copy-start.2 = (f32[20,48,128]{2,1,0:T(8,128)}, f32[20,48,128]{2,1,0:T(8,128)S(1)}, u32[]{:S(2)}) copy-start(f32[20,48,128]{2,1,0:T(8,128)S(1)} %get-tuple-element.58) | copy-start | bytes 1474564
  52.7 11.6 %copy-start.4 = (f32[20,48,128]{2,1,0:T(8,128)}, f32[20,48,128]{2,1,0:T(8,128)S(1)}, u32[]{:S(2)}) copy-start(f32[20,48,128]{2,1,0:T(8,128)S(1)} %get-tuple-element.59) | copy-start | bytes 1474564
  52.7 11.6 %copy-start.6 = (f32[20,48,128]{2,1,0:T(8,128)}, f32[20,48,128]{2,1,0:T(8,128)S(1)}, u32[]{:S(2)}) copy-start(f32[20,48,128]{2,1,0:T(8,128)S(1)} %get-tuple-element.60) | copy-start | bytes 1474564
  52.7 11.6 %copy-start.8 = (f32[20,48,128]{2,1,0:T(8,128)}, f32[20,48,128]{2,1,0:T(8,128)S(1)}, u32[]{:S(2)}) copy-start(f32[20,48,128]{2,1,0:T(8,128)S(1)} %get-tuple-element.61) | copy-start | bytes 1474564
  52.7 13.4 %copy-start.10 = (f32[20,48,128]{2,1,0:T(8,128)}, f32[20,48,128]{2,1,0:T(8,128)S(1)}, u32[]{:S(2)}) copy-start(f32[20,48,128]{2,1,0:T(8,128)S(1)} %get-tuple-element.62) | copy-start | bytes 1474564
  66.1 1.0 copy-start.15
  67.2 1.1 copy-start.24
  122.4 1.0 copy-start.1
  122.4 1.2 copy-start.3
  122.4 1.3 copy-start.5
  122.4 1.5 copy-start.7
  122.4 1.6 copy-start.9
  122.4 1.7 copy-start.11
  122.5 1.9 copy-start.18
  124.3 2.3 %copy-start.13 = (f32[20,48,128]{2,1,0:T(8,128)S(1)}, f32[20,48,128]{2,1,0:T(8,128)}, u32[]{:S(2)}) copy-start(f32[20,48,128]{2,1,0:T(8,128)} %copy-done.12) | copy-start | bytes 1474564
  136.9 1.0 copy-start.16
  141.5 18.1 %copy-start.22 = (f32[8,32,16]{1,2,0:T(8,128)S(1)}, f32[8,32,16]{1,2,0:T(8,128)}, u32[]{:S(2)}) copy-start(f32[8,32,16]{1,2,0:T(8,128)} %param.17) | copy-start | bytes 49156
  141.6 18.2 %copy-start.19 = (f32[8,32,16]{1,2,0:T(8,128)S(1)}, f32[8,32,16]{1,2,0:T(8,128)}, u32[]{:S(2)}) copy-start(f32[8,32,16]{1,2,0:T(8,128)} %param.15) | copy-start | bytes 49156
  141.6 18.3 %copy-start.23 = (f32[8,32,16]{1,2,0:T(8,128)S(1)}, f32[8,32,16]{1,2,0:T(8,128)}, u32[]{:S(2)}) copy-start(f32[8,32,16]{1,2,0:T(8,128)} %param.18) | copy-start | bytes 49156
  141.6 18.4 %copy-start.20 = (f32[8,32,16]{1,2,0:T(8,128)S(1)}, f32[8,32,16]{1,2,0:T(8,128)}, u32[]{:S(2)}) copy-start(f32[8,32,16]{1,2,0:T(8,128)} %param.16) | copy-start | bytes 49156

commit v9 on v8

--- a/solution.py
+++ b/solution.py
@@ -62,7 +62,12 @@
     )(x)
 
 
-def _halo_kernel(hx, hy, x_ref, o_ref, wide, send_sem, recv_sem, local_sem):
+def _halo_kernel(hx, hy, gather, *refs):
+    if gather:
+        x_ref, g_ref, o_ref, go_ref, wide, send_sem, recv_sem, local_sem = refs[:8]
+        g_slots, g_send, g_recv, g_local = refs[8:]
+    else:
+        x_ref, o_ref, wide, send_sem, recv_sem, local_sem = refs
     fields, cx, cy, cz = x_ref.shape
     ax, ay = lax.axis_index("gx"), lax.axis_index("gy")
     nx, ny = lax.axis_size("gx"), lax.axis_size("gy")
@@ -88,7 +93,30 @@
             )
     across = 1 + (ax + nx - 1) // nx + (2 * nx - 2 - ax) // nx
     along = 1 + (ay + ny - 1) // ny + (2 * ny - 2 - ay) // ny
-    pl.semaphore_wait(barrier, across * along - 1)
+    if gather:
+        n = lax.axis_size("src")
+        me = lax.axis_index("src")
+        for k in range(1, n):
+            pl.semaphore_signal(
+                barrier, inc=1, device_id={"src": lax.rem(me + k, n)}, device_id_type=MESH
+            )
+        pl.semaphore_wait(barrier, across * along - 1 + n - 1)
+        pulls = []
+        for k in range(1, n):
+            pull = pltpu.make_async_remote_copy(
+                src_ref=g_ref,
+                dst_ref=g_slots.at[me],
+                send_sem=g_send.at[k - 1],
+                recv_sem=g_recv.at[k - 1],
+                device_id={"src": lax.rem(me + k, n)},
+                device_id_type=MESH,
+            )
+            pull.start()
+            pulls.append(pull)
+        own = pltpu.make_async_copy(g_ref, g_slots.at[me], g_local)
+        own.start()
+    else:
+        pl.semaphore_wait(barrier, across * along - 1)
 
     local = pltpu.make_async_copy(
         x_ref, wide.at[:, pl.ds(hx, cx), pl.ds(hy, cy), :], local_sem
@@ -124,27 +152,49 @@
         def _():
             copy.wait_recv()
 
+    if gather:
+        own.wait()
+        for pull in pulls:
+            pull.wait()
+        go_ref[...] = g_slots[...]
     o_ref[...] = wide[...]
 
 
-def halo_block(x, hx, hy, cid):
+def halo_block(x, hx, hy, cid, gather=None):
     fields, cx, cy, cz = x.shape
     shape = (fields, cx + 2 * hx, cy + 2 * hy, cz)
+    vmem = pl.BlockSpec(memory_space=pltpu.VMEM)
+    scratch = [
+        pltpu.VMEM(shape, x.dtype),
+        pltpu.SemaphoreType.DMA((8,)),
+        pltpu.SemaphoreType.DMA((8,)),
+        pltpu.SemaphoreType.DMA,
+    ]
+    operands = (x,)
+    out_shape = jax.ShapeDtypeStruct(shape, x.dtype)
+    out_specs = vmem
+    if gather is not None:
+        n = lax.axis_size("src")
+        slots = (n,) + gather.shape
+        scratch += [
+            pltpu.VMEM(slots, gather.dtype),
+            pltpu.SemaphoreType.DMA((n - 1,)),
+            pltpu.SemaphoreType.DMA((n - 1,)),
+            pltpu.SemaphoreType.DMA,
+        ]
+        operands = (x, gather)
+        out_shape = (out_shape, jax.ShapeDtypeStruct(slots, gather.dtype))
+        out_specs = (vmem, vmem)
     return pl.pallas_call(
-        functools.partial(_halo_kernel, hx, hy),
-        out_shape=jax.ShapeDtypeStruct(shape, x.dtype),
-        in_specs=[pl.BlockSpec(memory_space=pltpu.VMEM)],
-        out_specs=pl.BlockSpec(memory_space=pltpu.VMEM),
-        scratch_shapes=[
-            pltpu.VMEM(shape, x.dtype),
-            pltpu.SemaphoreType.DMA((8,)),
-            pltpu.SemaphoreType.DMA((8,)),
-            pltpu.SemaphoreType.DMA,
-        ],
+        functools.partial(_halo_kernel, hx, hy, gather is not None),
+        out_shape=out_shape,
+        in_specs=[vmem] * len(operands),
+        out_specs=out_specs,
+        scratch_shapes=scratch,
         compiler_params=pltpu.CompilerParams(
             collective_id=cid, has_side_effects=True, vmem_limit_bytes=48 * 1024 * 1024
         ),
-    )(x)
+    )(*operands)
 
 
 def _group(axes):
@@ -310,14 +360,15 @@
     n_src = lax.axis_size("src")
     slab = v_kappa.shape[2]
     pair = jnp.stack([v_kappa, v_absorb]).reshape(-1, 128)
-    gathered = exchange(pair, "src", 0).reshape((n_src, 2, cx, cy, slab))
-    full_k, full_a = jnp.transpose(gathered, (1, 2, 3, 0, 4)).reshape(2, cx, cy, cz)
     width = ITERS
     width_y = 8
     region_of = labels.astype(jnp.float32)[None]
-    stacked = jnp.concatenate([background, region_of, full_k[None], full_a[None]], axis=0)
-    wide = halo_block(stacked, width, width_y, 10)
-    phi_w, region_w, vk_w, va_w = wide[:sources], wide[sources], wide[sources + 1], wide[sources + 2]
+    stacked = jnp.concatenate([background, region_of], axis=0)
+    wide, gathered = halo_block(stacked, width, width_y, 10, gather=pair)
+    gathered = gathered.reshape((n_src, 2, cx, cy, slab))
+    full_k, full_a = jnp.transpose(gathered, (1, 2, 3, 0, 4)).reshape(2, cx, cy, cz)
+    wide_v = halo_block(jnp.stack([full_k, full_a]), width, width_y, 11)
+    phi_w, region_w, vk_w, va_w = wide[:sources], wide[sources], wide_v[0], wide_v[1]
     wx = cx + 2 * width
     wy = cy + 2 * width_y
     gx_at = lax.axis_index("gx") * cx - width + jnp.arange(wx)

time: 207 us -> 211 us (1.019)
  local copies, waits for them, and re-layouts: 20.2 us -> 24.5 us
  other arithmetic: 39.2 us -> 41.5 us
    pallas_call x1 -> x2, Pallas kernels: 23 us -> 55.1 us  [halo_block(): pl.pallas_call(functools.partial(_halo_kernel, hx, hy, gather is not None...]
    pallas_call x3, Pallas kernels: 72.8 us -> 53 us  [small_sum(): pl.pallas_call(functools.partial(_reduce_kernel, stages), out_shape=jax.S...]
    pallas_call x2 -> x1, Pallas kernels: 31.6 us -> 16.7 us  [exchange(): pl.pallas_call(functools.partial(_exchange_kernel, axis, n, scatter), out...]
    another operation x5, local copies, waits for them, and re-layouts: 3.49 us -> 9.32 us  [per_device(): full_k, full_a = jnp.transpose(gathered, (1, 2, 3, 0, 4)).reshape(2, cx,...]
    unnamed x60 -> x50, local copies, waits for them, and re-layouts: 6.06 us -> 4.9 us
where the time goes in v9:
time: 211 us; the launch traced here: 210 us
  Pallas kernels  125 us (59%)
  other arithmetic  41.5 us (20%)
  local copies, waits for them, and re-layouts  24.5 us (12%)
  matrix products  11.3 us (5%)
  between operations  7.94 us (4%)
    pallas_call x2, Pallas kernels, halo_block(): pl.pallas_call(functools.partial(_halo_kernel, hx, hy, gather is not None...  55.1 us
    pallas_call x3, Pallas kernels, small_sum(): pl.pallas_call(functools.partial(_reduce_kernel, stages), out_shape=jax.S...  53 us
    add x8, other arithmetic, chebyshev(): step_dir = rho_next * rho * step_dir + 2.0 * rho_next / delta * remain  18.3 us
    pallas_call x1, Pallas kernels, exchange(): pl.pallas_call(functools.partial(_exchange_kernel, axis, n, scatter), out...  16.7 us
    another operation x5, local copies, waits for them, and re-layouts, per_device(): full_k, full_a = jnp.transpose(gathered, (1, 2, 3, 0, 4)).reshape(2, cx,...  9.32 us
    dot_general x1, matrix products, per_device(): jnp.dot(both, depth_hot, precision=lax.Precision.HIGHEST)  5.58 us
    unnamed x50, local copies, waits for them, and re-layouts  4.9 us

profile of v9, /device:TPU:1, one launch (start us, length us, event | category | flops | bytes accessed | tf_op | source)
XLA Modules:
  0.0 210.2 jit_solution(17606108224309360706)
XLA Ops:
  1.7 1.1 pad_maximum_fusion.1.refs_0_
  3.9 28.2 %shard_map.121 = (f32[5,20,48,128]{3,2,1,0:T(8,128)S(1)}, f32[8,64,128]{2,1,0:T(8,128)S(1)}) custom-call(f32[5,8,32,128]{3,2,1,0:T(8,128)S(1)} %pad_maximum_fusion.1.refs_0_, f32[64,128]{1,0:T(8,128)S(1)} %reshape.409.refs_1_), custom_call_target="tpu_custom_call" | custom-call | tf_op jit(solution)/shard_map/pallas_call | solution.py:188
  32.3 2.3 %fusion = f32[2,122880]{1,0:T(2,128)S(1)} fusion(f32[122880]{0:T(1024)S(1)} %bitcast.72, f32[1,16]{1,0:T(1,128)S(1)} %bitcast.75, f32[1,16]{1,0:T(1,128)S(1)} %bitcast.76), kind=kOutput, calls=%fused_computation.68 | convolution fusion | flops 49152032 | bytes 1474688 | tf_op jit(solution)/shard_map/dot_general | solution.py:383
  35.3 1.3 broadcast_multiply_fusion.2
  36.7 1.9 reshape.410
  38.6 2.8 %fusion.288 = (f32[1,8,32,8,16]{4,2,1,0,3:T(8,128)}, f32[1,8,32,8,16]{4,2,1,0,3:T(8,128)S(1)}) fusion(f32[2,8,32,8,16]{4,2,1,0,3:T(8,128)} %bitcast.62), kind=kLoop, calls=%fused_computation.439 | loop fusion | bytes 524288 | tf_op jit(solution)/shard_map/unstack | solution.py:369
  41.4 2.3 %copy.30 = f32[1,8,32,8,16]{2,4,3,1,0:T(8,128)} copy(f32[1,8,32,8,16]{4,2,1,0,3:T(8,128)} %get-tuple-element.51) | data formatting | bytes 262144 | tf_op jit(solution)/shard_map/unstack | solution.py:369
  43.8 1.9 copy.32
  45.6 1.1 copy.31
  46.8 1.2 copy.33
  49.0 26.9 %shard_map.122 = f32[2,20,48,128]{3,2,1,0:T(8,128)S(1)} custom-call(f32[2,8,32,128]{3,2,1,0:T(8,128)S(1)} %pad_maximum_fusion.2.refs_0_), custom_call_target="tpu_custom_call" | custom-call | tf_op jit(solution)/shard_map/pallas_call | solution.py:188
  76.9 2.2 %broadcast_multiply_fusion.1 = (f32[4,20,48,128]{3,2,1,0:T(8,128)S(1)}, f32[4,20,48,128]{3,2,1,0:T(8,128)S(1)}) fusion(f32[4,20,48,128]{3,2,1,0:T(8,128)S(1)} %slice.349, f32[20,48,128]{2,1,0:T(8,128)S(1)} %get-tuple-element.78, f32[20,48,128]{2,1,0:T(8,128)S(1)} %get-tuple-element.82, f32[20,48,128]{2,1,0:T(8,128)S(1)} %get-tuple-element.81, ...), kind=kLoop, calls=%fused_computation.317 | loop fusion | flops 10321920 | bytes 9338880 | tf_op jit(solution)/shard_map/div | solution.py:336
  79.1 2.3 %multiply_add_fusion.7 = (f32[4,20,48,128]{3,2,1,0:T(8,128)S(1)}, f32[4,20,48,128]{3,2,1,0:T(8,128)S(1)}) fusion(f32[4,20,48,128]{3,2,1,0:T(8,128)S(1)} %get-tuple-element.45, f32[4,20,48,128]{3,2,1,0:T(8,128)S(1)} %get-tuple-element.44, f32[20,48,128]{2,1,0:T(8,128)S(1)} %get-tuple-element.65, f32[20,48,128]{2,1,0:T(8,128)S(1)} %get-tuple-element.61, ...), kind=kLoop, calls=%fused_computation.303 | loop fusion | flops 11304960 | bytes 11304960 | tf_op jit(solution)/shard_map/add | solution.py:342
  81.4 2.3 %multiply_add_fusion.6 = (f32[4,20,48,128]{3,2,1,0:T(8,128)S(1)}, f32[4,20,48,128]{3,2,1,0:T(8,128)S(1)}) fusion(f32[4,20,48,128]{3,2,1,0:T(8,128)S(1)} %get-tuple-element.40, f32[4,20,48,128]{3,2,1,0:T(8,128)S(1)} %get-tuple-element.41, f32[20,48,128]{2,1,0:T(8,128)S(1)} %get-tuple-element.65, f32[20,48,128]{2,1,0:T(8,128)S(1)} %get-tuple-element.61, ...), kind=kLoop, calls=%fused_computation.302 | loop fusion | flops 11304960 | bytes 11304960 | tf_op jit(solution)/shard_map/add | solution.py:342
  83.7 2.3 %multiply_add_fusion.5 = (f32[4,20,48,128]{3,2,1,0:T(8,128)S(1)}, f32[4,20,48,128]{3,2,1,0:T(8,128)S(1)}) fusion(f32[4,20,48,128]{3,2,1,0:T(8,128)S(1)} %get-tuple-element.38, f32[4,20,48,128]{3,2,1,0:T(8,128)S(1)} %get-tuple-element.39, f32[20,48,128]{2,1,0:T(8,128)S(1)} %get-tuple-element.65, f32[20,48,128]{2,1,0:T(8,128)S(1)} %get-tuple-element.61, ...), kind=kLoop, calls=%fused_computation.301 | loop fusion | flops 11304960 | bytes 11304960 | tf_op jit(solution)/shard_map/add | solution.py:342
  86.0 2.3 %multiply_add_fusion.4 = (f32[4,20,48,128]{3,2,1,0:T(8,128)S(1)}, f32[4,20,48,128]{3,2,1,0:T(8,128)S(1)}) fusion(f32[4,20,48,128]{3,2,1,0:T(8,128)S(1)} %get-tuple-element.36, f32[4,20,48,128]{3,2,1,0:T(8,128)S(1)} %get-tuple-element.37, f32[20,48,128]{2,1,0:T(8,128)S(1)} %get-tuple-element.65, f32[20,48,128]{2,1,0:T(8,128)S(1)} %get-tuple-element.61, ...), kind=kLoop, calls=%fused_computation.300 | loop fusion | flops 11304960 | bytes 11304960 | tf_op jit(solution)/shard_map/add | solution.py:342
  88.3 1.8 fusion.108
  91.1 1.1 pad_maximum_fusion
  92.5 5.6 %select_reduce_fusion = f32[8,1024]{1,0:T(8,128)S(1)} fusion(pred[256,1024]{1,0:T(8,128)(4,1)S(1)} %fusion.220, f32[8,256,128]{2,1,0:T(8,128)} %bitcast.69, s32[1024]{0:T(1024)S(1)} %get-tuple-element.89), kind=kOutput, calls=%fused_computation.66 | convolution fusion | flops 3225542656 | bytes 1347584 | tf_op jit(solution)/shard_map/dot_general | solution.py:410
  98.7 21.4 %shard_map.123 = f32[64,128]{1,0:T(8,128)} custom-call(f32[64,128]{1,0:T(8,128)} %reshape.411.x_ref), custom_call_target="tpu_custom_call" | custom-call | tf_op jit(solution)/shard_map/pallas_call | solution.py:272
  123.1 3.5 %fusion.4 = f32[960,4,128]{2,0,1:T(8,128)S(1)} fusion(s32[1024]{0:T(1024)S(1)} %get-tuple-element.90, pred[1024]{0:T(1024)(128)(4,1)S(1)} %get-tuple-element.87, f32[1024,128]{0,1:T(8,128)S(1)} %fusion.244, f32[1024,4]{0,1:T(4,128)S(1)} %divide_bitcast_fusion), kind=kOutput, calls=%fused_computation.73 | convolution fusion | flops 6042288128 | bytes 2511872 | tf_op jit(solution)/shard_map/dot_general | solution.py:425
  128.2 2.2 %multiply_add_fusion.3 = (f32[4,20,48,128]{3,2,1,0:T(8,128)S(1)}, f32[4,20,48,128]{3,2,1,0:T(8,128)S(1)}) fusion(f32[4,20,48,128]{3,2,1,0:T(8,128)S(1)} %bitcast.60, f32[4,20,48,128]{3,2,1,0:T(8,128)S(1)} %broadcast_multiply_fusion, f32[20,48,128]{2,1,0:T(8,128)S(1)} %copy-done.7, f32[20,48,128]{2,1,0:T(8,128)S(1)} %get-tuple-element.61, ...), kind=kLoop, calls=%fused_computation.299 | loop fusion | flops 11304960 | bytes 11304960 | tf_op jit(solution)/shard_map/add | solution.py:342
  130.5 2.3 %multiply_add_fusion.2 = (f32[4,20,48,128]{3,2,1,0:T(8,128)S(1)}, f32[4,20,48,128]{3,2,1,0:T(8,128)S(1)}) fusion(f32[4,20,48,128]{3,2,1,0:T(8,128)S(1)} %get-tuple-element.32, f32[4,20,48,128]{3,2,1,0:T(8,128)S(1)} %get-tuple-element.33, f32[20,48,128]{2,1,0:T(8,128)S(1)} %copy-done.7, f32[20,48,128]{2,1,0:T(8,128)S(1)} %get-tuple-element.61, ...), kind=kLoop, calls=%fused_computation.298 | loop fusion | flops 11304960 | bytes 11304960 | tf_op jit(solution)/shard_map/add | solution.py:342
  132.8 2.3 %multiply_add_fusion.1 = (f32[4,20,48,128]{3,2,1,0:T(8,128)S(1)}, f32[4,20,48,128]{3,2,1,0:T(8,128)S(1)}) fusion(f32[4,20,48,128]{3,2,1,0:T(8,128)S(1)} %get-tuple-element.30, f32[4,20,48,128]{3,2,1,0:T(8,128)S(1)} %get-tuple-element.31, f32[20,48,128]{2,1,0:T(8,128)S(1)} %copy-done.7, f32[20,48,128]{2,1,0:T(8,128)S(1)} %get-tuple-element.61, ...), kind=kLoop, calls=%fused_computation.297 | loop fusion | flops 11304960 | bytes 11304960 | tf_op jit(solution)/shard_map/add | solution.py:342
  135.2 2.3 %multiply_add_fusion = (f32[4,20,48,128]{3,2,1,0:T(8,128)S(1)}, f32[4,20,48,128]{3,2,1,0:T(8,128)S(1)}) fusion(f32[4,20,48,128]{3,2,1,0:T(8,128)S(1)} %get-tuple-element.28, f32[4,20,48,128]{3,2,1,0:T(8,128)S(1)} %get-tuple-element.29, f32[20,48,128]{2,1,0:T(8,128)S(1)} %copy-done.7, f32[20,48,128]{2,1,0:T(8,128)S(1)} %get-tuple-element.61, ...), kind=kLoop, calls=%fused_computation.296 | loop fusion | flops 11304960 | bytes 11304960 | tf_op jit(solution)/shard_map/add | solution.py:342
  137.5 3.3 %fusion.205 = f32[4,20,48,128]{3,2,1,0:T(8,128)S(1)} fusion(f32[4,20,48,128]{3,2,1,0:T(8,128)S(1)} %get-tuple-element.27, f32[4,20,48,128]{3,2,1,0:T(8,128)S(1)} %get-tuple-element.26, f32[4,20,48,128]{3,2,1,0:T(8,128)S(1)} %get-tuple-element.28, f32[4,20,48,128]{3,2,1,0:T(8,128)S(1)} %get-tuple-element.30, f32[4,20,48,128]{3,2,1,0:T(8,128)S(1)} %get-tuple-element.32, ...), kind=kLoop, calls=%fused_computation.285 | loop fusion | flops 14254080 | bytes 17203200 | tf_op jit(solution)/shard_map/add | solution.py:338
  143.9 1.3 reshape.413.x_ref
  145.2 16.7 %shard_map.124 = f32[8,64,128]{2,1,0:T(8,128)} custom-call(f32[8,64,128]{2,1,0:T(8,128)} %reshape.413.x_ref), custom_call_target="tpu_custom_call" | custom-call | tf_op jit(solution)/shard_map/pallas_call | solution.py:50
  168.7 15.7 %shard_map.125 = f32[8,128]{1,0:T(8,128)} custom-call(f32[8,128]{1,0:T(8,128)} %fusion.272.x_ref), custom_call_target="tpu_custom_call" | custom-call | tf_op jit(solution)/shard_map/pallas_call | solution.py:272
  184.5 1.3 fusion.291
  190.3 15.9 %shard_map.126 = f32[8,128]{1,0:T(8,128)} custom-call(f32[8,128]{1,0:T(8,128)} %pad_bitcast_fusion.x_ref), custom_call_target="tpu_custom_call" | custom-call | tf_op jit(solution)/shard_map/pallas_call | solution.py:272
  206.2 1.2 slice.453
  (112 shorter events, 22.0 us)
Async XLA Ops:
  1.7 30.6 %copy-start.20 = (f32[16]{0:T(128)S(1)}, f32[16]{0:T(128)}, u32[]{:S(2)}) copy-start(f32[16]{0:T(128)} %param.12) | copy-start | bytes 196
  1.7 30.6 %copy-start.21 = (f32[16]{0:T(128)S(1)}, f32[16]{0:T(128)}, u32[]{:S(2)}) copy-start(f32[16]{0:T(128)} %param.11) | copy-start | bytes 196
  48.0 28.0 %copy-start.14 = (f32[20,48,128]{2,1,0:T(8,128)S(1)}, f32[20,48,128]{2,1,0:T(8,128)}, u32[]{:S(2)}) copy-start(f32[20,48,128]{2,1,0:T(8,128)} %get-tuple-element.77) | copy-start | bytes 1474564
  76.7 11.5 %copy-start = (f32[20,48,128]{2,1,0:T(8,128)}, f32[20,48,128]{2,1,0:T(8,128)S(1)}, u32[]{:S(2)}) copy-start(f32[20,48,128]{2,1,0:T(8,128)S(1)} %get-tuple-element.62) | copy-start | bytes 1474564
  76.7 11.5 %copy-start.2 = (f32[20,48,128]{2,1,0:T(8,128)}, f32[20,48,128]{2,1,0:T(8,128)S(1)}, u32[]{:S(2)}) copy-start(f32[20,48,128]{2,1,0:T(8,128)S(1)} %get-tuple-element.63) | copy-start | bytes 1474564
  76.7 11.5 %copy-start.4 = (f32[20,48,128]{2,1,0:T(8,128)}, f32[20,48,128]{2,1,0:T(8,128)S(1)}, u32[]{:S(2)}) copy-start(f32[20,48,128]{2,1,0:T(8,128)S(1)} %get-tuple-element.64) | copy-start | bytes 1474564
  76.7 13.3 %copy-start.6 = (f32[20,48,128]{2,1,0:T(8,128)}, f32[20,48,128]{2,1,0:T(8,128)S(1)}, u32[]{:S(2)}) copy-start(f32[20,48,128]{2,1,0:T(8,128)S(1)} %get-tuple-element.65) | copy-start | bytes 1474564
  76.9 2.2 %copy-start.12 = (f32[20,48,128]{2,1,0:T(8,128)S(1)}, f32[20,48,128]{2,1,0:T(8,128)}, u32[]{:S(2)}) copy-start(f32[20,48,128]{2,1,0:T(8,128)} %get-tuple-element.42) | copy-start | bytes 1474564
  79.1 2.3 %copy-start.8 = (f32[20,48,128]{2,1,0:T(8,128)S(1)}, f32[20,48,128]{2,1,0:T(8,128)}, u32[]{:S(2)}) copy-start(f32[20,48,128]{2,1,0:T(8,128)} %get-tuple-element.43) | copy-start | bytes 1474564
  90.1 1.0 copy-start.10
  91.1 1.1 copy-start.19
  126.6 1.0 copy-start.1
  126.6 1.2 copy-start.3
  126.6 1.3 copy-start.5
  126.6 1.5 copy-start.7
  126.6 1.6 copy-start.13
  128.2 2.3 %copy-start.9 = (f32[20,48,128]{2,1,0:T(8,128)S(1)}, f32[20,48,128]{2,1,0:T(8,128)}, u32[]{:S(2)}) copy-start(f32[20,48,128]{2,1,0:T(8,128)} %get-tuple-element.43) | copy-start | bytes 1474564
  140.8 1.0 copy-start.11
  143.9 19.9 %copy-start.17 = (f32[8,32,16]{1,2,0:T(8,128)S(1)}, f32[8,32,16]{1,2,0:T(8,128)}, u32[]{:S(2)}) copy-start(f32[8,32,16]{1,2,0:T(8,128)} %param.17) | copy-start | bytes 49156
  143.9 20.0 %copy-start.15 = (f32[8,32,16]{1,2,0:T(8,128)S(1)}, f32[8,32,16]{1,2,0:T(8,128)}, u32[]{:S(2)}) copy-start(f32[8,32,16]{1,2,0:T(8,128)} %param.15) | copy-start | bytes 49156
  143.9 20.1 %copy-start.18 = (f32[8,32,16]{1,2,0:T(8,128)S(1)}, f32[8,32,16]{1,2,0:T(8,128)}, u32[]{:S(2)}) copy-start(f32[8,32,16]{1,2,0:T(8,128)} %param.18) | copy-start | bytes 49156
  143.9 20.1 %copy-start.16 = (f32[8,32,16]{1,2,0:T(8,128)S(1)}, f32[8,32,16]{1,2,0:T(8,128)}, u32[]{:S(2)}) copy-start(f32[8,32,16]{1,2,0:T(8,128)} %param.16) | copy-start | bytes 49156

commit v10 on v8

--- a/solution.py
+++ b/solution.py
@@ -67,7 +67,7 @@
     ax, ay = lax.axis_index("gx"), lax.axis_index("gy")
     nx, ny = lax.axis_size("gx"), lax.axis_size("gy")
     wide[...] = jnp.zeros_like(wide)
-    steps = [(dx, dy) for dx in (-1, 0, 1) for dy in (-1, 0, 1) if (dx, dy) != (0, 0)]
+    steps = [(-1, 0), (1, 0), (0, -1), (0, 1), (-1, -1), (-1, 1), (1, -1), (1, 1)]
 
     def exists(dx, dy):
         return (ax + dx >= 0) & (ax + dx < nx) & (ay + dy >= 0) & (ay + dy < ny)
@@ -100,22 +100,23 @@
         src_y, dst_y = window(dy, cy, hy)
         tx = jnp.clip(ax + dx, 0, nx - 1)
         ty = jnp.clip(ay + dy, 0, ny - 1)
-        copy = pltpu.make_async_remote_copy(
-            src_ref=x_ref.at[:, src_x, src_y, :],
-            dst_ref=wide.at[:, dst_x, dst_y, :],
-            send_sem=send_sem.at[k],
-            recv_sem=recv_sem.at[k],
-            device_id={"gx": tx, "gy": ty},
-            device_id_type=MESH,
-        )
-        copies.append(copy)
-
-        @pl.when(exists(dx, dy))
-        def _():
-            copy.start()
+        for f in range(fields):
+            copy = pltpu.make_async_remote_copy(
+                src_ref=x_ref.at[f, src_x, src_y, :],
+                dst_ref=wide.at[f, dst_x, dst_y, :],
+                send_sem=send_sem.at[k * fields + f],
+                recv_sem=recv_sem.at[k * fields + f],
+                device_id={"gx": tx, "gy": ty},
+                device_id_type=MESH,
+            )
+            copies.append((copy, dx, dy))
+
+            @pl.when(exists(dx, dy))
+            def _():
+                copy.start()
 
     local.wait()
-    for copy, (dx, dy) in zip(copies, steps):
+    for copy, dx, dy in copies:
         @pl.when(exists(dx, dy))
         def _():
             copy.wait_send()
@@ -137,8 +138,8 @@
         out_specs=pl.BlockSpec(memory_space=pltpu.VMEM),
         scratch_shapes=[
             pltpu.VMEM(shape, x.dtype),
-            pltpu.SemaphoreType.DMA((8,)),
-            pltpu.SemaphoreType.DMA((8,)),
+            pltpu.SemaphoreType.DMA((8 * fields,)),
+            pltpu.SemaphoreType.DMA((8 * fields,)),
             pltpu.SemaphoreType.DMA,
         ],
         compiler_params=pltpu.CompilerParams(

time: 207 us -> 207 us (level)
    pallas_call x1, Pallas kernels: 23 us -> 39.7 us  [halo_block(): pl.pallas_call(functools.partial(_halo_kernel, hx, hy), out_shape=jax.Sha...]
    pallas_call x3, Pallas kernels: 72.8 us -> 56.3 us  [small_sum(): pl.pallas_call(functools.partial(_reduce_kernel, stages), out_shape=jax.S...]
where the time goes in v10:
time: 207 us; the launch traced here: 206 us
  Pallas kernels  128 us (62%)
  other arithmetic  39.4 us (19%)
  local copies, waits for them, and re-layouts  20.2 us (10%)
  matrix products  11.3 us (5%)
  between operations  7.97 us (4%)
    pallas_call x3, Pallas kernels, small_sum(): pl.pallas_call(functools.partial(_reduce_kernel, stages), out_shape=jax.S...  56.3 us
    pallas_call x1, Pallas kernels, halo_block(): pl.pallas_call(functools.partial(_halo_kernel, hx, hy), out_shape=jax.Sha...  39.7 us
    pallas_call x2, Pallas kernels, exchange(): pl.pallas_call(functools.partial(_exchange_kernel, axis, n, scatter), out...  31.6 us
    add x8, other arithmetic, chebyshev(): step_dir = rho_next * rho * step_dir + 2.0 * rho_next / delta * remain  18.4 us
    unnamed x60, local copies, waits for them, and re-layouts  6.06 us
    dot_general x1, matrix products, per_device(): jnp.dot(both, depth_hot, precision=lax.Precision.HIGHEST)  5.57 us

profile of v10, /device:TPU:1, one launch (start us, length us, event | category | flops | bytes accessed | tf_op | source)
XLA Modules:
  0.0 206.4 jit_solution(8937620606206607995)
XLA Ops:
  2.5 16.7 %shard_map.121 = f32[8,64,128]{2,1,0:T(8,128)} custom-call(f32[64,128]{1,0:T(8,128)} %reshape.409.x_ref), custom_call_target="tpu_custom_call" | custom-call | tf_op jit(solution)/shard_map/pallas_call | solution.py:50
  19.2 1.7 reshape.410
  20.9 1.2 fusion.289
  22.1 1.6 copy.30
  24.8 39.7 %shard_map.122 = f32[7,20,48,128]{3,2,1,0:T(8,128)S(1)} custom-call(f32[7,8,32,128]{3,2,1,0:T(8,128)S(1)} %pad_maximum_fusion.1.x_ref), custom_call_target="tpu_custom_call" | custom-call | tf_op jit(solution)/shard_map/pallas_call | solution.py:134
  65.2 2.3 %fusion = f32[2,122880]{1,0:T(2,128)S(1)} fusion(f32[122880]{0:T(1024)S(1)} %bitcast.72, f32[1,16]{1,0:T(1,128)S(1)} %bitcast.75, f32[1,16]{1,0:T(1,128)S(1)} %bitcast.76), kind=kOutput, calls=%fused_computation.68 | convolution fusion | flops 49152032 | bytes 1474688 | tf_op jit(solution)/shard_map/dot_general | solution.py:333
  69.5 2.3 %broadcast_multiply_fusion.1 = (f32[4,20,48,128]{3,2,1,0:T(8,128)S(1)}, f32[4,20,48,128]{3,2,1,0:T(8,128)S(1)}) fusion(f32[4,20,48,128]{3,2,1,0:T(8,128)S(1)} %slice.349, f32[20,48,128]{2,1,0:T(8,128)S(1)} %get-tuple-element.75, f32[20,48,128]{2,1,0:T(8,128)S(1)} %get-tuple-element.79, f32[20,48,128]{2,1,0:T(8,128)S(1)} %get-tuple-element.78, ...), kind=kLoop, calls=%fused_computation.317 | loop fusion | flops 10321920 | bytes 9338880 | tf_op jit(solution)/shard_map/div | solution.py:287
  71.9 2.3 %multiply_add_fusion.7 = (f32[4,20,48,128]{3,2,1,0:T(8,128)S(1)}, f32[4,20,48,128]{3,2,1,0:T(8,128)S(1)}) fusion(f32[4,20,48,128]{3,2,1,0:T(8,128)S(1)} %get-tuple-element.41, f32[4,20,48,128]{3,2,1,0:T(8,128)S(1)} %get-tuple-element.40, f32[20,48,128]{2,1,0:T(8,128)S(1)} %get-tuple-element.62, f32[20,48,128]{2,1,0:T(8,128)S(1)} %get-tuple-element.58, ...), kind=kLoop, calls=%fused_computation.303 | loop fusion | flops 11304960 | bytes 11304960 | tf_op jit(solution)/shard_map/add | solution.py:293
  74.2 2.3 %multiply_add_fusion.6 = (f32[4,20,48,128]{3,2,1,0:T(8,128)S(1)}, f32[4,20,48,128]{3,2,1,0:T(8,128)S(1)}) fusion(f32[4,20,48,128]{3,2,1,0:T(8,128)S(1)} %get-tuple-element.36, f32[4,20,48,128]{3,2,1,0:T(8,128)S(1)} %get-tuple-element.37, f32[20,48,128]{2,1,0:T(8,128)S(1)} %get-tuple-element.62, f32[20,48,128]{2,1,0:T(8,128)S(1)} %get-tuple-element.58, ...), kind=kLoop, calls=%fused_computation.302 | loop fusion | flops 11304960 | bytes 11304960 | tf_op jit(solution)/shard_map/add | solution.py:293
  76.5 2.3 %multiply_add_fusion.5 = (f32[4,20,48,128]{3,2,1,0:T(8,128)S(1)}, f32[4,20,48,128]{3,2,1,0:T(8,128)S(1)}) fusion(f32[4,20,48,128]{3,2,1,0:T(8,128)S(1)} %get-tuple-element.34, f32[4,20,48,128]{3,2,1,0:T(8,128)S(1)} %get-tuple-element.35, f32[20,48,128]{2,1,0:T(8,128)S(1)} %get-tuple-element.62, f32[20,48,128]{2,1,0:T(8,128)S(1)} %get-tuple-element.58, ...), kind=kLoop, calls=%fused_computation.301 | loop fusion | flops 11304960 | bytes 11304960 | tf_op jit(solution)/shard_map/add | solution.py:293
  78.8 2.3 %multiply_add_fusion.4 = (f32[4,20,48,128]{3,2,1,0:T(8,128)S(1)}, f32[4,20,48,128]{3,2,1,0:T(8,128)S(1)}) fusion(f32[4,20,48,128]{3,2,1,0:T(8,128)S(1)} %get-tuple-element.32, f32[4,20,48,128]{3,2,1,0:T(8,128)S(1)} %get-tuple-element.33, f32[20,48,128]{2,1,0:T(8,128)S(1)} %get-tuple-element.62, f32[20,48,128]{2,1,0:T(8,128)S(1)} %get-tuple-element.58, ...), kind=kLoop, calls=%fused_computation.300 | loop fusion | flops 11304960 | bytes 11304960 | tf_op jit(solution)/shard_map/add | solution.py:293
  81.1 1.8 fusion.108
  84.0 1.1 pad_maximum_fusion
  85.3 5.6 %select_reduce_fusion = f32[8,1024]{1,0:T(8,128)S(1)} fusion(pred[256,1024]{1,0:T(8,128)(4,1)S(1)} %fusion.220, f32[8,256,128]{2,1,0:T(8,128)} %bitcast.69, s32[1024]{0:T(1024)S(1)} %get-tuple-element.86), kind=kOutput, calls=%fused_computation.66 | convolution fusion | flops 3225542656 | bytes 1347584 | tf_op jit(solution)/shard_map/dot_general | solution.py:360
  91.6 22.8 %shard_map.123 = f32[64,128]{1,0:T(8,128)} custom-call(f32[64,128]{1,0:T(8,128)} %reshape.411.x_ref), custom_call_target="tpu_custom_call" | custom-call | tf_op jit(solution)/shard_map/pallas_call | solution.py:223
  116.1 0.9 multiply_reduce_fusion.7
  117.4 3.5 %fusion.4 = f32[960,4,128]{2,0,1:T(8,128)S(1)} fusion(s32[1024]{0:T(1024)S(1)} %get-tuple-element.87, pred[1024]{0:T(1024)(128)(4,1)S(1)} %get-tuple-element.84, f32[1024,128]{0,1:T(8,128)S(1)} %fusion.244, f32[1024,4]{0,1:T(4,128)S(1)} %divide_bitcast_fusion), kind=kOutput, calls=%fused_computation.73 | convolution fusion | flops 6042288128 | bytes 2511872 | tf_op jit(solution)/shard_map/dot_general | solution.py:375
  122.9 2.2 %multiply_add_fusion.3 = (f32[4,20,48,128]{3,2,1,0:T(8,128)S(1)}, f32[4,20,48,128]{3,2,1,0:T(8,128)S(1)}) fusion(f32[4,20,48,128]{3,2,1,0:T(8,128)S(1)} %bitcast.60, f32[4,20,48,128]{3,2,1,0:T(8,128)S(1)} %broadcast_multiply_fusion, f32[20,48,128]{2,1,0:T(8,128)S(1)} %copy-done.11, f32[20,48,128]{2,1,0:T(8,128)S(1)} %copy-done.3, ...), kind=kLoop, calls=%fused_computation.299 | loop fusion | flops 11304960 | bytes 11304960 | tf_op jit(solution)/shard_map/add | solution.py:293
  125.1 2.3 %multiply_add_fusion.2 = (f32[4,20,48,128]{3,2,1,0:T(8,128)S(1)}, f32[4,20,48,128]{3,2,1,0:T(8,128)S(1)}) fusion(f32[4,20,48,128]{3,2,1,0:T(8,128)S(1)} %get-tuple-element.28, f32[4,20,48,128]{3,2,1,0:T(8,128)S(1)} %get-tuple-element.29, f32[20,48,128]{2,1,0:T(8,128)S(1)} %copy-done.11, f32[20,48,128]{2,1,0:T(8,128)S(1)} %copy-done.3, ...), kind=kLoop, calls=%fused_computation.298 | loop fusion | flops 11304960 | bytes 11304960 | tf_op jit(solution)/shard_map/add | solution.py:293
  127.5 2.3 %multiply_add_fusion.1 = (f32[4,20,48,128]{3,2,1,0:T(8,128)S(1)}, f32[4,20,48,128]{3,2,1,0:T(8,128)S(1)}) fusion(f32[4,20,48,128]{3,2,1,0:T(8,128)S(1)} %get-tuple-element.26, f32[4,20,48,128]{3,2,1,0:T(8,128)S(1)} %get-tuple-element.27, f32[20,48,128]{2,1,0:T(8,128)S(1)} %copy-done.11, f32[20,48,128]{2,1,0:T(8,128)S(1)} %copy-done.3, ...), kind=kLoop, calls=%fused_computation.297 | loop fusion | flops 11304960 | bytes 11304960 | tf_op jit(solution)/shard_map/add | solution.py:293
  129.8 2.3 %multiply_add_fusion = (f32[4,20,48,128]{3,2,1,0:T(8,128)S(1)}, f32[4,20,48,128]{3,2,1,0:T(8,128)S(1)}) fusion(f32[4,20,48,128]{3,2,1,0:T(8,128)S(1)} %get-tuple-element.24, f32[4,20,48,128]{3,2,1,0:T(8,128)S(1)} %get-tuple-element.25, f32[20,48,128]{2,1,0:T(8,128)S(1)} %copy-done.11, f32[20,48,128]{2,1,0:T(8,128)S(1)} %copy-done.3, ...), kind=kLoop, calls=%fused_computation.296 | loop fusion | flops 11304960 | bytes 11304960 | tf_op jit(solution)/shard_map/add | solution.py:293
  132.1 3.3 %fusion.205 = f32[4,20,48,128]{3,2,1,0:T(8,128)S(1)} fusion(f32[4,20,48,128]{3,2,1,0:T(8,128)S(1)} %get-tuple-element.23, f32[4,20,48,128]{3,2,1,0:T(8,128)S(1)} %get-tuple-element.22, f32[4,20,48,128]{3,2,1,0:T(8,128)S(1)} %get-tuple-element.24, f32[4,20,48,128]{3,2,1,0:T(8,128)S(1)} %get-tuple-element.26, f32[4,20,48,128]{3,2,1,0:T(8,128)S(1)} %get-tuple-element.28, ...), kind=kLoop, calls=%fused_computation.285 | loop fusion | flops 14254080 | bytes 17203200 | tf_op jit(solution)/shard_map/add | solution.py:289
  135.6 0.9 copy-done.16
  136.5 1.4 fusion.223
  138.2 0.9 neg.18
  140.1 1.3 reshape.413.x_ref
  141.4 14.9 %shard_map.124 = f32[8,64,128]{2,1,0:T(8,128)} custom-call(f32[8,64,128]{2,1,0:T(8,128)} %reshape.413.x_ref), custom_call_target="tpu_custom_call" | custom-call | tf_op jit(solution)/shard_map/pallas_call | solution.py:50
  156.3 1.0 reduce_sum.200
  163.1 18.2 %shard_map.125 = f32[8,128]{1,0:T(8,128)} custom-call(f32[8,128]{1,0:T(8,128)} %fusion.272.x_ref), custom_call_target="tpu_custom_call" | custom-call | tf_op jit(solution)/shard_map/pallas_call | solution.py:223
  181.3 1.3 fusion.292
  187.2 15.3 %shard_map.126 = f32[8,128]{1,0:T(8,128)} custom-call(f32[8,128]{1,0:T(8,128)} %pad_bitcast_fusion.x_ref), custom_call_target="tpu_custom_call" | custom-call | tf_op jit(solution)/shard_map/pallas_call | solution.py:223
  202.5 1.2 slice.453
  (120 shorter events, 19.2 us)
Async XLA Ops:
  22.1 2.3 %copy-start.21 = (s32[8,32,128]{2,1,0:T(8,128)S(1)}, s32[8,32,128]{2,1,0:T(8,128)}, u32[]{:S(2)}) copy-start(s32[8,32,128]{2,1,0:T(8,128)} %param.10) | copy-start | bytes 393220
  23.7 1.1 copy-start.14
  64.5 0.7 copy-start.25
  64.5 0.7 copy-start.26
  68.4 3.5 %copy-start.17 = (f32[20,48,128]{2,1,0:T(8,128)}, f32[20,48,128]{2,1,0:T(8,128)S(1)}, u32[]{:S(2)}) copy-start(f32[20,48,128]{2,1,0:T(8,128)S(1)} %get-tuple-element.38) | copy-start | bytes 1474564
  68.4 12.6 %copy-start.12 = (f32[20,48,128]{2,1,0:T(8,128)}, f32[20,48,128]{2,1,0:T(8,128)S(1)}, u32[]{:S(2)}) copy-start(f32[20,48,128]{2,1,0:T(8,128)S(1)} %get-tuple-element.39) | copy-start | bytes 1474564
  69.3 11.8 %copy-start = (f32[20,48,128]{2,1,0:T(8,128)}, f32[20,48,128]{2,1,0:T(8,128)S(1)}, u32[]{:S(2)}) copy-start(f32[20,48,128]{2,1,0:T(8,128)S(1)} %get-tuple-element.57) | copy-start | bytes 1474564
  69.3 11.8 %copy-start.2 = (f32[20,48,128]{2,1,0:T(8,128)}, f32[20,48,128]{2,1,0:T(8,128)S(1)}, u32[]{:S(2)}) copy-start(f32[20,48,128]{2,1,0:T(8,128)S(1)} %get-tuple-element.58) | copy-start | bytes 1474564
  69.3 11.8 %copy-start.4 = (f32[20,48,128]{2,1,0:T(8,128)}, f32[20,48,128]{2,1,0:T(8,128)S(1)}, u32[]{:S(2)}) copy-start(f32[20,48,128]{2,1,0:T(8,128)S(1)} %get-tuple-element.59) | copy-start | bytes 1474564
  69.3 11.8 %copy-start.6 = (f32[20,48,128]{2,1,0:T(8,128)}, f32[20,48,128]{2,1,0:T(8,128)S(1)}, u32[]{:S(2)}) copy-start(f32[20,48,128]{2,1,0:T(8,128)S(1)} %get-tuple-element.60) | copy-start | bytes 1474564
  69.3 11.8 %copy-start.8 = (f32[20,48,128]{2,1,0:T(8,128)}, f32[20,48,128]{2,1,0:T(8,128)S(1)}, u32[]{:S(2)}) copy-start(f32[20,48,128]{2,1,0:T(8,128)S(1)} %get-tuple-element.61) | copy-start | bytes 1474564
  69.4 13.6 %copy-start.10 = (f32[20,48,128]{2,1,0:T(8,128)}, f32[20,48,128]{2,1,0:T(8,128)S(1)}, u32[]{:S(2)}) copy-start(f32[20,48,128]{2,1,0:T(8,128)S(1)} %get-tuple-element.62) | copy-start | bytes 1474564
  83.0 1.0 copy-start.15
  84.0 1.1 copy-start.24
  120.9 1.0 copy-start.1
  120.9 1.2 copy-start.3
  120.9 1.3 copy-start.5
  120.9 1.5 copy-start.7
  121.0 1.6 copy-start.9
  121.0 1.7 copy-start.11
  121.0 1.9 copy-start.18
  122.8 2.3 %copy-start.13 = (f32[20,48,128]{2,1,0:T(8,128)S(1)}, f32[20,48,128]{2,1,0:T(8,128)}, u32[]{:S(2)}) copy-start(f32[20,48,128]{2,1,0:T(8,128)} %copy-done.12) | copy-start | bytes 1474564
  135.5 1.0 copy-start.16
  140.1 18.1 %copy-start.22 = (f32[8,32,16]{1,2,0:T(8,128)S(1)}, f32[8,32,16]{1,2,0:T(8,128)}, u32[]{:S(2)}) copy-start(f32[8,32,16]{1,2,0:T(8,128)} %param.17) | copy-start | bytes 49156
  140.1 18.2 %copy-start.19 = (f32[8,32,16]{1,2,0:T(8,128)S(1)}, f32[8,32,16]{1,2,0:T(8,128)}, u32[]{:S(2)}) copy-start(f32[8,32,16]{1,2,0:T(8,128)} %param.15) | copy-start | bytes 49156
  140.1 18.3 %copy-start.23 = (f32[8,32,16]{1,2,0:T(8,128)S(1)}, f32[8,32,16]{1,2,0:T(8,128)}, u32[]{:S(2)}) copy-start(f32[8,32,16]{1,2,0:T(8,128)} %param.18) | copy-start | bytes 49156
  140.1 18.4 %copy-start.20 = (f32[8,32,16]{1,2,0:T(8,128)S(1)}, f32[8,32,16]{1,2,0:T(8,128)}, u32[]{:S(2)}) copy-start(f32[8,32,16]{1,2,0:T(8,128)} %param.16) | copy-start | bytes 49156

commit v11 on v8

--- a/solution.py
+++ b/solution.py
@@ -355,9 +355,11 @@
     plane = (ix - anchor_x) * cy + (iy - anchor_y)
     plane_hot = (jnp.arange(cx * cy)[:, None] == plane[None, :]) & owned[None, :]
     depth_hot = (jnp.arange(cz)[:, None] == iz[None, :]).astype(jnp.float32)
-    both = jnp.concatenate([change, background], axis=0).reshape(-1, cz)
-    picked = jnp.dot(both, depth_hot, precision=lax.Precision.HIGHEST).reshape(2 * sources, cx * cy, -1)
-    picked = jnp.sum(jnp.where(plane_hot[None], picked, 0.0), axis=1)
+    both = jnp.concatenate([change, background], axis=0).reshape(2 * sources, cx * cy, cz)
+    picked = jnp.einsum(
+        "spz,pd->szd", both, plane_hot.astype(jnp.float32), precision=lax.Precision.HIGHEST
+    )
+    picked = jnp.sum(picked * depth_hot[None], axis=1)
     picks = small_sum(picked.reshape(-1), ("gy", "gx"), 1).reshape(2 * sources, -1)
     seen, base = picks[:sources], picks[sources:]
     total = jnp.sum(base, axis=1, keepdims=True)

time: 207 us -> 205 us (level)
  matrix products: 11.3 us -> 9.14 us
    dot_general x1, matrix products: 5.58 us -> 3.38 us  [per_device(): jnp.einsum('spz,pd->szd', both, plane_hot.astype(jnp.float32), precision=...]
where the time goes in v11:
time: 205 us; the launch traced here: 204 us
  Pallas kernels  127 us (62%)
  other arithmetic  39.3 us (19%)
  local copies, waits for them, and re-layouts  20.2 us (10%)
  matrix products  9.14 us (4%)
  between operations  7.97 us (4%)
    pallas_call x3, Pallas kernels, small_sum(): pl.pallas_call(functools.partial(_reduce_kernel, stages), out_shape=jax.S...  72.8 us
    pallas_call x2, Pallas kernels, exchange(): pl.pallas_call(functools.partial(_exchange_kernel, axis, n, scatter), out...  31.6 us
    pallas_call x1, Pallas kernels, halo_block(): pl.pallas_call(functools.partial(_halo_kernel, hx, hy), out_shape=jax.Sha...  23 us
    add x8, other arithmetic, chebyshev(): step_dir = rho_next * rho * step_dir + 2.0 * rho_next / delta * remain  18.4 us
    unnamed x60, local copies, waits for them, and re-layouts  6.06 us

profile of v11, /device:TPU:1, one launch (start us, length us, event | category | flops | bytes accessed | tf_op | source)
XLA Modules:
  0.0 204.0 jit_solution(7836429556646974122)
XLA Ops:
  2.5 16.7 %shard_map.121 = f32[8,64,128]{2,1,0:T(8,128)} custom-call(f32[64,128]{1,0:T(8,128)} %reshape.394.x_ref), custom_call_target="tpu_custom_call" | custom-call | tf_op jit(solution)/shard_map/pallas_call | solution.py:50
  19.2 1.7 reshape.395
  20.9 1.2 fusion.291
  22.1 1.6 copy.32
  24.8 23.0 %shard_map.122 = f32[7,20,48,128]{3,2,1,0:T(8,128)S(1)} custom-call(f32[7,8,32,128]{3,2,1,0:T(8,128)S(1)} %pad_maximum_fusion.1.x_ref), custom_call_target="tpu_custom_call" | custom-call | tf_op jit(solution)/shard_map/pallas_call | solution.py:133
  48.5 2.3 %fusion = f32[2,122880]{1,0:T(2,128)S(1)} fusion(f32[122880]{0:T(1024)S(1)} %bitcast.72, f32[1,16]{1,0:T(1,128)S(1)} %bitcast.75, f32[1,16]{1,0:T(1,128)S(1)} %bitcast.76), kind=kOutput, calls=%fused_computation.67 | convolution fusion | flops 49152032 | bytes 1474688 | tf_op jit(solution)/shard_map/dot_general | solution.py:332
  52.9 2.2 %broadcast_multiply_fusion.1 = (f32[4,20,48,128]{3,2,1,0:T(8,128)S(1)}, f32[4,20,48,128]{3,2,1,0:T(8,128)S(1)}) fusion(f32[4,20,48,128]{3,2,1,0:T(8,128)S(1)} %slice.349, f32[20,48,128]{2,1,0:T(8,128)S(1)} %get-tuple-element.75, f32[20,48,128]{2,1,0:T(8,128)S(1)} %get-tuple-element.79, f32[20,48,128]{2,1,0:T(8,128)S(1)} %get-tuple-element.78, ...), kind=kLoop, calls=%fused_computation.318 | loop fusion | flops 10321920 | bytes 9338880 | tf_op jit(solution)/shard_map/div | solution.py:286
  55.0 2.3 %multiply_add_fusion.7 = (f32[4,20,48,128]{3,2,1,0:T(8,128)S(1)}, f32[4,20,48,128]{3,2,1,0:T(8,128)S(1)}) fusion(f32[4,20,48,128]{3,2,1,0:T(8,128)S(1)} %get-tuple-element.41, f32[4,20,48,128]{3,2,1,0:T(8,128)S(1)} %get-tuple-element.40, f32[20,48,128]{2,1,0:T(8,128)S(1)} %get-tuple-element.62, f32[20,48,128]{2,1,0:T(8,128)S(1)} %get-tuple-element.58, ...), kind=kLoop, calls=%fused_computation.303 | loop fusion | flops 11304960 | bytes 11304960 | tf_op jit(solution)/shard_map/add | solution.py:292
  57.4 2.3 %multiply_add_fusion.6 = (f32[4,20,48,128]{3,2,1,0:T(8,128)S(1)}, f32[4,20,48,128]{3,2,1,0:T(8,128)S(1)}) fusion(f32[4,20,48,128]{3,2,1,0:T(8,128)S(1)} %get-tuple-element.36, f32[4,20,48,128]{3,2,1,0:T(8,128)S(1)} %get-tuple-element.37, f32[20,48,128]{2,1,0:T(8,128)S(1)} %get-tuple-element.62, f32[20,48,128]{2,1,0:T(8,128)S(1)} %get-tuple-element.58, ...), kind=kLoop, calls=%fused_computation.302 | loop fusion | flops 11304960 | bytes 11304960 | tf_op jit(solution)/shard_map/add | solution.py:292
  59.7 2.3 %multiply_add_fusion.5 = (f32[4,20,48,128]{3,2,1,0:T(8,128)S(1)}, f32[4,20,48,128]{3,2,1,0:T(8,128)S(1)}) fusion(f32[4,20,48,128]{3,2,1,0:T(8,128)S(1)} %get-tuple-element.34, f32[4,20,48,128]{3,2,1,0:T(8,128)S(1)} %get-tuple-element.35, f32[20,48,128]{2,1,0:T(8,128)S(1)} %get-tuple-element.62, f32[20,48,128]{2,1,0:T(8,128)S(1)} %get-tuple-element.58, ...), kind=kLoop, calls=%fused_computation.301 | loop fusion | flops 11304960 | bytes 11304960 | tf_op jit(solution)/shard_map/add | solution.py:292
  61.9 2.3 %multiply_add_fusion.4 = (f32[4,20,48,128]{3,2,1,0:T(8,128)S(1)}, f32[4,20,48,128]{3,2,1,0:T(8,128)S(1)}) fusion(f32[4,20,48,128]{3,2,1,0:T(8,128)S(1)} %get-tuple-element.32, f32[4,20,48,128]{3,2,1,0:T(8,128)S(1)} %get-tuple-element.33, f32[20,48,128]{2,1,0:T(8,128)S(1)} %get-tuple-element.62, f32[20,48,128]{2,1,0:T(8,128)S(1)} %get-tuple-element.58, ...), kind=kLoop, calls=%fused_computation.300 | loop fusion | flops 11304960 | bytes 11304960 | tf_op jit(solution)/shard_map/add | solution.py:292
  64.3 2.0 fusion.108
  67.4 1.1 pad_maximum_fusion
  68.6 3.4 %multiply_reduce_fusion = f32[8,1024]{1,0:T(8,128)S(1)} fusion(f32[8,256,128]{2,1,0:T(8,128)} %bitcast.69, f32[128,1024]{1,0:T(8,128)S(1)} %fusion.245, s32[1024]{0:T(1024)S(1)} %get-tuple-element.85, pred[1024]{0:T(1024)(128)(4,1)S(1)} %get-tuple-element.83), kind=kOutput, calls=%fused_computation.68 | convolution fusion | flops 3223838720 | bytes 1610752 | tf_op jit(solution)/shard_map/spz,pd->szd/dot_general | solution.py:359
  72.6 41.1 %shard_map.123 = f32[64,128]{1,0:T(8,128)} custom-call(f32[64,128]{1,0:T(8,128)} %reshape.397.x_ref), custom_call_target="tpu_custom_call" | custom-call | tf_op jit(solution)/shard_map/pallas_call | solution.py:222
  115.5 0.9 multiply_reduce_fusion.8
  116.8 3.5 %fusion.4 = f32[960,4,128]{2,0,1:T(8,128)S(1)} fusion(s32[1024]{0:T(1024)S(1)} %get-tuple-element.87, pred[1024]{0:T(1024)(128)(4,1)S(1)} %get-tuple-element.84, f32[1024,128]{0,1:T(8,128)S(1)} %fusion.246, f32[1024,4]{0,1:T(4,128)S(1)} %divide_bitcast_fusion), kind=kOutput, calls=%fused_computation.73 | convolution fusion | flops 6042288128 | bytes 2511872 | tf_op jit(solution)/shard_map/dot_general | solution.py:376
  122.2 2.2 %multiply_add_fusion.3 = (f32[4,20,48,128]{3,2,1,0:T(8,128)S(1)}, f32[4,20,48,128]{3,2,1,0:T(8,128)S(1)}) fusion(f32[4,20,48,128]{3,2,1,0:T(8,128)S(1)} %bitcast.60, f32[4,20,48,128]{3,2,1,0:T(8,128)S(1)} %broadcast_multiply_fusion, f32[20,48,128]{2,1,0:T(8,128)S(1)} %copy-done.11, f32[20,48,128]{2,1,0:T(8,128)S(1)} %copy-done.3, ...), kind=kLoop, calls=%fused_computation.299 | loop fusion | flops 11304960 | bytes 11304960 | tf_op jit(solution)/shard_map/add | solution.py:292
  124.5 2.3 %multiply_add_fusion.2 = (f32[4,20,48,128]{3,2,1,0:T(8,128)S(1)}, f32[4,20,48,128]{3,2,1,0:T(8,128)S(1)}) fusion(f32[4,20,48,128]{3,2,1,0:T(8,128)S(1)} %get-tuple-element.28, f32[4,20,48,128]{3,2,1,0:T(8,128)S(1)} %get-tuple-element.29, f32[20,48,128]{2,1,0:T(8,128)S(1)} %copy-done.11, f32[20,48,128]{2,1,0:T(8,128)S(1)} %copy-done.3, ...), kind=kLoop, calls=%fused_computation.298 | loop fusion | flops 11304960 | bytes 11304960 | tf_op jit(solution)/shard_map/add | solution.py:292
  126.8 2.3 %multiply_add_fusion.1 = (f32[4,20,48,128]{3,2,1,0:T(8,128)S(1)}, f32[4,20,48,128]{3,2,1,0:T(8,128)S(1)}) fusion(f32[4,20,48,128]{3,2,1,0:T(8,128)S(1)} %get-tuple-element.26, f32[4,20,48,128]{3,2,1,0:T(8,128)S(1)} %get-tuple-element.27, f32[20,48,128]{2,1,0:T(8,128)S(1)} %copy-done.11, f32[20,48,128]{2,1,0:T(8,128)S(1)} %copy-done.3, ...), kind=kLoop, calls=%fused_computation.297 | loop fusion | flops 11304960 | bytes 11304960 | tf_op jit(solution)/shard_map/add | solution.py:292
  129.2 2.3 %multiply_add_fusion = (f32[4,20,48,128]{3,2,1,0:T(8,128)S(1)}, f32[4,20,48,128]{3,2,1,0:T(8,128)S(1)}) fusion(f32[4,20,48,128]{3,2,1,0:T(8,128)S(1)} %get-tuple-element.24, f32[4,20,48,128]{3,2,1,0:T(8,128)S(1)} %get-tuple-element.25, f32[20,48,128]{2,1,0:T(8,128)S(1)} %copy-done.11, f32[20,48,128]{2,1,0:T(8,128)S(1)} %copy-done.3, ...), kind=kLoop, calls=%fused_computation.296 | loop fusion | flops 11304960 | bytes 11304960 | tf_op jit(solution)/shard_map/add | solution.py:292
  131.5 3.3 %fusion.205 = f32[4,20,48,128]{3,2,1,0:T(8,128)S(1)} fusion(f32[4,20,48,128]{3,2,1,0:T(8,128)S(1)} %get-tuple-element.23, f32[4,20,48,128]{3,2,1,0:T(8,128)S(1)} %get-tuple-element.22, f32[4,20,48,128]{3,2,1,0:T(8,128)S(1)} %get-tuple-element.24, f32[4,20,48,128]{3,2,1,0:T(8,128)S(1)} %get-tuple-element.26, f32[4,20,48,128]{3,2,1,0:T(8,128)S(1)} %get-tuple-element.28, ...), kind=kLoop, calls=%fused_computation.285 | loop fusion | flops 14254080 | bytes 17203200 | tf_op jit(solution)/shard_map/add | solution.py:288
  135.0 0.9 copy-done.16
  135.9 1.4 fusion.225
  137.6 0.9 neg.18
  139.5 1.3 reshape.399.x_ref
  140.7 15.0 %shard_map.124 = f32[8,64,128]{2,1,0:T(8,128)} custom-call(f32[8,64,128]{2,1,0:T(8,128)} %reshape.399.x_ref), custom_call_target="tpu_custom_call" | custom-call | tf_op jit(solution)/shard_map/pallas_call | solution.py:50
  155.7 1.0 reduce_sum.200
  162.5 17.2 %shard_map.125 = f32[8,128]{1,0:T(8,128)} custom-call(f32[8,128]{1,0:T(8,128)} %fusion.274.x_ref), custom_call_target="tpu_custom_call" | custom-call | tf_op jit(solution)/shard_map/pallas_call | solution.py:222
  179.7 1.3 fusion.294
  185.6 14.5 %shard_map.126 = f32[8,128]{1,0:T(8,128)} custom-call(f32[8,128]{1,0:T(8,128)} %pad_bitcast_fusion.x_ref), custom_call_target="tpu_custom_call" | custom-call | tf_op jit(solution)/shard_map/pallas_call | solution.py:222
  200.1 1.2 slice.453
  (120 shorter events, 19.1 us)
Async XLA Ops:
  22.1 2.3 %copy-start.21 = (s32[8,32,128]{2,1,0:T(8,128)S(1)}, s32[8,32,128]{2,1,0:T(8,128)}, u32[]{:S(2)}) copy-start(s32[8,32,128]{2,1,0:T(8,128)} %param.10) | copy-start | bytes 393220
  23.7 1.1 copy-start.14
  47.8 0.7 copy-start.25
  47.8 0.7 copy-start.26
  51.8 3.3 %copy-start.17 = (f32[20,48,128]{2,1,0:T(8,128)}, f32[20,48,128]{2,1,0:T(8,128)S(1)}, u32[]{:S(2)}) copy-start(f32[20,48,128]{2,1,0:T(8,128)S(1)} %get-tuple-element.38) | copy-start | bytes 1474564
  51.8 12.5 %copy-start.12 = (f32[20,48,128]{2,1,0:T(8,128)}, f32[20,48,128]{2,1,0:T(8,128)S(1)}, u32[]{:S(2)}) copy-start(f32[20,48,128]{2,1,0:T(8,128)S(1)} %get-tuple-element.39) | copy-start | bytes 1474564
  52.6 11.6 %copy-start = (f32[20,48,128]{2,1,0:T(8,128)}, f32[20,48,128]{2,1,0:T(8,128)S(1)}, u32[]{:S(2)}) copy-start(f32[20,48,128]{2,1,0:T(8,128)S(1)} %get-tuple-element.57) | copy-start | bytes 1474564
  52.7 11.6 %copy-start.2 = (f32[20,48,128]{2,1,0:T(8,128)}, f32[20,48,128]{2,1,0:T(8,128)S(1)}, u32[]{:S(2)}) copy-start(f32[20,48,128]{2,1,0:T(8,128)S(1)} %get-tuple-element.58) | copy-start | bytes 1474564
  52.7 11.6 %copy-start.4 = (f32[20,48,128]{2,1,0:T(8,128)}, f32[20,48,128]{2,1,0:T(8,128)S(1)}, u32[]{:S(2)}) copy-start(f32[20,48,128]{2,1,0:T(8,128)S(1)} %get-tuple-element.59) | copy-start | bytes 1474564
  52.7 11.6 %copy-start.6 = (f32[20,48,128]{2,1,0:T(8,128)}, f32[20,48,128]{2,1,0:T(8,128)S(1)}, u32[]{:S(2)}) copy-start(f32[20,48,128]{2,1,0:T(8,128)S(1)} %get-tuple-element.60) | copy-start | bytes 1474564
  52.7 11.6 %copy-start.8 = (f32[20,48,128]{2,1,0:T(8,128)}, f32[20,48,128]{2,1,0:T(8,128)S(1)}, u32[]{:S(2)}) copy-start(f32[20,48,128]{2,1,0:T(8,128)S(1)} %get-tuple-element.61) | copy-start | bytes 1474564
  52.7 13.6 %copy-start.10 = (f32[20,48,128]{2,1,0:T(8,128)}, f32[20,48,128]{2,1,0:T(8,128)S(1)}, u32[]{:S(2)}) copy-start(f32[20,48,128]{2,1,0:T(8,128)S(1)} %get-tuple-element.62) | copy-start | bytes 1474564
  66.3 1.0 copy-start.15
  67.4 1.1 copy-start.24
  120.3 1.0 copy-start.1
  120.3 1.2 copy-start.3
  120.3 1.3 copy-start.5
  120.3 1.5 copy-start.7
  120.3 1.6 copy-start.9
  120.3 1.7 copy-start.11
  120.4 1.9 copy-start.18
  122.2 2.3 %copy-start.13 = (f32[20,48,128]{2,1,0:T(8,128)S(1)}, f32[20,48,128]{2,1,0:T(8,128)}, u32[]{:S(2)}) copy-start(f32[20,48,128]{2,1,0:T(8,128)} %copy-done.12) | copy-start | bytes 1474564
  134.8 1.0 copy-start.16
  139.4 18.1 %copy-start.22 = (f32[8,32,16]{1,2,0:T(8,128)S(1)}, f32[8,32,16]{1,2,0:T(8,128)}, u32[]{:S(2)}) copy-start(f32[8,32,16]{1,2,0:T(8,128)} %param.17) | copy-start | bytes 49156
  139.5 18.2 %copy-start.19 = (f32[8,32,16]{1,2,0:T(8,128)S(1)}, f32[8,32,16]{1,2,0:T(8,128)}, u32[]{:S(2)}) copy-start(f32[8,32,16]{1,2,0:T(8,128)} %param.15) | copy-start | bytes 49156
  139.5 18.3 %copy-start.23 = (f32[8,32,16]{1,2,0:T(8,128)S(1)}, f32[8,32,16]{1,2,0:T(8,128)}, u32[]{:S(2)}) copy-start(f32[8,32,16]{1,2,0:T(8,128)} %param.18) | copy-start | bytes 49156
  139.5 18.4 %copy-start.20 = (f32[8,32,16]{1,2,0:T(8,128)S(1)}, f32[8,32,16]{1,2,0:T(8,128)}, u32[]{:S(2)}) copy-start(f32[8,32,16]{1,2,0:T(8,128)} %param.16) | copy-start | bytes 49156

commit v12 on v11

--- a/solution.py
+++ b/solution.py
@@ -166,7 +166,13 @@
     return n, me, member
 
 
-def _reduce_kernel(stages, x_ref, o_ref, *scratch):
+def _reduce_kernel(stages, scatter, *refs):
+    if scatter:
+        g_ref, x_ref, h_ref, o_ref, g_slots, g_send, g_recv, g_local = refs[:8]
+        scratch = refs[8:]
+    else:
+        x_ref, o_ref = refs[:2]
+        scratch = refs[2:]
     count = len(stages)
     slots, sends, recvs = scratch[:count], scratch[count : 2 * count], scratch[2 * count : 3 * count]
     held = scratch[3 * count :]
@@ -180,6 +186,24 @@
             )
         peers += n - 1
     pl.semaphore_wait(barrier, peers)
+    if scatter:
+        n = lax.axis_size("src")
+        me = lax.axis_index("src")
+        parts = []
+        for k in range(1, n):
+            peer = lax.rem(me + k, n)
+            part = pltpu.make_async_remote_copy(
+                src_ref=g_ref.at[peer],
+                dst_ref=g_slots.at[me],
+                send_sem=g_send.at[k - 1],
+                recv_sem=g_recv.at[k - 1],
+                device_id={"src": peer},
+                device_id_type=MESH,
+            )
+            part.start()
+            parts.append(part)
+        own = pltpu.make_async_copy(g_ref.at[me], g_slots.at[me], g_local)
+        own.start()
     value = x_ref
     for i, axes in enumerate(stages):
         n, me, member = _group(axes)
@@ -206,8 +230,16 @@
             value = held[i]
         else:
             o_ref[...] = total
-
-def small_sum(values, axes, cid):
+    if scatter:
+        own.wait()
+        for part in parts:
+            part.wait()
+        total = g_slots[0]
+        for j in range(1, lax.axis_size("src")):
+            total = total + g_slots[j]
+        h_ref[...] = total
+
+def small_sum(values, axes, cid, spread=None):
     count = values.shape[0]
     rows = -(-count // 1024) * 8
     packed = jnp.pad(values, (0, rows * 128 - count)).reshape(rows, 128)
@@ -219,15 +251,31 @@
         + [pltpu.SemaphoreType.DMA((n - 1,)) for n in sizes]
         + [pltpu.VMEM((rows, 128), jnp.float32) for n in sizes[:-1]]
     )
-    total = pl.pallas_call(
-        functools.partial(_reduce_kernel, stages),
-        out_shape=jax.ShapeDtypeStruct((rows, 128), jnp.float32),
-        in_specs=[pl.BlockSpec(memory_space=pltpu.VMEM)],
-        out_specs=pl.BlockSpec(memory_space=pltpu.VMEM),
+    vmem = pl.BlockSpec(memory_space=pltpu.VMEM)
+    small = jax.ShapeDtypeStruct((rows, 128), jnp.float32)
+    operands, out_shape, out_specs = (packed,), small, vmem
+    if spread is not None:
+        n = spread.shape[0]
+        scratch = [
+            pltpu.VMEM(spread.shape, jnp.float32),
+            pltpu.SemaphoreType.DMA((n - 1,)),
+            pltpu.SemaphoreType.DMA((n - 1,)),
+            pltpu.SemaphoreType.DMA,
+        ] + scratch
+        operands = (spread, packed)
+        out_shape = (jax.ShapeDtypeStruct(spread.shape[1:], jnp.float32), small)
+        out_specs = (vmem, vmem)
+    result = pl.pallas_call(
+        functools.partial(_reduce_kernel, stages, spread is not None),
+        out_shape=out_shape,
+        in_specs=[vmem] * len(operands),
+        out_specs=out_specs,
         scratch_shapes=scratch,
         compiler_params=pltpu.CompilerParams(collective_id=cid, has_side_effects=True),
-    )(packed)
-    return total.reshape(-1)[:count]
+    )(*operands)
+    if spread is not None:
+        return result[0], result[1].reshape(-1)[:count]
+    return result.reshape(-1)[:count]
 
 
 def padded_2(block, sides, width):
@@ -386,14 +434,19 @@
         grad_k = grad_k - 0.5 * jnp.sum((background - near_phi) * (dual - near_dual), axis=0)
     grads = jnp.stack([grad_k, grad_a]).reshape(2, cx, cy, n_src, slab)
     grads = jnp.transpose(grads, (3, 0, 1, 2, 4)).reshape(n_src, -1, 128)
-    hv = jnp.sum(exchange(grads, "src", 3, scatter=True), axis=0).reshape(2, cx, cy, slab)
+    local_hv = jnp.sum(grad_k * full_k) + jnp.sum(grad_a * full_a)
+    local_qv = jnp.sum(q_kappa * v_kappa) + jnp.sum(q_absorb * v_absorb)
+    local_vv = jnp.sum(v_kappa * v_kappa) + jnp.sum(v_absorb * v_absorb)
+    hv, dots = small_sum(
+        jnp.stack([local_hv, local_qv, local_vv]), (("gx", "gy"), "src"), 3, spread=grads
+    )
+    hv = hv.reshape(2, cx, cy, slab)
     hv_k, hv_a = hv[0], hv[1]
     cell_count = cx * lax.axis_size("gx") * cy * lax.axis_size("gy") * cz
     w_k = hv_k - beta_prev[0] * q_kappa
     w_a = hv_a - beta_prev[0] * q_absorb
-    local_wv = jnp.sum(w_k * v_kappa) + jnp.sum(w_a * v_absorb)
-    local_vv = jnp.sum(v_kappa * v_kappa) + jnp.sum(v_absorb * v_absorb)
-    wv_sum, vv_sum = small_sum(jnp.stack([local_wv, local_vv]), (("gx", "gy"), "src"), 4)
+    wv_sum = dots[0] - beta_prev[0] * dots[1]
+    vv_sum = dots[2]
     alpha = wv_sum / cell_count / (vv_sum / cell_count + eps_norm)
     r_k = w_k - alpha * v_kappa
     r_a = w_a - alpha * v_absorb

time: 205 us -> 204 us (level)
  Pallas kernels: 127 us -> 121 us
  local copies, waits for them, and re-layouts: 20.2 us -> 24.2 us
    pallas_call x2 -> x1, Pallas kernels: 31.6 us -> 16.7 us  [exchange(): pl.pallas_call(functools.partial(_exchange_kernel, axis, n, scatter), out...]
    pallas_call x3, Pallas kernels: 72.8 us -> 80.8 us  [small_sum(): pl.pallas_call(functools.partial(_reduce_kernel, stages, spread is not No...]
    unnamed x60 -> x66, local copies, waits for them, and re-layouts: 6.06 us -> 6.31 us
where the time goes in v12:
time: 204 us; the launch traced here: 203 us
  Pallas kernels  121 us (59%)
  other arithmetic  39.2 us (19%)
  local copies, waits for them, and re-layouts  24.2 us (12%)
  between operations  9.8 us (5%)
  matrix products  9.14 us (4%)
    pallas_call x3, Pallas kernels, small_sum(): pl.pallas_call(functools.partial(_reduce_kernel, stages, spread is not No...  80.8 us
    pallas_call x1, Pallas kernels, halo_block(): pl.pallas_call(functools.partial(_halo_kernel, hx, hy), out_shape=jax.Sha...  23 us
    add x8, other arithmetic, chebyshev(): step_dir = rho_next * rho * step_dir + 2.0 * rho_next / delta * remain  18.4 us
    pallas_call x1, Pallas kernels, exchange(): pl.pallas_call(functools.partial(_exchange_kernel, axis, n, scatter), out...  16.7 us
    unnamed x66, local copies, waits for them, and re-layouts  6.31 us

profile of v12, /device:TPU:1, one launch (start us, length us, event | category | flops | bytes accessed | tf_op | source)
XLA Modules:
  0.0 202.8 jit_solution(3867532224159635734)
XLA Ops:
  2.5 16.7 %shard_map.121 = f32[8,64,128]{2,1,0:T(8,128)} custom-call(f32[64,128]{1,0:T(8,128)} %reshape.399.x_ref), custom_call_target="tpu_custom_call" | custom-call | tf_op jit(solution)/shard_map/pallas_call | solution.py:50
  19.2 1.7 reshape.400
  20.9 1.5 fusion.291
  22.6 1.6 copy.35
  25.3 23.0 %shard_map.122 = f32[7,20,48,128]{3,2,1,0:T(8,128)S(1)} custom-call(f32[7,8,32,128]{3,2,1,0:T(8,128)S(1)} %pad_maximum_fusion.1.x_ref), custom_call_target="tpu_custom_call" | custom-call | tf_op jit(solution)/shard_map/pallas_call | solution.py:133
  49.0 2.3 %fusion = f32[2,122880]{1,0:T(2,128)S(1)} fusion(f32[122880]{0:T(1024)S(1)} %bitcast.79, f32[1,16]{1,0:T(1,128)S(1)} %bitcast.82, f32[1,16]{1,0:T(1,128)S(1)} %bitcast.83), kind=kOutput, calls=%fused_computation.67 | convolution fusion | flops 49152032 | bytes 1474688 | tf_op jit(solution)/shard_map/dot_general | solution.py:380
  53.3 2.2 %broadcast_multiply_fusion.1 = (f32[4,20,48,128]{3,2,1,0:T(8,128)S(1)}, f32[4,20,48,128]{3,2,1,0:T(8,128)S(1)}) fusion(f32[4,20,48,128]{3,2,1,0:T(8,128)S(1)} %slice.359, f32[20,48,128]{2,1,0:T(8,128)S(1)} %get-tuple-element.85, f32[20,48,128]{2,1,0:T(8,128)S(1)} %get-tuple-element.89, f32[20,48,128]{2,1,0:T(8,128)S(1)} %get-tuple-element.88, ...), kind=kLoop, calls=%fused_computation.320 | loop fusion | flops 10321920 | bytes 9338880 | tf_op jit(solution)/shard_map/div | solution.py:334
  55.5 2.3 %multiply_add_fusion.7 = (f32[4,20,48,128]{3,2,1,0:T(8,128)S(1)}, f32[4,20,48,128]{3,2,1,0:T(8,128)S(1)}) fusion(f32[4,20,48,128]{3,2,1,0:T(8,128)S(1)} %get-tuple-element.51, f32[4,20,48,128]{3,2,1,0:T(8,128)S(1)} %get-tuple-element.50, f32[20,48,128]{2,1,0:T(8,128)S(1)} %get-tuple-element.72, f32[20,48,128]{2,1,0:T(8,128)S(1)} %get-tuple-element.68, ...), kind=kLoop, calls=%fused_computation.303 | loop fusion | flops 11304960 | bytes 11304960 | tf_op jit(solution)/shard_map/add | solution.py:340
  57.9 2.3 %multiply_add_fusion.6 = (f32[4,20,48,128]{3,2,1,0:T(8,128)S(1)}, f32[4,20,48,128]{3,2,1,0:T(8,128)S(1)}) fusion(f32[4,20,48,128]{3,2,1,0:T(8,128)S(1)} %get-tuple-element.46, f32[4,20,48,128]{3,2,1,0:T(8,128)S(1)} %get-tuple-element.47, f32[20,48,128]{2,1,0:T(8,128)S(1)} %get-tuple-element.72, f32[20,48,128]{2,1,0:T(8,128)S(1)} %get-tuple-element.68, ...), kind=kLoop, calls=%fused_computation.302 | loop fusion | flops 11304960 | bytes 11304960 | tf_op jit(solution)/shard_map/add | solution.py:340
  60.1 2.3 %multiply_add_fusion.5 = (f32[4,20,48,128]{3,2,1,0:T(8,128)S(1)}, f32[4,20,48,128]{3,2,1,0:T(8,128)S(1)}) fusion(f32[4,20,48,128]{3,2,1,0:T(8,128)S(1)} %get-tuple-element.44, f32[4,20,48,128]{3,2,1,0:T(8,128)S(1)} %get-tuple-element.45, f32[20,48,128]{2,1,0:T(8,128)S(1)} %get-tuple-element.72, f32[20,48,128]{2,1,0:T(8,128)S(1)} %get-tuple-element.68, ...), kind=kLoop, calls=%fused_computation.301 | loop fusion | flops 11304960 | bytes 11304960 | tf_op jit(solution)/shard_map/add | solution.py:340
  62.4 2.3 %multiply_add_fusion.4 = (f32[4,20,48,128]{3,2,1,0:T(8,128)S(1)}, f32[4,20,48,128]{3,2,1,0:T(8,128)S(1)}) fusion(f32[4,20,48,128]{3,2,1,0:T(8,128)S(1)} %get-tuple-element.42, f32[4,20,48,128]{3,2,1,0:T(8,128)S(1)} %get-tuple-element.43, f32[20,48,128]{2,1,0:T(8,128)S(1)} %get-tuple-element.72, f32[20,48,128]{2,1,0:T(8,128)S(1)} %get-tuple-element.68, ...), kind=kLoop, calls=%fused_computation.300 | loop fusion | flops 11304960 | bytes 11304960 | tf_op jit(solution)/shard_map/add | solution.py:340
  64.8 2.0 fusion.108
  67.9 1.1 pad_maximum_fusion
  69.1 3.4 %multiply_reduce_fusion = f32[8,1024]{1,0:T(8,128)S(1)} fusion(f32[8,256,128]{2,1,0:T(8,128)} %bitcast.76, f32[128,1024]{1,0:T(8,128)S(1)} %fusion.245, s32[1024]{0:T(1024)S(1)} %get-tuple-element.96, pred[1024]{0:T(1024)(128)(4,1)S(1)} %get-tuple-element.94), kind=kOutput, calls=%fused_computation.68 | convolution fusion | flops 3223838720 | bytes 1610752 | tf_op jit(solution)/shard_map/spz,pd->szd/dot_general | solution.py:407
  73.1 41.1 %shard_map.123 = f32[64,128]{1,0:T(8,128)} custom-call(f32[64,128]{1,0:T(8,128)} %reshape.402.refs_0_), custom_call_target="tpu_custom_call" | custom-call | tf_op jit(solution)/shard_map/pallas_call | solution.py:268
  116.0 0.9 multiply_reduce_fusion.10
  117.3 3.5 %fusion.4 = f32[960,4,128]{2,0,1:T(8,128)S(1)} fusion(s32[1024]{0:T(1024)S(1)} %get-tuple-element.98, pred[1024]{0:T(1024)(128)(4,1)S(1)} %get-tuple-element.95, f32[1024,128]{0,1:T(8,128)S(1)} %fusion.246, f32[1024,4]{0,1:T(4,128)S(1)} %divide_bitcast_fusion), kind=kOutput, calls=%fused_computation.73 | convolution fusion | flops 6042288128 | bytes 2511872 | tf_op jit(solution)/shard_map/dot_general | solution.py:424
  122.7 2.2 %multiply_add_fusion.3 = (f32[4,20,48,128]{3,2,1,0:T(8,128)S(1)}, f32[4,20,48,128]{3,2,1,0:T(8,128)S(1)}) fusion(f32[4,20,48,128]{3,2,1,0:T(8,128)S(1)} %bitcast.66, f32[4,20,48,128]{3,2,1,0:T(8,128)S(1)} %broadcast_multiply_fusion, f32[20,48,128]{2,1,0:T(8,128)S(1)} %copy-done.11, f32[20,48,128]{2,1,0:T(8,128)S(1)} %copy-done.3, ...), kind=kLoop, calls=%fused_computation.299 | loop fusion | flops 11304960 | bytes 11304960 | tf_op jit(solution)/shard_map/add | solution.py:340
  125.0 2.3 %multiply_add_fusion.2 = (f32[4,20,48,128]{3,2,1,0:T(8,128)S(1)}, f32[4,20,48,128]{3,2,1,0:T(8,128)S(1)}) fusion(f32[4,20,48,128]{3,2,1,0:T(8,128)S(1)} %get-tuple-element.38, f32[4,20,48,128]{3,2,1,0:T(8,128)S(1)} %get-tuple-element.39, f32[20,48,128]{2,1,0:T(8,128)S(1)} %copy-done.11, f32[20,48,128]{2,1,0:T(8,128)S(1)} %copy-done.3, ...), kind=kLoop, calls=%fused_computation.298 | loop fusion | flops 11304960 | bytes 11304960 | tf_op jit(solution)/shard_map/add | solution.py:340
  127.3 2.3 %multiply_add_fusion.1 = (f32[4,20,48,128]{3,2,1,0:T(8,128)S(1)}, f32[4,20,48,128]{3,2,1,0:T(8,128)S(1)}) fusion(f32[4,20,48,128]{3,2,1,0:T(8,128)S(1)} %get-tuple-element.36, f32[4,20,48,128]{3,2,1,0:T(8,128)S(1)} %get-tuple-element.37, f32[20,48,128]{2,1,0:T(8,128)S(1)} %copy-done.11, f32[20,48,128]{2,1,0:T(8,128)S(1)} %copy-done.3, ...), kind=kLoop, calls=%fused_computation.297 | loop fusion | flops 11304960 | bytes 11304960 | tf_op jit(solution)/shard_map/add | solution.py:340
  129.6 2.3 %multiply_add_fusion = (f32[4,20,48,128]{3,2,1,0:T(8,128)S(1)}, f32[4,20,48,128]{3,2,1,0:T(8,128)S(1)}) fusion(f32[4,20,48,128]{3,2,1,0:T(8,128)S(1)} %get-tuple-element.34, f32[4,20,48,128]{3,2,1,0:T(8,128)S(1)} %get-tuple-element.35, f32[20,48,128]{2,1,0:T(8,128)S(1)} %copy-done.11, f32[20,48,128]{2,1,0:T(8,128)S(1)} %copy-done.3, ...), kind=kLoop, calls=%fused_computation.296 | loop fusion | flops 11304960 | bytes 11304960 | tf_op jit(solution)/shard_map/add | solution.py:340
  132.0 3.3 %fusion.205 = f32[4,20,48,128]{3,2,1,0:T(8,128)S(1)} fusion(f32[4,20,48,128]{3,2,1,0:T(8,128)S(1)} %get-tuple-element.33, f32[4,20,48,128]{3,2,1,0:T(8,128)S(1)} %get-tuple-element.32, f32[4,20,48,128]{3,2,1,0:T(8,128)S(1)} %get-tuple-element.34, f32[4,20,48,128]{3,2,1,0:T(8,128)S(1)} %get-tuple-element.36, f32[4,20,48,128]{3,2,1,0:T(8,128)S(1)} %get-tuple-element.38, ...), kind=kLoop, calls=%fused_computation.285 | loop fusion | flops 14254080 | bytes 17203200 | tf_op jit(solution)/shard_map/add | solution.py:336
  135.5 0.9 copy-done.18
  136.3 1.4 fusion.225
  138.1 1.4 copy.43
  139.6 1.3 copy.44
  141.0 2.5 %multiply_reduce_fusion.1 = (f32[]{:T(128)}, f32[]{:T(128)}) fusion(f32[1,8,32,8,16]{4,2,1,0,3:T(8,128)} %copy.44, f32[2,8,32,8,16]{4,2,1,0,3:T(8,128)S(1)} %bitcast.64, f32[1,8,32,8,16]{4,2,1,0,3:T(8,128)} %copy.43), kind=kLoop, calls=%fused_computation.312 | loop fusion | flops 131070 | bytes 524296 | tf_op jit(solution)/shard_map/reduce_sum | solution.py:437
  149.4 1.2 reshape.404.refs_0_
  150.6 23.3 %shard_map.124 = (f32[64,128]{1,0:T(8,128)}, f32[8,128]{1,0:T(8,128)}) custom-call(f32[8,64,128]{2,1,0:T(8,128)} %reshape.404.refs_0_, f32[8,128]{1,0:T(8,128)} %fusion.274.refs_1_), custom_call_target="tpu_custom_call" | custom-call | tf_op jit(solution)/shard_map/pallas_call | solution.py:268
  174.7 1.4 fusion.294
  182.4 16.4 %shard_map.125 = f32[8,128]{1,0:T(8,128)} custom-call(f32[8,128]{1,0:T(8,128)} %pad_bitcast_fusion.refs_0_), custom_call_target="tpu_custom_call" | custom-call | tf_op jit(solution)/shard_map/pallas_call | solution.py:268
  198.9 1.2 slice.466
  (126 shorter events, 19.5 us)
Async XLA Ops:
  20.9 1.7 copy-start.14
  22.6 2.3 %copy-start.26 = (s32[8,32,128]{2,1,0:T(8,128)S(1)}, s32[8,32,128]{2,1,0:T(8,128)}, u32[]{:S(2)}) copy-start(s32[8,32,128]{2,1,0:T(8,128)} %param.10) | copy-start | bytes 393220
  24.2 1.1 copy-start.16
  48.3 0.7 copy-start.28
  48.3 0.7 copy-start.29
  52.2 3.3 %copy-start.19 = (f32[20,48,128]{2,1,0:T(8,128)}, f32[20,48,128]{2,1,0:T(8,128)S(1)}, u32[]{:S(2)}) copy-start(f32[20,48,128]{2,1,0:T(8,128)S(1)} %get-tuple-element.48) | copy-start | bytes 1474564
  52.2 12.5 %copy-start.12 = (f32[20,48,128]{2,1,0:T(8,128)}, f32[20,48,128]{2,1,0:T(8,128)S(1)}, u32[]{:S(2)}) copy-start(f32[20,48,128]{2,1,0:T(8,128)S(1)} %get-tuple-element.49) | copy-start | bytes 1474564
  53.1 11.6 %copy-start = (f32[20,48,128]{2,1,0:T(8,128)}, f32[20,48,128]{2,1,0:T(8,128)S(1)}, u32[]{:S(2)}) copy-start(f32[20,48,128]{2,1,0:T(8,128)S(1)} %get-tuple-element.67) | copy-start | bytes 1474564
  53.1 11.6 %copy-start.2 = (f32[20,48,128]{2,1,0:T(8,128)}, f32[20,48,128]{2,1,0:T(8,128)S(1)}, u32[]{:S(2)}) copy-start(f32[20,48,128]{2,1,0:T(8,128)S(1)} %get-tuple-element.68) | copy-start | bytes 1474564
  53.1 11.6 %copy-start.4 = (f32[20,48,128]{2,1,0:T(8,128)}, f32[20,48,128]{2,1,0:T(8,128)S(1)}, u32[]{:S(2)}) copy-start(f32[20,48,128]{2,1,0:T(8,128)S(1)} %get-tuple-element.69) | copy-start | bytes 1474564
  53.1 11.6 %copy-start.6 = (f32[20,48,128]{2,1,0:T(8,128)}, f32[20,48,128]{2,1,0:T(8,128)S(1)}, u32[]{:S(2)}) copy-start(f32[20,48,128]{2,1,0:T(8,128)S(1)} %get-tuple-element.70) | copy-start | bytes 1474564
  53.2 11.6 %copy-start.8 = (f32[20,48,128]{2,1,0:T(8,128)}, f32[20,48,128]{2,1,0:T(8,128)S(1)}, u32[]{:S(2)}) copy-start(f32[20,48,128]{2,1,0:T(8,128)S(1)} %get-tuple-element.71) | copy-start | bytes 1474564
  53.2 13.6 %copy-start.10 = (f32[20,48,128]{2,1,0:T(8,128)}, f32[20,48,128]{2,1,0:T(8,128)S(1)}, u32[]{:S(2)}) copy-start(f32[20,48,128]{2,1,0:T(8,128)S(1)} %get-tuple-element.72) | copy-start | bytes 1474564
  66.8 1.0 copy-start.17
  67.9 1.1 copy-start.27
  120.8 1.0 copy-start.1
  120.8 1.2 copy-start.3
  120.8 1.3 copy-start.5
  120.8 1.5 copy-start.7
  120.8 1.6 copy-start.9
  120.8 1.7 copy-start.11
  120.8 1.9 copy-start.20
  122.7 2.3 %copy-start.13 = (f32[20,48,128]{2,1,0:T(8,128)S(1)}, f32[20,48,128]{2,1,0:T(8,128)}, u32[]{:S(2)}) copy-start(f32[20,48,128]{2,1,0:T(8,128)} %copy-done.12) | copy-start | bytes 1474564
  135.3 1.0 copy-start.18
  137.8 1.6 copy-start.23
  138.1 2.9 %copy-start.15 = (f32[8,2,8,32,16]{4,3,2,1,0:T(8,128)S(1)}, f32[8,2,8,32,16]{4,3,2,1,0:T(8,128)}, u32[]{:S(2)}) copy-start(f32[8,2,8,32,16]{4,3,2,1,0:T(8,128)} %copy-done.14) | copy-start | bytes 786436
  141.0 3.8 %copy-start.21 = (f32[8,32,16]{1,2,0:T(8,128)S(1)}, f32[8,32,16]{1,2,0:T(8,128)}, u32[]{:S(2)}) copy-start(f32[8,32,16]{1,2,0:T(8,128)} %param.16) | copy-start | bytes 49156
  141.0 3.8 %copy-start.22 = (f32[8,32,16]{1,2,0:T(8,128)S(1)}, f32[8,32,16]{1,2,0:T(8,128)}, u32[]{:S(2)}) copy-start(f32[8,32,16]{1,2,0:T(8,128)} %param.15) | copy-start | bytes 49156
  141.0 3.8 %copy-start.24 = (f32[8,32,16]{1,2,0:T(8,128)S(1)}, f32[8,32,16]{1,2,0:T(8,128)}, u32[]{:S(2)}) copy-start(f32[8,32,16]{1,2,0:T(8,128)} %param.18) | copy-start | bytes 49156
  141.0 3.8 %copy-start.25 = (f32[8,32,16]{1,2,0:T(8,128)S(1)}, f32[8,32,16]{1,2,0:T(8,128)}, u32[]{:S(2)}) copy-start(f32[8,32,16]{1,2,0:T(8,128)} %param.17) | copy-start | bytes 49156

commit v13 on v12

--- a/solution.py
+++ b/solution.py
@@ -62,12 +62,15 @@
     )(x)
 
 
-def _halo_kernel(hx, hy, x_ref, o_ref, wide, send_sem, recv_sem, local_sem):
+def _halo_kernel(hx, hy, own_fields, x_ref, o_ref, wide, send_sem, recv_sem, local_sem, fwd_send, fwd_recv):
     fields, cx, cy, cz = x_ref.shape
     ax, ay = lax.axis_index("gx"), lax.axis_index("gy")
     nx, ny = lax.axis_size("gx"), lax.axis_size("gy")
+    me_src = lax.axis_index("src")
+    half = me_src % 2
+    partner = me_src + 1 - 2 * half
     wide[...] = jnp.zeros_like(wide)
-    steps = [(dx, dy) for dx in (-1, 0, 1) for dy in (-1, 0, 1) if (dx, dy) != (0, 0)]
+    steps = [(-1, 0), (1, 0), (0, -1), (0, 1), (-1, -1), (-1, 1), (1, -1), (1, 1)]
 
     def exists(dx, dy):
         return (ax + dx >= 0) & (ax + dx < nx) & (ay + dy >= 0) & (ay + dy < ny)
@@ -86,66 +89,95 @@
             pl.semaphore_signal(
                 barrier, inc=1, device_id={"gx": ax + dx, "gy": ay + dy}, device_id_type=MESH
             )
+    pl.semaphore_signal(barrier, inc=1, device_id={"src": partner}, device_id_type=MESH)
     across = 1 + (ax + nx - 1) // nx + (2 * nx - 2 - ax) // nx
     along = 1 + (ay + ny - 1) // ny + (2 * ny - 2 - ay) // ny
-    pl.semaphore_wait(barrier, across * along - 1)
+    pl.semaphore_wait(barrier, across * along)
 
     local = pltpu.make_async_copy(
         x_ref, wide.at[:, pl.ds(hx, cx), pl.ds(hy, cy), :], local_sem
     )
     local.start()
-    copies = []
+    direct, relayed = [], []
     for k, (dx, dy) in enumerate(steps):
         src_x, dst_x = window(dx, cx, hx)
         src_y, dst_y = window(dy, cy, hy)
         tx = jnp.clip(ax + dx, 0, nx - 1)
         ty = jnp.clip(ay + dy, 0, ny - 1)
-        copy = pltpu.make_async_remote_copy(
-            src_ref=x_ref.at[:, src_x, src_y, :],
-            dst_ref=wide.at[:, dst_x, dst_y, :],
-            send_sem=send_sem.at[k],
-            recv_sem=recv_sem.at[k],
-            device_id={"gx": tx, "gy": ty},
-            device_id_type=MESH,
-        )
-        copies.append(copy)
-
-        @pl.when(exists(dx, dy))
-        def _():
-            copy.start()
+        for f in range(fields):
+            slot = k * fields + f
+            copy = pltpu.make_async_remote_copy(
+                src_ref=x_ref.at[f, src_x, src_y, :],
+                dst_ref=wide.at[f, dst_x, dst_y, :],
+                send_sem=send_sem.at[slot],
+                recv_sem=recv_sem.at[slot],
+                device_id={"gx": tx, "gy": ty},
+                device_id_type=MESH,
+            )
+            relay = None if f < own_fields else pltpu.make_async_remote_copy(
+                src_ref=wide.at[f, dst_x, dst_y, :],
+                dst_ref=wide.at[f, dst_x, dst_y, :],
+                send_sem=fwd_send.at[slot],
+                recv_sem=fwd_recv.at[slot],
+                device_id={"src": partner},
+                device_id_type=MESH,
+            )
+            mine = True if f < own_fields else ((f - own_fields) % 2 == half)
+            direct.append((copy, relay, dx, dy, f, mine))
+
+            @pl.when(exists(dx, dy) & mine)
+            def _():
+                copy.start()
 
     local.wait()
-    for copy, (dx, dy) in zip(copies, steps):
-        @pl.when(exists(dx, dy))
+    for copy, relay, dx, dy, f, mine in direct:
+        if f >= own_fields:
+            @pl.when(exists(-dx, -dy) & mine)
+            def _():
+                copy.wait_recv()
+                relay.start()
+    for copy, relay, dx, dy, f, mine in direct:
+        @pl.when(exists(dx, dy) & mine)
         def _():
             copy.wait_send()
 
-        @pl.when(exists(-dx, -dy))
-        def _():
-            copy.wait_recv()
+        if f < own_fields:
+            @pl.when(exists(-dx, -dy))
+            def _():
+                copy.wait_recv()
+        else:
+            @pl.when(exists(-dx, -dy) & mine)
+            def _():
+                relay.wait_send()
+
+            @pl.when(exists(-dx, -dy) & jnp.logical_not(mine))
+            def _():
+                relay.wait_recv()
 
     o_ref[...] = wide[...]
 
 
-def halo_block(x, hx, hy, cid):
+def halo_block(x, hx, hy, cid, own_fields=None):
     fields, cx, cy, cz = x.shape
+    own_fields = fields if own_fields is None else own_fields
     shape = (fields, cx + 2 * hx, cy + 2 * hy, cz)
     return pl.pallas_call(
-        functools.partial(_halo_kernel, hx, hy),
+        functools.partial(_halo_kernel, hx, hy, own_fields),
         out_shape=jax.ShapeDtypeStruct(shape, x.dtype),
         in_specs=[pl.BlockSpec(memory_space=pltpu.VMEM)],
         out_specs=pl.BlockSpec(memory_space=pltpu.VMEM),
         scratch_shapes=[
             pltpu.VMEM(shape, x.dtype),
-            pltpu.SemaphoreType.DMA((8,)),
-            pltpu.SemaphoreType.DMA((8,)),
+            pltpu.SemaphoreType.DMA((8 * fields,)),
+            pltpu.SemaphoreType.DMA((8 * fields,)),
             pltpu.SemaphoreType.DMA,
+            pltpu.SemaphoreType.DMA((8 * fields,)),
+            pltpu.SemaphoreType.DMA((8 * fields,)),
         ],
         compiler_params=pltpu.CompilerParams(
             collective_id=cid, has_side_effects=True, vmem_limit_bytes=48 * 1024 * 1024
         ),
     )(x)
-
 
 def _group(axes):
     sizes = [lax.axis_size(axis) for axis in axes]
@@ -364,7 +396,7 @@
     width_y = 8
     region_of = labels.astype(jnp.float32)[None]
     stacked = jnp.concatenate([background, region_of, full_k[None], full_a[None]], axis=0)
-    wide = halo_block(stacked, width, width_y, 10)
+    wide = halo_block(stacked, width, width_y, 10, own_fields=sources)
     phi_w, region_w, vk_w, va_w = wide[:sources], wide[sources], wide[sources + 1], wide[sources + 2]
     wx = cx + 2 * width
     wy = cy + 2 * width_y

time: 204 us -> 196 us (0.961)
  Pallas kernels: 121 us -> 113 us
    pallas_call x3, Pallas kernels: 80.8 us -> 57.4 us  [small_sum(): pl.pallas_call(functools.partial(_reduce_kernel, stages, spread is not No...]
    pallas_call x1, Pallas kernels: 23 us -> 38.5 us  [halo_block(): pl.pallas_call(functools.partial(_halo_kernel, hx, hy, own_fields), out_s...]
where the time goes in v13:
time: 196 us; the launch traced here: 195 us
  Pallas kernels  113 us (58%)
  other arithmetic  39.2 us (20%)
  local copies, waits for them, and re-layouts  24.2 us (12%)
  between operations  9.8 us (5%)
  matrix products  9.14 us (5%)
    pallas_call x3, Pallas kernels, small_sum(): pl.pallas_call(functools.partial(_reduce_kernel, stages, spread is not No...  57.4 us
    pallas_call x1, Pallas kernels, halo_block(): pl.pallas_call(functools.partial(_halo_kernel, hx, hy, own_fields), out_s...  38.5 us
    add x8, other arithmetic, chebyshev(): step_dir = rho_next * rho * step_dir + 2.0 * rho_next / delta * remain  18.7 us
    pallas_call x1, Pallas kernels, exchange(): pl.pallas_call(functools.partial(_exchange_kernel, axis, n, scatter), out...  16.7 us
    unnamed x66, local copies, waits for them, and re-layouts  6.31 us

profile of v13, /device:TPU:1, one launch (start us, length us, event | category | flops | bytes accessed | tf_op | source)
XLA Modules:
  0.0 195.0 jit_solution(15621970212342675748)
XLA Ops:
  2.5 16.7 %shard_map.121 = f32[8,64,128]{2,1,0:T(8,128)} custom-call(f32[64,128]{1,0:T(8,128)} %reshape.399.x_ref), custom_call_target="tpu_custom_call" | custom-call | tf_op jit(solution)/shard_map/pallas_call | solution.py:50
  19.2 1.7 reshape.400
  20.9 1.5 fusion.291
  22.6 1.6 copy.35
  25.3 38.5 %shard_map.122 = f32[7,20,48,128]{3,2,1,0:T(8,128)S(1)} custom-call(f32[7,8,32,128]{3,2,1,0:T(8,128)S(1)} %pad_maximum_fusion.1.x_ref), custom_call_target="tpu_custom_call" | custom-call | tf_op jit(solution)/shard_map/pallas_call | solution.py:164
  64.5 2.3 %fusion = f32[2,122880]{1,0:T(2,128)S(1)} fusion(f32[122880]{0:T(1024)S(1)} %bitcast.79, f32[1,16]{1,0:T(1,128)S(1)} %bitcast.82, f32[1,16]{1,0:T(1,128)S(1)} %bitcast.83), kind=kOutput, calls=%fused_computation.67 | convolution fusion | flops 49152032 | bytes 1474688 | tf_op jit(solution)/shard_map/dot_general | solution.py:412
  68.9 2.2 %broadcast_multiply_fusion.1 = (f32[4,20,48,128]{3,2,1,0:T(8,128)S(1)}, f32[4,20,48,128]{3,2,1,0:T(8,128)S(1)}) fusion(f32[4,20,48,128]{3,2,1,0:T(8,128)S(1)} %slice.359, f32[20,48,128]{2,1,0:T(8,128)S(1)} %get-tuple-element.85, f32[20,48,128]{2,1,0:T(8,128)S(1)} %get-tuple-element.89, f32[20,48,128]{2,1,0:T(8,128)S(1)} %get-tuple-element.88, ...), kind=kLoop, calls=%fused_computation.320 | loop fusion | flops 10321920 | bytes 9338880 | tf_op jit(solution)/shard_map/div | solution.py:366
  71.0 2.3 %multiply_add_fusion.7 = (f32[4,20,48,128]{3,2,1,0:T(8,128)S(1)}, f32[4,20,48,128]{3,2,1,0:T(8,128)S(1)}) fusion(f32[4,20,48,128]{3,2,1,0:T(8,128)S(1)} %get-tuple-element.51, f32[4,20,48,128]{3,2,1,0:T(8,128)S(1)} %get-tuple-element.50, f32[20,48,128]{2,1,0:T(8,128)S(1)} %get-tuple-element.72, f32[20,48,128]{2,1,0:T(8,128)S(1)} %get-tuple-element.68, ...), kind=kLoop, calls=%fused_computation.303 | loop fusion | flops 11304960 | bytes 11304960 | tf_op jit(solution)/shard_map/add | solution.py:372
  73.4 2.3 %multiply_add_fusion.6 = (f32[4,20,48,128]{3,2,1,0:T(8,128)S(1)}, f32[4,20,48,128]{3,2,1,0:T(8,128)S(1)}) fusion(f32[4,20,48,128]{3,2,1,0:T(8,128)S(1)} %get-tuple-element.46, f32[4,20,48,128]{3,2,1,0:T(8,128)S(1)} %get-tuple-element.47, f32[20,48,128]{2,1,0:T(8,128)S(1)} %get-tuple-element.72, f32[20,48,128]{2,1,0:T(8,128)S(1)} %get-tuple-element.68, ...), kind=kLoop, calls=%fused_computation.302 | loop fusion | flops 11304960 | bytes 11304960 | tf_op jit(solution)/shard_map/add | solution.py:372
  75.7 2.3 %multiply_add_fusion.5 = (f32[4,20,48,128]{3,2,1,0:T(8,128)S(1)}, f32[4,20,48,128]{3,2,1,0:T(8,128)S(1)}) fusion(f32[4,20,48,128]{3,2,1,0:T(8,128)S(1)} %get-tuple-element.44, f32[4,20,48,128]{3,2,1,0:T(8,128)S(1)} %get-tuple-element.45, f32[20,48,128]{2,1,0:T(8,128)S(1)} %get-tuple-element.72, f32[20,48,128]{2,1,0:T(8,128)S(1)} %get-tuple-element.68, ...), kind=kLoop, calls=%fused_computation.301 | loop fusion | flops 11304960 | bytes 11304960 | tf_op jit(solution)/shard_map/add | solution.py:372
  77.9 2.3 %multiply_add_fusion.4 = (f32[4,20,48,128]{3,2,1,0:T(8,128)S(1)}, f32[4,20,48,128]{3,2,1,0:T(8,128)S(1)}) fusion(f32[4,20,48,128]{3,2,1,0:T(8,128)S(1)} %get-tuple-element.42, f32[4,20,48,128]{3,2,1,0:T(8,128)S(1)} %get-tuple-element.43, f32[20,48,128]{2,1,0:T(8,128)S(1)} %get-tuple-element.72, f32[20,48,128]{2,1,0:T(8,128)S(1)} %get-tuple-element.68, ...), kind=kLoop, calls=%fused_computation.300 | loop fusion | flops 11304960 | bytes 11304960 | tf_op jit(solution)/shard_map/add | solution.py:372
  80.3 2.0 %fusion.108 = (f32[4,20,48,128]{3,2,1,0:T(8,128)S(1)}, f32[4,20,48,128]{3,2,1,0:T(8,128)S(1)}, f32[4,20,48,128]{3,2,1,0:T(8,128)S(1)}) fusion(f32[4,20,48,128]{3,2,1,0:T(8,128)S(1)} %get-tuple-element.40, f32[20,48,128]{2,1,0:T(8,128)S(1)} %get-tuple-element.49, f32[20,48,128]{2,1,0:T(8,128)S(1)} %get-tuple-element.69, ...), kind=kLoop, calls=%fused_computation.188 | loop fusion | flops 7864320 | bytes 10813440 | tf_op jit(solution)/shard_map/add | solution.py:420
  83.4 1.1 pad_maximum_fusion
  84.6 3.4 %multiply_reduce_fusion = f32[8,1024]{1,0:T(8,128)S(1)} fusion(f32[8,256,128]{2,1,0:T(8,128)} %bitcast.76, f32[128,1024]{1,0:T(8,128)S(1)} %fusion.245, s32[1024]{0:T(1024)S(1)} %get-tuple-element.96, pred[1024]{0:T(1024)(128)(4,1)S(1)} %get-tuple-element.94), kind=kOutput, calls=%fused_computation.68 | convolution fusion | flops 3223838720 | bytes 1610752 | tf_op jit(solution)/shard_map/spz,pd->szd/dot_general | solution.py:439
  88.6 17.2 %shard_map.123 = f32[64,128]{1,0:T(8,128)} custom-call(f32[64,128]{1,0:T(8,128)} %reshape.402.refs_0_), custom_call_target="tpu_custom_call" | custom-call | tf_op jit(solution)/shard_map/pallas_call | solution.py:300
  107.6 0.9 multiply_reduce_fusion.10
  108.9 3.5 %fusion.4 = f32[960,4,128]{2,0,1:T(8,128)S(1)} fusion(s32[1024]{0:T(1024)S(1)} %get-tuple-element.98, pred[1024]{0:T(1024)(128)(4,1)S(1)} %get-tuple-element.95, f32[1024,128]{0,1:T(8,128)S(1)} %fusion.246, f32[1024,4]{0,1:T(4,128)S(1)} %divide_bitcast_fusion), kind=kOutput, calls=%fused_computation.73 | convolution fusion | flops 6042288128 | bytes 2511872 | tf_op jit(solution)/shard_map/dot_general | solution.py:456
  114.3 2.2 %multiply_add_fusion.3 = (f32[4,20,48,128]{3,2,1,0:T(8,128)S(1)}, f32[4,20,48,128]{3,2,1,0:T(8,128)S(1)}) fusion(f32[4,20,48,128]{3,2,1,0:T(8,128)S(1)} %bitcast.66, f32[4,20,48,128]{3,2,1,0:T(8,128)S(1)} %broadcast_multiply_fusion, f32[20,48,128]{2,1,0:T(8,128)S(1)} %copy-done.11, f32[20,48,128]{2,1,0:T(8,128)S(1)} %copy-done.3, ...), kind=kLoop, calls=%fused_computation.299 | loop fusion | flops 11304960 | bytes 11304960 | tf_op jit(solution)/shard_map/add | solution.py:372
  116.6 2.3 %multiply_add_fusion.2 = (f32[4,20,48,128]{3,2,1,0:T(8,128)S(1)}, f32[4,20,48,128]{3,2,1,0:T(8,128)S(1)}) fusion(f32[4,20,48,128]{3,2,1,0:T(8,128)S(1)} %get-tuple-element.38, f32[4,20,48,128]{3,2,1,0:T(8,128)S(1)} %get-tuple-element.39, f32[20,48,128]{2,1,0:T(8,128)S(1)} %copy-done.11, f32[20,48,128]{2,1,0:T(8,128)S(1)} %copy-done.3, ...), kind=kLoop, calls=%fused_computation.298 | loop fusion | flops 11304960 | bytes 11304960 | tf_op jit(solution)/shard_map/add | solution.py:372
  118.9 2.3 %multiply_add_fusion.1 = (f32[4,20,48,128]{3,2,1,0:T(8,128)S(1)}, f32[4,20,48,128]{3,2,1,0:T(8,128)S(1)}) fusion(f32[4,20,48,128]{3,2,1,0:T(8,128)S(1)} %get-tuple-element.36, f32[4,20,48,128]{3,2,1,0:T(8,128)S(1)} %get-tuple-element.37, f32[20,48,128]{2,1,0:T(8,128)S(1)} %copy-done.11, f32[20,48,128]{2,1,0:T(8,128)S(1)} %copy-done.3, ...), kind=kLoop, calls=%fused_computation.297 | loop fusion | flops 11304960 | bytes 11304960 | tf_op jit(solution)/shard_map/add | solution.py:372
  121.2 2.6 %multiply_add_fusion = (f32[4,20,48,128]{3,2,1,0:T(8,128)S(1)}, f32[4,20,48,128]{3,2,1,0:T(8,128)S(1)}) fusion(f32[4,20,48,128]{3,2,1,0:T(8,128)S(1)} %get-tuple-element.34, f32[4,20,48,128]{3,2,1,0:T(8,128)S(1)} %get-tuple-element.35, f32[20,48,128]{2,1,0:T(8,128)S(1)} %copy-done.11, f32[20,48,128]{2,1,0:T(8,128)S(1)} %copy-done.3, ...), kind=kLoop, calls=%fused_computation.296 | loop fusion | flops 11304960 | bytes 11304960 | tf_op jit(solution)/shard_map/add | solution.py:372
  123.8 3.0 %fusion.205 = f32[4,20,48,128]{3,2,1,0:T(8,128)S(1)} fusion(f32[4,20,48,128]{3,2,1,0:T(8,128)S(1)} %get-tuple-element.33, f32[4,20,48,128]{3,2,1,0:T(8,128)S(1)} %get-tuple-element.32, f32[4,20,48,128]{3,2,1,0:T(8,128)S(1)} %get-tuple-element.34, f32[4,20,48,128]{3,2,1,0:T(8,128)S(1)} %get-tuple-element.36, f32[4,20,48,128]{3,2,1,0:T(8,128)S(1)} %get-tuple-element.38, ...), kind=kLoop, calls=%fused_computation.285 | loop fusion | flops 14254080 | bytes 17203200 | tf_op jit(solution)/shard_map/add | solution.py:368
  127.1 0.9 copy-done.18
  127.9 1.4 fusion.225
  129.7 1.4 copy.43
  131.2 1.3 copy.44
  132.6 2.5 %multiply_reduce_fusion.1 = (f32[]{:T(128)}, f32[]{:T(128)}) fusion(f32[1,8,32,8,16]{4,2,1,0,3:T(8,128)} %copy.44, f32[2,8,32,8,16]{4,2,1,0,3:T(8,128)S(1)} %bitcast.64, f32[1,8,32,8,16]{4,2,1,0,3:T(8,128)} %copy.43), kind=kLoop, calls=%fused_computation.312 | loop fusion | flops 131070 | bytes 524296 | tf_op jit(solution)/shard_map/reduce_sum | solution.py:469
  141.0 1.2 reshape.404.refs_0_
  142.2 24.0 %shard_map.124 = (f32[64,128]{1,0:T(8,128)}, f32[8,128]{1,0:T(8,128)}) custom-call(f32[8,64,128]{2,1,0:T(8,128)} %reshape.404.refs_0_, f32[8,128]{1,0:T(8,128)} %fusion.274.refs_1_), custom_call_target="tpu_custom_call" | custom-call | tf_op jit(solution)/shard_map/pallas_call | solution.py:300
  167.0 1.4 fusion.294
  174.7 16.2 %shard_map.125 = f32[8,128]{1,0:T(8,128)} custom-call(f32[8,128]{1,0:T(8,128)} %pad_bitcast_fusion.refs_0_), custom_call_target="tpu_custom_call" | custom-call | tf_op jit(solution)/shard_map/pallas_call | solution.py:300
  191.0 1.2 slice.466
  (126 shorter events, 19.5 us)
Async XLA Ops:
  20.9 1.7 copy-start.14
  22.6 2.3 %copy-start.26 = (s32[8,32,128]{2,1,0:T(8,128)S(1)}, s32[8,32,128]{2,1,0:T(8,128)}, u32[]{:S(2)}) copy-start(s32[8,32,128]{2,1,0:T(8,128)} %param.10) | copy-start | bytes 393220
  24.2 1.1 copy-start.16
  63.8 0.7 copy-start.28
  63.8 0.7 copy-start.29
  67.8 3.3 %copy-start.19 = (f32[20,48,128]{2,1,0:T(8,128)}, f32[20,48,128]{2,1,0:T(8,128)S(1)}, u32[]{:S(2)}) copy-start(f32[20,48,128]{2,1,0:T(8,128)S(1)} %get-tuple-element.48) | copy-start | bytes 1474564
  67.8 12.5 %copy-start.12 = (f32[20,48,128]{2,1,0:T(8,128)}, f32[20,48,128]{2,1,0:T(8,128)S(1)}, u32[]{:S(2)}) copy-start(f32[20,48,128]{2,1,0:T(8,128)S(1)} %get-tuple-element.49) | copy-start | bytes 1474564
  68.6 11.6 %copy-start = (f32[20,48,128]{2,1,0:T(8,128)}, f32[20,48,128]{2,1,0:T(8,128)S(1)}, u32[]{:S(2)}) copy-start(f32[20,48,128]{2,1,0:T(8,128)S(1)} %get-tuple-element.67) | copy-start | bytes 1474564
  68.7 11.6 %copy-start.2 = (f32[20,48,128]{2,1,0:T(8,128)}, f32[20,48,128]{2,1,0:T(8,128)S(1)}, u32[]{:S(2)}) copy-start(f32[20,48,128]{2,1,0:T(8,128)S(1)} %get-tuple-element.68) | copy-start | bytes 1474564
  68.7 11.6 %copy-start.4 = (f32[20,48,128]{2,1,0:T(8,128)}, f32[20,48,128]{2,1,0:T(8,128)S(1)}, u32[]{:S(2)}) copy-start(f32[20,48,128]{2,1,0:T(8,128)S(1)} %get-tuple-element.69) | copy-start | bytes 1474564
  68.7 11.6 %copy-start.6 = (f32[20,48,128]{2,1,0:T(8,128)}, f32[20,48,128]{2,1,0:T(8,128)S(1)}, u32[]{:S(2)}) copy-start(f32[20,48,128]{2,1,0:T(8,128)S(1)} %get-tuple-element.70) | copy-start | bytes 1474564
  68.7 11.6 %copy-start.8 = (f32[20,48,128]{2,1,0:T(8,128)}, f32[20,48,128]{2,1,0:T(8,128)S(1)}, u32[]{:S(2)}) copy-start(f32[20,48,128]{2,1,0:T(8,128)S(1)} %get-tuple-element.71) | copy-start | bytes 1474564
  68.7 13.6 %copy-start.10 = (f32[20,48,128]{2,1,0:T(8,128)}, f32[20,48,128]{2,1,0:T(8,128)S(1)}, u32[]{:S(2)}) copy-start(f32[20,48,128]{2,1,0:T(8,128)S(1)} %get-tuple-element.72) | copy-start | bytes 1474564
  82.3 1.0 copy-start.17
  83.4 1.1 copy-start.27
  112.4 1.0 copy-start.1
  112.4 1.2 copy-start.3
  112.4 1.3 copy-start.5
  112.4 1.5 copy-start.7
  112.4 1.6 copy-start.9
  112.4 1.7 copy-start.11
  112.4 1.9 copy-start.20
  114.3 2.3 %copy-start.13 = (f32[20,48,128]{2,1,0:T(8,128)S(1)}, f32[20,48,128]{2,1,0:T(8,128)}, u32[]{:S(2)}) copy-start(f32[20,48,128]{2,1,0:T(8,128)} %copy-done.12) | copy-start | bytes 1474564
  126.9 1.0 copy-start.18
  129.4 1.6 copy-start.23
  129.7 2.9 %copy-start.15 = (f32[8,2,8,32,16]{4,3,2,1,0:T(8,128)S(1)}, f32[8,2,8,32,16]{4,3,2,1,0:T(8,128)}, u32[]{:S(2)}) copy-start(f32[8,2,8,32,16]{4,3,2,1,0:T(8,128)} %copy-done.14) | copy-start | bytes 786436
  132.6 3.8 %copy-start.21 = (f32[8,32,16]{1,2,0:T(8,128)S(1)}, f32[8,32,16]{1,2,0:T(8,128)}, u32[]{:S(2)}) copy-start(f32[8,32,16]{1,2,0:T(8,128)} %param.16) | copy-start | bytes 49156
  132.6 3.8 %copy-start.22 = (f32[8,32,16]{1,2,0:T(8,128)S(1)}, f32[8,32,16]{1,2,0:T(8,128)}, u32[]{:S(2)}) copy-start(f32[8,32,16]{1,2,0:T(8,128)} %param.15) | copy-start | bytes 49156
  132.6 3.8 %copy-start.24 = (f32[8,32,16]{1,2,0:T(8,128)S(1)}, f32[8,32,16]{1,2,0:T(8,128)}, u32[]{:S(2)}) copy-start(f32[8,32,16]{1,2,0:T(8,128)} %param.18) | copy-start | bytes 49156
  132.6 3.8 %copy-start.25 = (f32[8,32,16]{1,2,0:T(8,128)S(1)}, f32[8,32,16]{1,2,0:T(8,128)}, u32[]{:S(2)}) copy-start(f32[8,32,16]{1,2,0:T(8,128)} %param.17) | copy-start | bytes 49156

commit v14 on v13

--- a/solution.py
+++ b/solution.py
@@ -101,6 +101,10 @@
     direct, relayed = [], []
     for k, (dx, dy) in enumerate(steps):
         src_x, dst_x = window(dx, cx, hx)
+        if dy != 0 and dx < 0:
+            src_x, dst_x = pl.ds(0, hx - 1), pl.ds(cx + hx, hx - 1)
+        if dy != 0 and dx > 0:
+            src_x, dst_x = pl.ds(cx - hx + 1, hx - 1), pl.ds(1, hx - 1)
         src_y, dst_y = window(dy, cy, hy)
         tx = jnp.clip(ax + dx, 0, nx - 1)
         ty = jnp.clip(ay + dy, 0, ny - 1)

time: 196 us -> 194 us (0.990)
  Pallas kernels: 113 us -> 111 us
where the time goes in v14:
time: 194 us; the launch traced here: 193 us
  Pallas kernels  111 us (57%)
  other arithmetic  39.2 us (20%)
  local copies, waits for them, and re-layouts  24.2 us (12%)
  between operations  9.8 us (5%)
  matrix products  9.14 us (5%)
    pallas_call x3, Pallas kernels, small_sum(): pl.pallas_call(functools.partial(_reduce_kernel, stages, spread is not No...  56 us
    pallas_call x1, Pallas kernels, halo_block(): pl.pallas_call(functools.partial(_halo_kernel, hx, hy, own_fields), out_s...  38 us
    add x8, other arithmetic, chebyshev(): step_dir = rho_next * rho * step_dir + 2.0 * rho_next / delta * remain  18.7 us
    pallas_call x1, Pallas kernels, exchange(): pl.pallas_call(functools.partial(_exchange_kernel, axis, n, scatter), out...  16.7 us
    unnamed x66, local copies, waits for them, and re-layouts  6.31 us

profile of v14, /device:TPU:1, one launch (start us, length us, event | category | flops | bytes accessed | tf_op | source)
XLA Modules:
  0.0 193.0 jit_solution(644636470253552572)
XLA Ops:
  2.5 16.7 %shard_map.121 = f32[8,64,128]{2,1,0:T(8,128)} custom-call(f32[64,128]{1,0:T(8,128)} %reshape.399.x_ref), custom_call_target="tpu_custom_call" | custom-call | tf_op jit(solution)/shard_map/pallas_call | solution.py:50
  19.2 1.7 reshape.400
  20.9 1.5 fusion.291
  22.6 1.6 copy.35
  25.3 38.0 %shard_map.122 = f32[7,20,48,128]{3,2,1,0:T(8,128)S(1)} custom-call(f32[7,8,32,128]{3,2,1,0:T(8,128)S(1)} %pad_maximum_fusion.1.x_ref), custom_call_target="tpu_custom_call" | custom-call | tf_op jit(solution)/shard_map/pallas_call | solution.py:168
  64.0 2.3 %fusion = f32[2,122880]{1,0:T(2,128)S(1)} fusion(f32[122880]{0:T(1024)S(1)} %bitcast.79, f32[1,16]{1,0:T(1,128)S(1)} %bitcast.82, f32[1,16]{1,0:T(1,128)S(1)} %bitcast.83), kind=kOutput, calls=%fused_computation.67 | convolution fusion | flops 49152032 | bytes 1474688 | tf_op jit(solution)/shard_map/dot_general | solution.py:416
  68.3 2.2 %broadcast_multiply_fusion.1 = (f32[4,20,48,128]{3,2,1,0:T(8,128)S(1)}, f32[4,20,48,128]{3,2,1,0:T(8,128)S(1)}) fusion(f32[4,20,48,128]{3,2,1,0:T(8,128)S(1)} %slice.359, f32[20,48,128]{2,1,0:T(8,128)S(1)} %get-tuple-element.85, f32[20,48,128]{2,1,0:T(8,128)S(1)} %get-tuple-element.89, f32[20,48,128]{2,1,0:T(8,128)S(1)} %get-tuple-element.88, ...), kind=kLoop, calls=%fused_computation.320 | loop fusion | flops 10321920 | bytes 9338880 | tf_op jit(solution)/shard_map/div | solution.py:370
  70.5 2.3 %multiply_add_fusion.7 = (f32[4,20,48,128]{3,2,1,0:T(8,128)S(1)}, f32[4,20,48,128]{3,2,1,0:T(8,128)S(1)}) fusion(f32[4,20,48,128]{3,2,1,0:T(8,128)S(1)} %get-tuple-element.51, f32[4,20,48,128]{3,2,1,0:T(8,128)S(1)} %get-tuple-element.50, f32[20,48,128]{2,1,0:T(8,128)S(1)} %get-tuple-element.72, f32[20,48,128]{2,1,0:T(8,128)S(1)} %get-tuple-element.68, ...), kind=kLoop, calls=%fused_computation.303 | loop fusion | flops 11304960 | bytes 11304960 | tf_op jit(solution)/shard_map/add | solution.py:376
  72.9 2.3 %multiply_add_fusion.6 = (f32[4,20,48,128]{3,2,1,0:T(8,128)S(1)}, f32[4,20,48,128]{3,2,1,0:T(8,128)S(1)}) fusion(f32[4,20,48,128]{3,2,1,0:T(8,128)S(1)} %get-tuple-element.46, f32[4,20,48,128]{3,2,1,0:T(8,128)S(1)} %get-tuple-element.47, f32[20,48,128]{2,1,0:T(8,128)S(1)} %get-tuple-element.72, f32[20,48,128]{2,1,0:T(8,128)S(1)} %get-tuple-element.68, ...), kind=kLoop, calls=%fused_computation.302 | loop fusion | flops 11304960 | bytes 11304960 | tf_op jit(solution)/shard_map/add | solution.py:376
  75.1 2.3 %multiply_add_fusion.5 = (f32[4,20,48,128]{3,2,1,0:T(8,128)S(1)}, f32[4,20,48,128]{3,2,1,0:T(8,128)S(1)}) fusion(f32[4,20,48,128]{3,2,1,0:T(8,128)S(1)} %get-tuple-element.44, f32[4,20,48,128]{3,2,1,0:T(8,128)S(1)} %get-tuple-element.45, f32[20,48,128]{2,1,0:T(8,128)S(1)} %get-tuple-element.72, f32[20,48,128]{2,1,0:T(8,128)S(1)} %get-tuple-element.68, ...), kind=kLoop, calls=%fused_computation.301 | loop fusion | flops 11304960 | bytes 11304960 | tf_op jit(solution)/shard_map/add | solution.py:376
  77.4 2.3 %multiply_add_fusion.4 = (f32[4,20,48,128]{3,2,1,0:T(8,128)S(1)}, f32[4,20,48,128]{3,2,1,0:T(8,128)S(1)}) fusion(f32[4,20,48,128]{3,2,1,0:T(8,128)S(1)} %get-tuple-element.42, f32[4,20,48,128]{3,2,1,0:T(8,128)S(1)} %get-tuple-element.43, f32[20,48,128]{2,1,0:T(8,128)S(1)} %get-tuple-element.72, f32[20,48,128]{2,1,0:T(8,128)S(1)} %get-tuple-element.68, ...), kind=kLoop, calls=%fused_computation.300 | loop fusion | flops 11304960 | bytes 11304960 | tf_op jit(solution)/shard_map/add | solution.py:376
  79.7 2.0 %fusion.108 = (f32[4,20,48,128]{3,2,1,0:T(8,128)S(1)}, f32[4,20,48,128]{3,2,1,0:T(8,128)S(1)}, f32[4,20,48,128]{3,2,1,0:T(8,128)S(1)}) fusion(f32[4,20,48,128]{3,2,1,0:T(8,128)S(1)} %get-tuple-element.40, f32[20,48,128]{2,1,0:T(8,128)S(1)} %get-tuple-element.49, f32[20,48,128]{2,1,0:T(8,128)S(1)} %get-tuple-element.69, ...), kind=kLoop, calls=%fused_computation.188 | loop fusion | flops 7864320 | bytes 10813440 | tf_op jit(solution)/shard_map/add | solution.py:424
  82.8 1.1 pad_maximum_fusion
  84.0 3.4 %multiply_reduce_fusion = f32[8,1024]{1,0:T(8,128)S(1)} fusion(f32[8,256,128]{2,1,0:T(8,128)} %bitcast.76, f32[128,1024]{1,0:T(8,128)S(1)} %fusion.245, s32[1024]{0:T(1024)S(1)} %get-tuple-element.96, pred[1024]{0:T(1024)(128)(4,1)S(1)} %get-tuple-element.94), kind=kOutput, calls=%fused_computation.68 | convolution fusion | flops 3223838720 | bytes 1610752 | tf_op jit(solution)/shard_map/spz,pd->szd/dot_general | solution.py:443
  88.1 15.8 %shard_map.123 = f32[64,128]{1,0:T(8,128)} custom-call(f32[64,128]{1,0:T(8,128)} %reshape.402.refs_0_), custom_call_target="tpu_custom_call" | custom-call | tf_op jit(solution)/shard_map/pallas_call | solution.py:304
  105.6 0.9 multiply_reduce_fusion.10
  106.9 3.5 %fusion.4 = f32[960,4,128]{2,0,1:T(8,128)S(1)} fusion(s32[1024]{0:T(1024)S(1)} %get-tuple-element.98, pred[1024]{0:T(1024)(128)(4,1)S(1)} %get-tuple-element.95, f32[1024,128]{0,1:T(8,128)S(1)} %fusion.246, f32[1024,4]{0,1:T(4,128)S(1)} %divide_bitcast_fusion), kind=kOutput, calls=%fused_computation.73 | convolution fusion | flops 6042288128 | bytes 2511872 | tf_op jit(solution)/shard_map/dot_general | solution.py:460
  112.4 2.2 %multiply_add_fusion.3 = (f32[4,20,48,128]{3,2,1,0:T(8,128)S(1)}, f32[4,20,48,128]{3,2,1,0:T(8,128)S(1)}) fusion(f32[4,20,48,128]{3,2,1,0:T(8,128)S(1)} %bitcast.66, f32[4,20,48,128]{3,2,1,0:T(8,128)S(1)} %broadcast_multiply_fusion, f32[20,48,128]{2,1,0:T(8,128)S(1)} %copy-done.11, f32[20,48,128]{2,1,0:T(8,128)S(1)} %copy-done.3, ...), kind=kLoop, calls=%fused_computation.299 | loop fusion | flops 11304960 | bytes 11304960 | tf_op jit(solution)/shard_map/add | solution.py:376
  114.6 2.3 %multiply_add_fusion.2 = (f32[4,20,48,128]{3,2,1,0:T(8,128)S(1)}, f32[4,20,48,128]{3,2,1,0:T(8,128)S(1)}) fusion(f32[4,20,48,128]{3,2,1,0:T(8,128)S(1)} %get-tuple-element.38, f32[4,20,48,128]{3,2,1,0:T(8,128)S(1)} %get-tuple-element.39, f32[20,48,128]{2,1,0:T(8,128)S(1)} %copy-done.11, f32[20,48,128]{2,1,0:T(8,128)S(1)} %copy-done.3, ...), kind=kLoop, calls=%fused_computation.298 | loop fusion | flops 11304960 | bytes 11304960 | tf_op jit(solution)/shard_map/add | solution.py:376
  117.0 2.3 %multiply_add_fusion.1 = (f32[4,20,48,128]{3,2,1,0:T(8,128)S(1)}, f32[4,20,48,128]{3,2,1,0:T(8,128)S(1)}) fusion(f32[4,20,48,128]{3,2,1,0:T(8,128)S(1)} %get-tuple-element.36, f32[4,20,48,128]{3,2,1,0:T(8,128)S(1)} %get-tuple-element.37, f32[20,48,128]{2,1,0:T(8,128)S(1)} %copy-done.11, f32[20,48,128]{2,1,0:T(8,128)S(1)} %copy-done.3, ...), kind=kLoop, calls=%fused_computation.297 | loop fusion | flops 11304960 | bytes 11304960 | tf_op jit(solution)/shard_map/add | solution.py:376
  119.3 2.6 %multiply_add_fusion = (f32[4,20,48,128]{3,2,1,0:T(8,128)S(1)}, f32[4,20,48,128]{3,2,1,0:T(8,128)S(1)}) fusion(f32[4,20,48,128]{3,2,1,0:T(8,128)S(1)} %get-tuple-element.34, f32[4,20,48,128]{3,2,1,0:T(8,128)S(1)} %get-tuple-element.35, f32[20,48,128]{2,1,0:T(8,128)S(1)} %copy-done.11, f32[20,48,128]{2,1,0:T(8,128)S(1)} %copy-done.3, ...), kind=kLoop, calls=%fused_computation.296 | loop fusion | flops 11304960 | bytes 11304960 | tf_op jit(solution)/shard_map/add | solution.py:376
  121.9 3.0 %fusion.205 = f32[4,20,48,128]{3,2,1,0:T(8,128)S(1)} fusion(f32[4,20,48,128]{3,2,1,0:T(8,128)S(1)} %get-tuple-element.33, f32[4,20,48,128]{3,2,1,0:T(8,128)S(1)} %get-tuple-element.32, f32[4,20,48,128]{3,2,1,0:T(8,128)S(1)} %get-tuple-element.34, f32[4,20,48,128]{3,2,1,0:T(8,128)S(1)} %get-tuple-element.36, f32[4,20,48,128]{3,2,1,0:T(8,128)S(1)} %get-tuple-element.38, ...), kind=kLoop, calls=%fused_computation.285 | loop fusion | flops 14254080 | bytes 17203200 | tf_op jit(solution)/shard_map/add | solution.py:372
  125.1 0.9 copy-done.18
  126.0 1.4 fusion.225
  127.7 1.4 copy.43
  129.3 1.3 copy.44
  130.7 2.5 %multiply_reduce_fusion.1 = (f32[]{:T(128)}, f32[]{:T(128)}) fusion(f32[1,8,32,8,16]{4,2,1,0,3:T(8,128)} %copy.44, f32[2,8,32,8,16]{4,2,1,0,3:T(8,128)S(1)} %bitcast.64, f32[1,8,32,8,16]{4,2,1,0,3:T(8,128)} %copy.43), kind=kLoop, calls=%fused_computation.312 | loop fusion | flops 131070 | bytes 524296 | tf_op jit(solution)/shard_map/reduce_sum | solution.py:473
  139.0 1.2 reshape.404.refs_0_
  140.3 24.0 %shard_map.124 = (f32[64,128]{1,0:T(8,128)}, f32[8,128]{1,0:T(8,128)}) custom-call(f32[8,64,128]{2,1,0:T(8,128)} %reshape.404.refs_0_, f32[8,128]{1,0:T(8,128)} %fusion.274.refs_1_), custom_call_target="tpu_custom_call" | custom-call | tf_op jit(solution)/shard_map/pallas_call | solution.py:304
  165.1 1.4 fusion.294
  172.8 16.2 %shard_map.125 = f32[8,128]{1,0:T(8,128)} custom-call(f32[8,128]{1,0:T(8,128)} %pad_bitcast_fusion.refs_0_), custom_call_target="tpu_custom_call" | custom-call | tf_op jit(solution)/shard_map/pallas_call | solution.py:304
  189.0 1.2 slice.466
  (126 shorter events, 19.5 us)
Async XLA Ops:
  20.9 1.7 copy-start.14
  22.6 2.3 %copy-start.26 = (s32[8,32,128]{2,1,0:T(8,128)S(1)}, s32[8,32,128]{2,1,0:T(8,128)}, u32[]{:S(2)}) copy-start(s32[8,32,128]{2,1,0:T(8,128)} %param.10) | copy-start | bytes 393220
  24.2 1.1 copy-start.16
  63.3 0.7 copy-start.28
  63.3 0.7 copy-start.29
  67.2 3.3 %copy-start.19 = (f32[20,48,128]{2,1,0:T(8,128)}, f32[20,48,128]{2,1,0:T(8,128)S(1)}, u32[]{:S(2)}) copy-start(f32[20,48,128]{2,1,0:T(8,128)S(1)} %get-tuple-element.48) | copy-start | bytes 1474564
  67.2 12.5 %copy-start.12 = (f32[20,48,128]{2,1,0:T(8,128)}, f32[20,48,128]{2,1,0:T(8,128)S(1)}, u32[]{:S(2)}) copy-start(f32[20,48,128]{2,1,0:T(8,128)S(1)} %get-tuple-element.49) | copy-start | bytes 1474564
  68.1 11.6 %copy-start = (f32[20,48,128]{2,1,0:T(8,128)}, f32[20,48,128]{2,1,0:T(8,128)S(1)}, u32[]{:S(2)}) copy-start(f32[20,48,128]{2,1,0:T(8,128)S(1)} %get-tuple-element.67) | copy-start | bytes 1474564
  68.1 11.6 %copy-start.2 = (f32[20,48,128]{2,1,0:T(8,128)}, f32[20,48,128]{2,1,0:T(8,128)S(1)}, u32[]{:S(2)}) copy-start(f32[20,48,128]{2,1,0:T(8,128)S(1)} %get-tuple-element.68) | copy-start | bytes 1474564
  68.1 11.6 %copy-start.4 = (f32[20,48,128]{2,1,0:T(8,128)}, f32[20,48,128]{2,1,0:T(8,128)S(1)}, u32[]{:S(2)}) copy-start(f32[20,48,128]{2,1,0:T(8,128)S(1)} %get-tuple-element.69) | copy-start | bytes 1474564
  68.1 11.6 %copy-start.6 = (f32[20,48,128]{2,1,0:T(8,128)}, f32[20,48,128]{2,1,0:T(8,128)S(1)}, u32[]{:S(2)}) copy-start(f32[20,48,128]{2,1,0:T(8,128)S(1)} %get-tuple-element.70) | copy-start | bytes 1474564
  68.1 11.6 %copy-start.8 = (f32[20,48,128]{2,1,0:T(8,128)}, f32[20,48,128]{2,1,0:T(8,128)S(1)}, u32[]{:S(2)}) copy-start(f32[20,48,128]{2,1,0:T(8,128)S(1)} %get-tuple-element.71) | copy-start | bytes 1474564
  68.2 13.6 %copy-start.10 = (f32[20,48,128]{2,1,0:T(8,128)}, f32[20,48,128]{2,1,0:T(8,128)S(1)}, u32[]{:S(2)}) copy-start(f32[20,48,128]{2,1,0:T(8,128)S(1)} %get-tuple-element.72) | copy-start | bytes 1474564
  81.8 1.0 copy-start.17
  82.8 1.1 copy-start.27
  110.4 1.0 copy-start.1
  110.4 1.2 copy-start.3
  110.4 1.3 copy-start.5
  110.4 1.5 copy-start.7
  110.5 1.6 copy-start.9
  110.5 1.7 copy-start.11
  110.5 1.9 copy-start.20
  112.3 2.3 %copy-start.13 = (f32[20,48,128]{2,1,0:T(8,128)S(1)}, f32[20,48,128]{2,1,0:T(8,128)}, u32[]{:S(2)}) copy-start(f32[20,48,128]{2,1,0:T(8,128)} %copy-done.12) | copy-start | bytes 1474564
  125.0 1.0 copy-start.18
  127.4 1.6 copy-start.23
  127.7 2.9 %copy-start.15 = (f32[8,2,8,32,16]{4,3,2,1,0:T(8,128)S(1)}, f32[8,2,8,32,16]{4,3,2,1,0:T(8,128)}, u32[]{:S(2)}) copy-start(f32[8,2,8,32,16]{4,3,2,1,0:T(8,128)} %copy-done.14) | copy-start | bytes 786436
  130.6 3.8 %copy-start.21 = (f32[8,32,16]{1,2,0:T(8,128)S(1)}, f32[8,32,16]{1,2,0:T(8,128)}, u32[]{:S(2)}) copy-start(f32[8,32,16]{1,2,0:T(8,128)} %param.16) | copy-start | bytes 49156
  130.7 3.8 %copy-start.22 = (f32[8,32,16]{1,2,0:T(8,128)S(1)}, f32[8,32,16]{1,2,0:T(8,128)}, u32[]{:S(2)}) copy-start(f32[8,32,16]{1,2,0:T(8,128)} %param.15) | copy-start | bytes 49156
  130.7 3.8 %copy-start.24 = (f32[8,32,16]{1,2,0:T(8,128)S(1)}, f32[8,32,16]{1,2,0:T(8,128)}, u32[]{:S(2)}) copy-start(f32[8,32,16]{1,2,0:T(8,128)} %param.18) | copy-start | bytes 49156
  130.7 3.8 %copy-start.25 = (f32[8,32,16]{1,2,0:T(8,128)S(1)}, f32[8,32,16]{1,2,0:T(8,128)}, u32[]{:S(2)}) copy-start(f32[8,32,16]{1,2,0:T(8,128)} %param.17) | copy-start | bytes 49156

commit v15 on v14

--- a/solution.py
+++ b/solution.py
@@ -98,40 +98,46 @@
         x_ref, wide.at[:, pl.ds(hx, cx), pl.ds(hy, cy), :], local_sem
     )
     local.start()
-    direct, relayed = [], []
+    direct = []
     for k, (dx, dy) in enumerate(steps):
         src_x, dst_x = window(dx, cx, hx)
         if dy != 0 and dx < 0:
             src_x, dst_x = pl.ds(0, hx - 1), pl.ds(cx + hx, hx - 1)
         if dy != 0 and dx > 0:
             src_x, dst_x = pl.ds(cx - hx + 1, hx - 1), pl.ds(1, hx - 1)
-        src_y, dst_y = window(dy, cy, hy)
         tx = jnp.clip(ax + dx, 0, nx - 1)
         ty = jnp.clip(ay + dy, 0, ny - 1)
         for f in range(fields):
-            slot = k * fields + f
-            copy = pltpu.make_async_remote_copy(
-                src_ref=x_ref.at[f, src_x, src_y, :],
-                dst_ref=wide.at[f, dst_x, dst_y, :],
-                send_sem=send_sem.at[slot],
-                recv_sem=recv_sem.at[slot],
-                device_id={"gx": tx, "gy": ty},
-                device_id_type=MESH,
-            )
-            relay = None if f < own_fields else pltpu.make_async_remote_copy(
-                src_ref=wide.at[f, dst_x, dst_y, :],
-                dst_ref=wide.at[f, dst_x, dst_y, :],
-                send_sem=fwd_send.at[slot],
-                recv_sem=fwd_recv.at[slot],
-                device_id={"src": partner},
-                device_id_type=MESH,
-            )
-            mine = True if f < own_fields else ((f - own_fields) % 2 == half)
-            direct.append((copy, relay, dx, dy, f, mine))
-
-            @pl.when(exists(dx, dy) & mine)
-            def _():
-                copy.start()
+            parts = 2 if (f >= own_fields and dy == 0) else 1
+            for part in range(parts):
+                if parts == 2:
+                    rows = cy // 2
+                    src_y, dst_y = pl.ds(part * rows, rows), pl.ds(hy + part * rows, rows)
+                else:
+                    src_y, dst_y = window(dy, cy, hy)
+                slot = (k * fields + f) * 2 + part
+                copy = pltpu.make_async_remote_copy(
+                    src_ref=x_ref.at[f, src_x, src_y, :],
+                    dst_ref=wide.at[f, dst_x, dst_y, :],
+                    send_sem=send_sem.at[slot],
+                    recv_sem=recv_sem.at[slot],
+                    device_id={"gx": tx, "gy": ty},
+                    device_id_type=MESH,
+                )
+                relay = None if f < own_fields else pltpu.make_async_remote_copy(
+                    src_ref=wide.at[f, dst_x, dst_y, :],
+                    dst_ref=wide.at[f, dst_x, dst_y, :],
+                    send_sem=fwd_send.at[slot],
+                    recv_sem=fwd_recv.at[slot],
+                    device_id={"src": partner},
+                    device_id_type=MESH,
+                )
+                mine = True if f < own_fields else ((f - own_fields + part) % 2 == half)
+                direct.append((copy, relay, dx, dy, f, mine))
+
+                @pl.when(exists(dx, dy) & mine)
+                def _():
+                    copy.start()
 
     local.wait()
     for copy, relay, dx, dy, f, mine in direct:
@@ -172,11 +178,11 @@
         out_specs=pl.BlockSpec(memory_space=pltpu.VMEM),
         scratch_shapes=[
             pltpu.VMEM(shape, x.dtype),
-            pltpu.SemaphoreType.DMA((8 * fields,)),
-            pltpu.SemaphoreType.DMA((8 * fields,)),
+            pltpu.SemaphoreType.DMA((16 * fields,)),
+            pltpu.SemaphoreType.DMA((16 * fields,)),
             pltpu.SemaphoreType.DMA,
-            pltpu.SemaphoreType.DMA((8 * fields,)),
-            pltpu.SemaphoreType.DMA((8 * fields,)),
+            pltpu.SemaphoreType.DMA((16 * fields,)),
+            pltpu.SemaphoreType.DMA((16 * fields,)),
         ],
         compiler_params=pltpu.CompilerParams(
             collective_id=cid, has_side_effects=True, vmem_limit_bytes=48 * 1024 * 1024

time: 194 us -> 196 us (1.010)
  Pallas kernels: 111 us -> 113 us
    pallas_call x3, Pallas kernels: 56 us -> 58.1 us  [small_sum(): pl.pallas_call(functools.partial(_reduce_kernel, stages, spread is not No...]
where the time goes in v15:
time: 196 us; the launch traced here: 195 us
  Pallas kernels  113 us (58%)
  other arithmetic  39.2 us (20%)
  local copies, waits for them, and re-layouts  24.2 us (12%)
  between operations  9.8 us (5%)
  matrix products  9.14 us (5%)
    pallas_call x3, Pallas kernels, small_sum(): pl.pallas_call(functools.partial(_reduce_kernel, stages, spread is not No...  58.1 us
    pallas_call x1, Pallas kernels, halo_block(): pl.pallas_call(functools.partial(_halo_kernel, hx, hy, own_fields), out_s...  37.9 us
    add x8, other arithmetic, chebyshev(): step_dir = rho_next * rho * step_dir + 2.0 * rho_next / delta * remain  18.9 us
    pallas_call x1, Pallas kernels, exchange(): pl.pallas_call(functools.partial(_exchange_kernel, axis, n, scatter), out...  16.7 us
    unnamed x66, local copies, waits for them, and re-layouts  6.31 us

profile of v15, /device:TPU:1, one launch (start us, length us, event | category | flops | bytes accessed | tf_op | source)
XLA Modules:
  0.0 195.0 jit_solution(760458947849252585)
XLA Ops:
  2.5 16.7 %shard_map.121 = f32[8,64,128]{2,1,0:T(8,128)} custom-call(f32[64,128]{1,0:T(8,128)} %reshape.399.x_ref), custom_call_target="tpu_custom_call" | custom-call | tf_op jit(solution)/shard_map/pallas_call | solution.py:50
  19.2 1.7 reshape.400
  20.9 1.5 fusion.291
  22.6 1.6 copy.35
  25.3 37.9 %shard_map.122 = f32[7,20,48,128]{3,2,1,0:T(8,128)S(1)} custom-call(f32[7,8,32,128]{3,2,1,0:T(8,128)S(1)} %pad_maximum_fusion.1.x_ref), custom_call_target="tpu_custom_call" | custom-call | tf_op jit(solution)/shard_map/pallas_call | solution.py:174
  63.9 2.3 %fusion = f32[2,122880]{1,0:T(2,128)S(1)} fusion(f32[122880]{0:T(1024)S(1)} %bitcast.79, f32[1,16]{1,0:T(1,128)S(1)} %bitcast.82, f32[1,16]{1,0:T(1,128)S(1)} %bitcast.83), kind=kOutput, calls=%fused_computation.67 | convolution fusion | flops 49152032 | bytes 1474688 | tf_op jit(solution)/shard_map/dot_general | solution.py:422
  68.2 2.2 %broadcast_multiply_fusion.1 = (f32[4,20,48,128]{3,2,1,0:T(8,128)S(1)}, f32[4,20,48,128]{3,2,1,0:T(8,128)S(1)}) fusion(f32[4,20,48,128]{3,2,1,0:T(8,128)S(1)} %slice.359, f32[20,48,128]{2,1,0:T(8,128)S(1)} %get-tuple-element.85, f32[20,48,128]{2,1,0:T(8,128)S(1)} %get-tuple-element.89, f32[20,48,128]{2,1,0:T(8,128)S(1)} %get-tuple-element.88, ...), kind=kLoop, calls=%fused_computation.320 | loop fusion | flops 10321920 | bytes 9338880 | tf_op jit(solution)/shard_map/div | solution.py:376
  70.4 2.3 %multiply_add_fusion.7 = (f32[4,20,48,128]{3,2,1,0:T(8,128)S(1)}, f32[4,20,48,128]{3,2,1,0:T(8,128)S(1)}) fusion(f32[4,20,48,128]{3,2,1,0:T(8,128)S(1)} %get-tuple-element.51, f32[4,20,48,128]{3,2,1,0:T(8,128)S(1)} %get-tuple-element.50, f32[20,48,128]{2,1,0:T(8,128)S(1)} %get-tuple-element.72, f32[20,48,128]{2,1,0:T(8,128)S(1)} %get-tuple-element.68, ...), kind=kLoop, calls=%fused_computation.303 | loop fusion | flops 11304960 | bytes 11304960 | tf_op jit(solution)/shard_map/add | solution.py:382
  72.8 2.3 %multiply_add_fusion.6 = (f32[4,20,48,128]{3,2,1,0:T(8,128)S(1)}, f32[4,20,48,128]{3,2,1,0:T(8,128)S(1)}) fusion(f32[4,20,48,128]{3,2,1,0:T(8,128)S(1)} %get-tuple-element.46, f32[4,20,48,128]{3,2,1,0:T(8,128)S(1)} %get-tuple-element.47, f32[20,48,128]{2,1,0:T(8,128)S(1)} %get-tuple-element.72, f32[20,48,128]{2,1,0:T(8,128)S(1)} %get-tuple-element.68, ...), kind=kLoop, calls=%fused_computation.302 | loop fusion | flops 11304960 | bytes 11304960 | tf_op jit(solution)/shard_map/add | solution.py:382
  75.0 2.3 %multiply_add_fusion.5 = (f32[4,20,48,128]{3,2,1,0:T(8,128)S(1)}, f32[4,20,48,128]{3,2,1,0:T(8,128)S(1)}) fusion(f32[4,20,48,128]{3,2,1,0:T(8,128)S(1)} %get-tuple-element.44, f32[4,20,48,128]{3,2,1,0:T(8,128)S(1)} %get-tuple-element.45, f32[20,48,128]{2,1,0:T(8,128)S(1)} %get-tuple-element.72, f32[20,48,128]{2,1,0:T(8,128)S(1)} %get-tuple-element.68, ...), kind=kLoop, calls=%fused_computation.301 | loop fusion | flops 11304960 | bytes 11304960 | tf_op jit(solution)/shard_map/add | solution.py:382
  77.3 2.5 %multiply_add_fusion.4 = (f32[4,20,48,128]{3,2,1,0:T(8,128)S(1)}, f32[4,20,48,128]{3,2,1,0:T(8,128)S(1)}) fusion(f32[4,20,48,128]{3,2,1,0:T(8,128)S(1)} %get-tuple-element.42, f32[4,20,48,128]{3,2,1,0:T(8,128)S(1)} %get-tuple-element.43, f32[20,48,128]{2,1,0:T(8,128)S(1)} %get-tuple-element.72, f32[20,48,128]{2,1,0:T(8,128)S(1)} %get-tuple-element.68, ...), kind=kLoop, calls=%fused_computation.300 | loop fusion | flops 11304960 | bytes 11304960 | tf_op jit(solution)/shard_map/add | solution.py:382
  79.9 1.8 fusion.108
  82.7 1.1 pad_maximum_fusion
  83.9 3.4 %multiply_reduce_fusion = f32[8,1024]{1,0:T(8,128)S(1)} fusion(f32[8,256,128]{2,1,0:T(8,128)} %bitcast.76, f32[128,1024]{1,0:T(8,128)S(1)} %fusion.245, s32[1024]{0:T(1024)S(1)} %get-tuple-element.96, pred[1024]{0:T(1024)(128)(4,1)S(1)} %get-tuple-element.94), kind=kOutput, calls=%fused_computation.68 | convolution fusion | flops 3223838720 | bytes 1610752 | tf_op jit(solution)/shard_map/spz,pd->szd/dot_general | solution.py:449
  88.0 17.9 %shard_map.123 = f32[64,128]{1,0:T(8,128)} custom-call(f32[64,128]{1,0:T(8,128)} %reshape.402.refs_0_), custom_call_target="tpu_custom_call" | custom-call | tf_op jit(solution)/shard_map/pallas_call | solution.py:310
  107.6 0.9 multiply_reduce_fusion.10
  108.9 3.5 %fusion.4 = f32[960,4,128]{2,0,1:T(8,128)S(1)} fusion(s32[1024]{0:T(1024)S(1)} %get-tuple-element.98, pred[1024]{0:T(1024)(128)(4,1)S(1)} %get-tuple-element.95, f32[1024,128]{0,1:T(8,128)S(1)} %fusion.246, f32[1024,4]{0,1:T(4,128)S(1)} %divide_bitcast_fusion), kind=kOutput, calls=%fused_computation.73 | convolution fusion | flops 6042288128 | bytes 2511872 | tf_op jit(solution)/shard_map/dot_general | solution.py:466
  114.4 2.2 %multiply_add_fusion.3 = (f32[4,20,48,128]{3,2,1,0:T(8,128)S(1)}, f32[4,20,48,128]{3,2,1,0:T(8,128)S(1)}) fusion(f32[4,20,48,128]{3,2,1,0:T(8,128)S(1)} %bitcast.66, f32[4,20,48,128]{3,2,1,0:T(8,128)S(1)} %broadcast_multiply_fusion, f32[20,48,128]{2,1,0:T(8,128)S(1)} %copy-done.11, f32[20,48,128]{2,1,0:T(8,128)S(1)} %copy-done.3, ...), kind=kLoop, calls=%fused_computation.299 | loop fusion | flops 11304960 | bytes 11304960 | tf_op jit(solution)/shard_map/add | solution.py:382
  116.6 2.3 %multiply_add_fusion.2 = (f32[4,20,48,128]{3,2,1,0:T(8,128)S(1)}, f32[4,20,48,128]{3,2,1,0:T(8,128)S(1)}) fusion(f32[4,20,48,128]{3,2,1,0:T(8,128)S(1)} %get-tuple-element.38, f32[4,20,48,128]{3,2,1,0:T(8,128)S(1)} %get-tuple-element.39, f32[20,48,128]{2,1,0:T(8,128)S(1)} %copy-done.11, f32[20,48,128]{2,1,0:T(8,128)S(1)} %copy-done.3, ...), kind=kLoop, calls=%fused_computation.298 | loop fusion | flops 11304960 | bytes 11304960 | tf_op jit(solution)/shard_map/add | solution.py:382
  119.0 2.6 %multiply_add_fusion.1 = (f32[4,20,48,128]{3,2,1,0:T(8,128)S(1)}, f32[4,20,48,128]{3,2,1,0:T(8,128)S(1)}) fusion(f32[4,20,48,128]{3,2,1,0:T(8,128)S(1)} %get-tuple-element.36, f32[4,20,48,128]{3,2,1,0:T(8,128)S(1)} %get-tuple-element.37, f32[20,48,128]{2,1,0:T(8,128)S(1)} %copy-done.11, f32[20,48,128]{2,1,0:T(8,128)S(1)} %copy-done.3, ...), kind=kLoop, calls=%fused_computation.297 | loop fusion | flops 11304960 | bytes 11304960 | tf_op jit(solution)/shard_map/add | solution.py:382
  121.6 2.3 %multiply_add_fusion = (f32[4,20,48,128]{3,2,1,0:T(8,128)S(1)}, f32[4,20,48,128]{3,2,1,0:T(8,128)S(1)}) fusion(f32[4,20,48,128]{3,2,1,0:T(8,128)S(1)} %get-tuple-element.34, f32[4,20,48,128]{3,2,1,0:T(8,128)S(1)} %get-tuple-element.35, f32[20,48,128]{2,1,0:T(8,128)S(1)} %copy-done.11, f32[20,48,128]{2,1,0:T(8,128)S(1)} %copy-done.3, ...), kind=kLoop, calls=%fused_computation.296 | loop fusion | flops 11304960 | bytes 11304960 | tf_op jit(solution)/shard_map/add | solution.py:382
  123.9 3.0 %fusion.205 = f32[4,20,48,128]{3,2,1,0:T(8,128)S(1)} fusion(f32[4,20,48,128]{3,2,1,0:T(8,128)S(1)} %get-tuple-element.33, f32[4,20,48,128]{3,2,1,0:T(8,128)S(1)} %get-tuple-element.32, f32[4,20,48,128]{3,2,1,0:T(8,128)S(1)} %get-tuple-element.34, f32[4,20,48,128]{3,2,1,0:T(8,128)S(1)} %get-tuple-element.36, f32[4,20,48,128]{3,2,1,0:T(8,128)S(1)} %get-tuple-element.38, ...), kind=kLoop, calls=%fused_computation.285 | loop fusion | flops 14254080 | bytes 17203200 | tf_op jit(solution)/shard_map/add | solution.py:378
  127.1 0.9 copy-done.18
  128.0 1.4 fusion.225
  129.7 1.4 copy.43
  131.3 1.3 copy.44
  132.7 2.5 %multiply_reduce_fusion.1 = (f32[]{:T(128)}, f32[]{:T(128)}) fusion(f32[1,8,32,8,16]{4,2,1,0,3:T(8,128)} %copy.44, f32[2,8,32,8,16]{4,2,1,0,3:T(8,128)S(1)} %bitcast.64, f32[1,8,32,8,16]{4,2,1,0,3:T(8,128)} %copy.43), kind=kLoop, calls=%fused_computation.312 | loop fusion | flops 131070 | bytes 524296 | tf_op jit(solution)/shard_map/reduce_sum | solution.py:479
  141.0 1.2 reshape.404.refs_0_
  142.3 24.0 %shard_map.124 = (f32[64,128]{1,0:T(8,128)}, f32[8,128]{1,0:T(8,128)}) custom-call(f32[8,64,128]{2,1,0:T(8,128)} %reshape.404.refs_0_, f32[8,128]{1,0:T(8,128)} %fusion.274.refs_1_), custom_call_target="tpu_custom_call" | custom-call | tf_op jit(solution)/shard_map/pallas_call | solution.py:310
  167.1 1.4 fusion.294
  174.8 16.2 %shard_map.125 = f32[8,128]{1,0:T(8,128)} custom-call(f32[8,128]{1,0:T(8,128)} %pad_bitcast_fusion.refs_0_), custom_call_target="tpu_custom_call" | custom-call | tf_op jit(solution)/shard_map/pallas_call | solution.py:310
  191.0 1.2 slice.466
  (126 shorter events, 19.5 us)
Async XLA Ops:
  20.9 1.7 copy-start.14
  22.6 2.3 %copy-start.26 = (s32[8,32,128]{2,1,0:T(8,128)S(1)}, s32[8,32,128]{2,1,0:T(8,128)}, u32[]{:S(2)}) copy-start(s32[8,32,128]{2,1,0:T(8,128)} %param.10) | copy-start | bytes 393220
  24.2 1.1 copy-start.16
  63.2 0.7 copy-start.28
  63.2 0.7 copy-start.29
  67.1 3.3 %copy-start.19 = (f32[20,48,128]{2,1,0:T(8,128)}, f32[20,48,128]{2,1,0:T(8,128)S(1)}, u32[]{:S(2)}) copy-start(f32[20,48,128]{2,1,0:T(8,128)S(1)} %get-tuple-element.48) | copy-start | bytes 1474564
  67.1 12.7 %copy-start.12 = (f32[20,48,128]{2,1,0:T(8,128)}, f32[20,48,128]{2,1,0:T(8,128)S(1)}, u32[]{:S(2)}) copy-start(f32[20,48,128]{2,1,0:T(8,128)S(1)} %get-tuple-element.49) | copy-start | bytes 1474564
  68.0 11.8 %copy-start = (f32[20,48,128]{2,1,0:T(8,128)}, f32[20,48,128]{2,1,0:T(8,128)S(1)}, u32[]{:S(2)}) copy-start(f32[20,48,128]{2,1,0:T(8,128)S(1)} %get-tuple-element.67) | copy-start | bytes 1474564
  68.0 11.8 %copy-start.2 = (f32[20,48,128]{2,1,0:T(8,128)}, f32[20,48,128]{2,1,0:T(8,128)S(1)}, u32[]{:S(2)}) copy-start(f32[20,48,128]{2,1,0:T(8,128)S(1)} %get-tuple-element.68) | copy-start | bytes 1474564
  68.0 11.8 %copy-start.4 = (f32[20,48,128]{2,1,0:T(8,128)}, f32[20,48,128]{2,1,0:T(8,128)S(1)}, u32[]{:S(2)}) copy-start(f32[20,48,128]{2,1,0:T(8,128)S(1)} %get-tuple-element.69) | copy-start | bytes 1474564
  68.0 11.8 %copy-start.6 = (f32[20,48,128]{2,1,0:T(8,128)}, f32[20,48,128]{2,1,0:T(8,128)S(1)}, u32[]{:S(2)}) copy-start(f32[20,48,128]{2,1,0:T(8,128)S(1)} %get-tuple-element.70) | copy-start | bytes 1474564
  68.0 11.8 %copy-start.8 = (f32[20,48,128]{2,1,0:T(8,128)}, f32[20,48,128]{2,1,0:T(8,128)S(1)}, u32[]{:S(2)}) copy-start(f32[20,48,128]{2,1,0:T(8,128)S(1)} %get-tuple-element.71) | copy-start | bytes 1474564
  68.1 13.6 %copy-start.10 = (f32[20,48,128]{2,1,0:T(8,128)}, f32[20,48,128]{2,1,0:T(8,128)S(1)}, u32[]{:S(2)}) copy-start(f32[20,48,128]{2,1,0:T(8,128)S(1)} %get-tuple-element.72) | copy-start | bytes 1474564
  81.7 1.0 copy-start.17
  82.7 1.1 copy-start.27
  112.4 1.0 copy-start.1
  112.4 1.2 copy-start.3
  112.4 1.3 copy-start.5
  112.5 1.5 copy-start.7
  112.5 1.6 copy-start.9
  112.5 1.7 copy-start.11
  112.5 1.9 copy-start.20
  114.4 2.3 %copy-start.13 = (f32[20,48,128]{2,1,0:T(8,128)S(1)}, f32[20,48,128]{2,1,0:T(8,128)}, u32[]{:S(2)}) copy-start(f32[20,48,128]{2,1,0:T(8,128)} %copy-done.12) | copy-start | bytes 1474564
  127.0 1.0 copy-start.18
  129.4 1.6 copy-start.23
  129.7 2.9 %copy-start.15 = (f32[8,2,8,32,16]{4,3,2,1,0:T(8,128)S(1)}, f32[8,2,8,32,16]{4,3,2,1,0:T(8,128)}, u32[]{:S(2)}) copy-start(f32[8,2,8,32,16]{4,3,2,1,0:T(8,128)} %copy-done.14) | copy-start | bytes 786436
  132.7 3.8 %copy-start.21 = (f32[8,32,16]{1,2,0:T(8,128)S(1)}, f32[8,32,16]{1,2,0:T(8,128)}, u32[]{:S(2)}) copy-start(f32[8,32,16]{1,2,0:T(8,128)} %param.16) | copy-start | bytes 49156
  132.7 3.8 %copy-start.22 = (f32[8,32,16]{1,2,0:T(8,128)S(1)}, f32[8,32,16]{1,2,0:T(8,128)}, u32[]{:S(2)}) copy-start(f32[8,32,16]{1,2,0:T(8,128)} %param.15) | copy-start | bytes 49156
  132.7 3.8 %copy-start.24 = (f32[8,32,16]{1,2,0:T(8,128)S(1)}, f32[8,32,16]{1,2,0:T(8,128)}, u32[]{:S(2)}) copy-start(f32[8,32,16]{1,2,0:T(8,128)} %param.18) | copy-start | bytes 49156
  132.7 3.8 %copy-start.25 = (f32[8,32,16]{1,2,0:T(8,128)S(1)}, f32[8,32,16]{1,2,0:T(8,128)}, u32[]{:S(2)}) copy-start(f32[8,32,16]{1,2,0:T(8,128)} %param.17) | copy-start | bytes 49156

commit v16 on v14

--- a/solution.py
+++ b/solution.py
@@ -62,7 +62,7 @@
     )(x)
 
 
-def _halo_kernel(hx, hy, own_fields, x_ref, o_ref, wide, send_sem, recv_sem, local_sem, fwd_send, fwd_recv):
+def _halo_kernel(hx, hy, own_fields, trim_last, x_ref, o_ref, wide, send_sem, recv_sem, local_sem, fwd_send, fwd_recv):
     fields, cx, cy, cz = x_ref.shape
     ax, ay = lax.axis_index("gx"), lax.axis_index("gy")
     nx, ny = lax.axis_size("gx"), lax.axis_size("gy")
@@ -110,6 +110,12 @@
         ty = jnp.clip(ay + dy, 0, ny - 1)
         for f in range(fields):
             slot = k * fields + f
+            if trim_last and f == fields - 1 and dx != 0:
+                depth = hx - 1 if dy == 0 else hx - 2
+                if dx < 0:
+                    src_x, dst_x = pl.ds(0, depth), pl.ds(cx + hx, depth)
+                else:
+                    src_x, dst_x = pl.ds(cx - depth, depth), pl.ds(hx - depth, depth)
             copy = pltpu.make_async_remote_copy(
                 src_ref=x_ref.at[f, src_x, src_y, :],
                 dst_ref=wide.at[f, dst_x, dst_y, :],
@@ -161,12 +167,12 @@
     o_ref[...] = wide[...]
 
 
-def halo_block(x, hx, hy, cid, own_fields=None):
+def halo_block(x, hx, hy, cid, own_fields=None, trim_last=False):
     fields, cx, cy, cz = x.shape
     own_fields = fields if own_fields is None else own_fields
     shape = (fields, cx + 2 * hx, cy + 2 * hy, cz)
     return pl.pallas_call(
-        functools.partial(_halo_kernel, hx, hy, own_fields),
+        functools.partial(_halo_kernel, hx, hy, own_fields, trim_last),
         out_shape=jax.ShapeDtypeStruct(shape, x.dtype),
         in_specs=[pl.BlockSpec(memory_space=pltpu.VMEM)],
         out_specs=pl.BlockSpec(memory_space=pltpu.VMEM),
@@ -400,7 +406,7 @@
     width_y = 8
     region_of = labels.astype(jnp.float32)[None]
     stacked = jnp.concatenate([background, region_of, full_k[None], full_a[None]], axis=0)
-    wide = halo_block(stacked, width, width_y, 10, own_fields=sources)
+    wide = halo_block(stacked, width, width_y, 10, own_fields=sources, trim_last=True)
     phi_w, region_w, vk_w, va_w = wide[:sources], wide[sources], wide[sources + 1], wide[sources + 2]
     wx = cx + 2 * width
     wy = cy + 2 * width_y

time: 194 us -> 193 us (level)
  no operation moved by 1% of the time
where the time goes in v16:
time: 193 us; the launch traced here: 192 us
  Pallas kernels  110 us (57%)
  other arithmetic  39.2 us (20%)
  local copies, waits for them, and re-layouts  24.2 us (13%)
  between operations  9.8 us (5%)
  matrix products  9.14 us (5%)
    pallas_call x3, Pallas kernels, small_sum(): pl.pallas_call(functools.partial(_reduce_kernel, stages, spread is not No...  56.3 us
    pallas_call x1, Pallas kernels, halo_block(): pl.pallas_call(functools.partial(_halo_kernel, hx, hy, own_fields, trim_l...  37.2 us
    add x8, other arithmetic, chebyshev(): step_dir = rho_next * rho * step_dir + 2.0 * rho_next / delta * remain  18.7 us
    pallas_call x1, Pallas kernels, exchange(): pl.pallas_call(functools.partial(_exchange_kernel, axis, n, scatter), out...  16.7 us
    unnamed x66, local copies, waits for them, and re-layouts  6.31 us

profile of v16, /device:TPU:1, one launch (start us, length us, event | category | flops | bytes accessed | tf_op | source)
XLA Modules:
  0.0 192.5 jit_solution(6944523069886706385)
XLA Ops:
  2.5 16.7 %shard_map.121 = f32[8,64,128]{2,1,0:T(8,128)} custom-call(f32[64,128]{1,0:T(8,128)} %reshape.399.x_ref), custom_call_target="tpu_custom_call" | custom-call | tf_op jit(solution)/shard_map/pallas_call | solution.py:50
  19.2 1.7 reshape.400
  20.9 1.5 fusion.291
  22.6 1.6 copy.35
  25.3 37.2 %shard_map.122 = f32[7,20,48,128]{3,2,1,0:T(8,128)S(1)} custom-call(f32[7,8,32,128]{3,2,1,0:T(8,128)S(1)} %pad_maximum_fusion.1.x_ref), custom_call_target="tpu_custom_call" | custom-call | tf_op jit(solution)/shard_map/pallas_call | solution.py:174
  63.2 2.3 %fusion = f32[2,122880]{1,0:T(2,128)S(1)} fusion(f32[122880]{0:T(1024)S(1)} %bitcast.79, f32[1,16]{1,0:T(1,128)S(1)} %bitcast.82, f32[1,16]{1,0:T(1,128)S(1)} %bitcast.83), kind=kOutput, calls=%fused_computation.67 | convolution fusion | flops 49152032 | bytes 1474688 | tf_op jit(solution)/shard_map/dot_general | solution.py:422
  67.5 2.2 %broadcast_multiply_fusion.1 = (f32[4,20,48,128]{3,2,1,0:T(8,128)S(1)}, f32[4,20,48,128]{3,2,1,0:T(8,128)S(1)}) fusion(f32[4,20,48,128]{3,2,1,0:T(8,128)S(1)} %slice.359, f32[20,48,128]{2,1,0:T(8,128)S(1)} %get-tuple-element.85, f32[20,48,128]{2,1,0:T(8,128)S(1)} %get-tuple-element.89, f32[20,48,128]{2,1,0:T(8,128)S(1)} %get-tuple-element.88, ...), kind=kLoop, calls=%fused_computation.320 | loop fusion | flops 10321920 | bytes 9338880 | tf_op jit(solution)/shard_map/div | solution.py:376
  69.7 2.3 %multiply_add_fusion.7 = (f32[4,20,48,128]{3,2,1,0:T(8,128)S(1)}, f32[4,20,48,128]{3,2,1,0:T(8,128)S(1)}) fusion(f32[4,20,48,128]{3,2,1,0:T(8,128)S(1)} %get-tuple-element.51, f32[4,20,48,128]{3,2,1,0:T(8,128)S(1)} %get-tuple-element.50, f32[20,48,128]{2,1,0:T(8,128)S(1)} %get-tuple-element.72, f32[20,48,128]{2,1,0:T(8,128)S(1)} %get-tuple-element.68, ...), kind=kLoop, calls=%fused_computation.303 | loop fusion | flops 11304960 | bytes 11304960 | tf_op jit(solution)/shard_map/add | solution.py:382
  72.1 2.3 %multiply_add_fusion.6 = (f32[4,20,48,128]{3,2,1,0:T(8,128)S(1)}, f32[4,20,48,128]{3,2,1,0:T(8,128)S(1)}) fusion(f32[4,20,48,128]{3,2,1,0:T(8,128)S(1)} %get-tuple-element.46, f32[4,20,48,128]{3,2,1,0:T(8,128)S(1)} %get-tuple-element.47, f32[20,48,128]{2,1,0:T(8,128)S(1)} %get-tuple-element.72, f32[20,48,128]{2,1,0:T(8,128)S(1)} %get-tuple-element.68, ...), kind=kLoop, calls=%fused_computation.302 | loop fusion | flops 11304960 | bytes 11304960 | tf_op jit(solution)/shard_map/add | solution.py:382
  74.3 2.3 %multiply_add_fusion.5 = (f32[4,20,48,128]{3,2,1,0:T(8,128)S(1)}, f32[4,20,48,128]{3,2,1,0:T(8,128)S(1)}) fusion(f32[4,20,48,128]{3,2,1,0:T(8,128)S(1)} %get-tuple-element.44, f32[4,20,48,128]{3,2,1,0:T(8,128)S(1)} %get-tuple-element.45, f32[20,48,128]{2,1,0:T(8,128)S(1)} %get-tuple-element.72, f32[20,48,128]{2,1,0:T(8,128)S(1)} %get-tuple-element.68, ...), kind=kLoop, calls=%fused_computation.301 | loop fusion | flops 11304960 | bytes 11304960 | tf_op jit(solution)/shard_map/add | solution.py:382
  76.6 2.3 %multiply_add_fusion.4 = (f32[4,20,48,128]{3,2,1,0:T(8,128)S(1)}, f32[4,20,48,128]{3,2,1,0:T(8,128)S(1)}) fusion(f32[4,20,48,128]{3,2,1,0:T(8,128)S(1)} %get-tuple-element.42, f32[4,20,48,128]{3,2,1,0:T(8,128)S(1)} %get-tuple-element.43, f32[20,48,128]{2,1,0:T(8,128)S(1)} %get-tuple-element.72, f32[20,48,128]{2,1,0:T(8,128)S(1)} %get-tuple-element.68, ...), kind=kLoop, calls=%fused_computation.300 | loop fusion | flops 11304960 | bytes 11304960 | tf_op jit(solution)/shard_map/add | solution.py:382
  79.0 2.0 %fusion.108 = (f32[4,20,48,128]{3,2,1,0:T(8,128)S(1)}, f32[4,20,48,128]{3,2,1,0:T(8,128)S(1)}, f32[4,20,48,128]{3,2,1,0:T(8,128)S(1)}) fusion(f32[4,20,48,128]{3,2,1,0:T(8,128)S(1)} %get-tuple-element.40, f32[20,48,128]{2,1,0:T(8,128)S(1)} %get-tuple-element.49, f32[20,48,128]{2,1,0:T(8,128)S(1)} %get-tuple-element.69, ...), kind=kLoop, calls=%fused_computation.188 | loop fusion | flops 7864320 | bytes 10813440 | tf_op jit(solution)/shard_map/add | solution.py:430
  82.0 1.1 pad_maximum_fusion
  83.3 3.4 %multiply_reduce_fusion = f32[8,1024]{1,0:T(8,128)S(1)} fusion(f32[8,256,128]{2,1,0:T(8,128)} %bitcast.76, f32[128,1024]{1,0:T(8,128)S(1)} %fusion.245, s32[1024]{0:T(1024)S(1)} %get-tuple-element.96, pred[1024]{0:T(1024)(128)(4,1)S(1)} %get-tuple-element.94), kind=kOutput, calls=%fused_computation.68 | convolution fusion | flops 3223838720 | bytes 1610752 | tf_op jit(solution)/shard_map/spz,pd->szd/dot_general | solution.py:449
  87.3 16.1 %shard_map.123 = f32[64,128]{1,0:T(8,128)} custom-call(f32[64,128]{1,0:T(8,128)} %reshape.402.refs_0_), custom_call_target="tpu_custom_call" | custom-call | tf_op jit(solution)/shard_map/pallas_call | solution.py:310
  105.1 0.9 multiply_reduce_fusion.10
  106.4 3.5 %fusion.4 = f32[960,4,128]{2,0,1:T(8,128)S(1)} fusion(s32[1024]{0:T(1024)S(1)} %get-tuple-element.98, pred[1024]{0:T(1024)(128)(4,1)S(1)} %get-tuple-element.95, f32[1024,128]{0,1:T(8,128)S(1)} %fusion.246, f32[1024,4]{0,1:T(4,128)S(1)} %divide_bitcast_fusion), kind=kOutput, calls=%fused_computation.73 | convolution fusion | flops 6042288128 | bytes 2511872 | tf_op jit(solution)/shard_map/dot_general | solution.py:466
  111.8 2.2 %multiply_add_fusion.3 = (f32[4,20,48,128]{3,2,1,0:T(8,128)S(1)}, f32[4,20,48,128]{3,2,1,0:T(8,128)S(1)}) fusion(f32[4,20,48,128]{3,2,1,0:T(8,128)S(1)} %bitcast.66, f32[4,20,48,128]{3,2,1,0:T(8,128)S(1)} %broadcast_multiply_fusion, f32[20,48,128]{2,1,0:T(8,128)S(1)} %copy-done.11, f32[20,48,128]{2,1,0:T(8,128)S(1)} %copy-done.3, ...), kind=kLoop, calls=%fused_computation.299 | loop fusion | flops 11304960 | bytes 11304960 | tf_op jit(solution)/shard_map/add | solution.py:382
  114.1 2.3 %multiply_add_fusion.2 = (f32[4,20,48,128]{3,2,1,0:T(8,128)S(1)}, f32[4,20,48,128]{3,2,1,0:T(8,128)S(1)}) fusion(f32[4,20,48,128]{3,2,1,0:T(8,128)S(1)} %get-tuple-element.38, f32[4,20,48,128]{3,2,1,0:T(8,128)S(1)} %get-tuple-element.39, f32[20,48,128]{2,1,0:T(8,128)S(1)} %copy-done.11, f32[20,48,128]{2,1,0:T(8,128)S(1)} %copy-done.3, ...), kind=kLoop, calls=%fused_computation.298 | loop fusion | flops 11304960 | bytes 11304960 | tf_op jit(solution)/shard_map/add | solution.py:382
  116.4 2.3 %multiply_add_fusion.1 = (f32[4,20,48,128]{3,2,1,0:T(8,128)S(1)}, f32[4,20,48,128]{3,2,1,0:T(8,128)S(1)}) fusion(f32[4,20,48,128]{3,2,1,0:T(8,128)S(1)} %get-tuple-element.36, f32[4,20,48,128]{3,2,1,0:T(8,128)S(1)} %get-tuple-element.37, f32[20,48,128]{2,1,0:T(8,128)S(1)} %copy-done.11, f32[20,48,128]{2,1,0:T(8,128)S(1)} %copy-done.3, ...), kind=kLoop, calls=%fused_computation.297 | loop fusion | flops 11304960 | bytes 11304960 | tf_op jit(solution)/shard_map/add | solution.py:382
  118.8 2.6 %multiply_add_fusion = (f32[4,20,48,128]{3,2,1,0:T(8,128)S(1)}, f32[4,20,48,128]{3,2,1,0:T(8,128)S(1)}) fusion(f32[4,20,48,128]{3,2,1,0:T(8,128)S(1)} %get-tuple-element.34, f32[4,20,48,128]{3,2,1,0:T(8,128)S(1)} %get-tuple-element.35, f32[20,48,128]{2,1,0:T(8,128)S(1)} %copy-done.11, f32[20,48,128]{2,1,0:T(8,128)S(1)} %copy-done.3, ...), kind=kLoop, calls=%fused_computation.296 | loop fusion | flops 11304960 | bytes 11304960 | tf_op jit(solution)/shard_map/add | solution.py:382
  121.4 3.0 %fusion.205 = f32[4,20,48,128]{3,2,1,0:T(8,128)S(1)} fusion(f32[4,20,48,128]{3,2,1,0:T(8,128)S(1)} %get-tuple-element.33, f32[4,20,48,128]{3,2,1,0:T(8,128)S(1)} %get-tuple-element.32, f32[4,20,48,128]{3,2,1,0:T(8,128)S(1)} %get-tuple-element.34, f32[4,20,48,128]{3,2,1,0:T(8,128)S(1)} %get-tuple-element.36, f32[4,20,48,128]{3,2,1,0:T(8,128)S(1)} %get-tuple-element.38, ...), kind=kLoop, calls=%fused_computation.285 | loop fusion | flops 14254080 | bytes 17203200 | tf_op jit(solution)/shard_map/add | solution.py:378
  124.6 0.9 copy-done.18
  125.5 1.4 fusion.225
  127.2 1.4 copy.43
  128.8 1.3 copy.44
  130.1 2.5 %multiply_reduce_fusion.1 = (f32[]{:T(128)}, f32[]{:T(128)}) fusion(f32[1,8,32,8,16]{4,2,1,0,3:T(8,128)} %copy.44, f32[2,8,32,8,16]{4,2,1,0,3:T(8,128)S(1)} %bitcast.64, f32[1,8,32,8,16]{4,2,1,0,3:T(8,128)} %copy.43), kind=kLoop, calls=%fused_computation.312 | loop fusion | flops 131070 | bytes 524296 | tf_op jit(solution)/shard_map/reduce_sum | solution.py:479
  138.5 1.2 reshape.404.refs_0_
  139.7 24.0 %shard_map.124 = (f32[64,128]{1,0:T(8,128)}, f32[8,128]{1,0:T(8,128)}) custom-call(f32[8,64,128]{2,1,0:T(8,128)} %reshape.404.refs_0_, f32[8,128]{1,0:T(8,128)} %fusion.274.refs_1_), custom_call_target="tpu_custom_call" | custom-call | tf_op jit(solution)/shard_map/pallas_call | solution.py:310
  164.6 1.4 fusion.294
  172.3 16.2 %shard_map.125 = f32[8,128]{1,0:T(8,128)} custom-call(f32[8,128]{1,0:T(8,128)} %pad_bitcast_fusion.refs_0_), custom_call_target="tpu_custom_call" | custom-call | tf_op jit(solution)/shard_map/pallas_call | solution.py:310
  188.5 1.2 slice.466
  (126 shorter events, 19.5 us)
Async XLA Ops:
  20.9 1.7 copy-start.14
  22.6 2.3 %copy-start.26 = (s32[8,32,128]{2,1,0:T(8,128)S(1)}, s32[8,32,128]{2,1,0:T(8,128)}, u32[]{:S(2)}) copy-start(s32[8,32,128]{2,1,0:T(8,128)} %param.10) | copy-start | bytes 393220
  24.2 1.1 copy-start.16
  62.5 0.7 copy-start.28
  62.5 0.7 copy-start.29
  66.4 3.3 %copy-start.19 = (f32[20,48,128]{2,1,0:T(8,128)}, f32[20,48,128]{2,1,0:T(8,128)S(1)}, u32[]{:S(2)}) copy-start(f32[20,48,128]{2,1,0:T(8,128)S(1)} %get-tuple-element.48) | copy-start | bytes 1474564
  66.4 12.5 %copy-start.12 = (f32[20,48,128]{2,1,0:T(8,128)}, f32[20,48,128]{2,1,0:T(8,128)S(1)}, u32[]{:S(2)}) copy-start(f32[20,48,128]{2,1,0:T(8,128)S(1)} %get-tuple-element.49) | copy-start | bytes 1474564
  67.3 11.6 %copy-start = (f32[20,48,128]{2,1,0:T(8,128)}, f32[20,48,128]{2,1,0:T(8,128)S(1)}, u32[]{:S(2)}) copy-start(f32[20,48,128]{2,1,0:T(8,128)S(1)} %get-tuple-element.67) | copy-start | bytes 1474564
  67.3 11.6 %copy-start.2 = (f32[20,48,128]{2,1,0:T(8,128)}, f32[20,48,128]{2,1,0:T(8,128)S(1)}, u32[]{:S(2)}) copy-start(f32[20,48,128]{2,1,0:T(8,128)S(1)} %get-tuple-element.68) | copy-start | bytes 1474564
  67.3 11.6 %copy-start.4 = (f32[20,48,128]{2,1,0:T(8,128)}, f32[20,48,128]{2,1,0:T(8,128)S(1)}, u32[]{:S(2)}) copy-start(f32[20,48,128]{2,1,0:T(8,128)S(1)} %get-tuple-element.69) | copy-start | bytes 1474564
  67.3 11.6 %copy-start.6 = (f32[20,48,128]{2,1,0:T(8,128)}, f32[20,48,128]{2,1,0:T(8,128)S(1)}, u32[]{:S(2)}) copy-start(f32[20,48,128]{2,1,0:T(8,128)S(1)} %get-tuple-element.70) | copy-start | bytes 1474564
  67.4 11.6 %copy-start.8 = (f32[20,48,128]{2,1,0:T(8,128)}, f32[20,48,128]{2,1,0:T(8,128)S(1)}, u32[]{:S(2)}) copy-start(f32[20,48,128]{2,1,0:T(8,128)S(1)} %get-tuple-element.71) | copy-start | bytes 1474564
  67.4 13.6 %copy-start.10 = (f32[20,48,128]{2,1,0:T(8,128)}, f32[20,48,128]{2,1,0:T(8,128)S(1)}, u32[]{:S(2)}) copy-start(f32[20,48,128]{2,1,0:T(8,128)S(1)} %get-tuple-element.72) | copy-start | bytes 1474564
  81.0 1.0 copy-start.17
  82.0 1.1 copy-start.27
  109.9 1.0 copy-start.1
  109.9 1.2 copy-start.3
  109.9 1.3 copy-start.5
  109.9 1.5 copy-start.7
  109.9 1.6 copy-start.9
  109.9 1.7 copy-start.11
  109.9 1.9 copy-start.20
  111.8 2.3 %copy-start.13 = (f32[20,48,128]{2,1,0:T(8,128)S(1)}, f32[20,48,128]{2,1,0:T(8,128)}, u32[]{:S(2)}) copy-start(f32[20,48,128]{2,1,0:T(8,128)} %copy-done.12) | copy-start | bytes 1474564
  124.4 1.0 copy-start.18
  126.9 1.6 copy-start.23
  127.2 2.9 %copy-start.15 = (f32[8,2,8,32,16]{4,3,2,1,0:T(8,128)S(1)}, f32[8,2,8,32,16]{4,3,2,1,0:T(8,128)}, u32[]{:S(2)}) copy-start(f32[8,2,8,32,16]{4,3,2,1,0:T(8,128)} %copy-done.14) | copy-start | bytes 786436
  130.1 3.8 %copy-start.21 = (f32[8,32,16]{1,2,0:T(8,128)S(1)}, f32[8,32,16]{1,2,0:T(8,128)}, u32[]{:S(2)}) copy-start(f32[8,32,16]{1,2,0:T(8,128)} %param.16) | copy-start | bytes 49156
  130.1 3.8 %copy-start.22 = (f32[8,32,16]{1,2,0:T(8,128)S(1)}, f32[8,32,16]{1,2,0:T(8,128)}, u32[]{:S(2)}) copy-start(f32[8,32,16]{1,2,0:T(8,128)} %param.15) | copy-start | bytes 49156
  130.1 3.8 %copy-start.24 = (f32[8,32,16]{1,2,0:T(8,128)S(1)}, f32[8,32,16]{1,2,0:T(8,128)}, u32[]{:S(2)}) copy-start(f32[8,32,16]{1,2,0:T(8,128)} %param.18) | copy-start | bytes 49156
  130.1 3.8 %copy-start.25 = (f32[8,32,16]{1,2,0:T(8,128)S(1)}, f32[8,32,16]{1,2,0:T(8,128)}, u32[]{:S(2)}) copy-start(f32[8,32,16]{1,2,0:T(8,128)} %param.17) | copy-start | bytes 49156
